TPU v7x, 32 devices: a whole 2x2x4 slice. The times are simulated.
32 devices in a mesh: freq: 16 (over z, y, x), tm: 2 (over core).
Axes of the slice: x: 2, y: 2, z: 4, core: 2. Of those that a mesh axis runs over, the one named last changes fastest.
Arguments:
- spectra: float32 [512, 2048], P('freq', 'tm'), may hold values from -500 to 500
- lead_delay: int32 [9, 512], replicated, may hold values from 0 to 255, as said below
- tail_delay: int32 [9, 512], replicated, may hold values from 0 to 255, as said below
- widths: int32 [16], replicated, may hold values from 1 to 128, as said below
Outputs:
- best_snr: float32 [2048], P('tm')
- trial_peak: float32 [512], P('freq')
Inputs may be any that keep to these rules, and one draw needn't show every extreme that they name: At section s with R = 2**s, for row c with d = c mod 2 R, B = min(R, 32) and m = floor(d / (2 B)): lead_delay[s, c] and tail_delay[s, c] both lie in B m to B m + B - 1, and lead_delay[s, c] <= d. `tail_delay`: same rows and bounds as lead_delay. The 16 widths are distinct and one of them is 128.
All inputs are finite; a program needn't handle non-finite values.
Results may differ from a plain program's by a relative error of at most 0.000035.
Values sent between devices are 32-bit elements; how exact they have to be, the bound alone decides.
No kernel may reach another device: no remote copies, remote signals or barrier semaphores. Data moves between devices by JAX's collectives and lax.ppermute only.
A program may use at most 64 MiB of HBM per device.

v0:
```python
import jax
import jax.numpy as jnp
from jax import lax
from jax.sharding import PartitionSpec as P

TIME_DEV = 1024
MAXW = 128


eps_var = 1e-06


def shifted(value, axis, by):
    length = lax.axis_size(axis)
    pairs = [(i, i + by) for i in range(length) if 0 <= i + by < length]
    return lax.ppermute(value, axis, pairs)


def partner_2(value, axis, stride):
    return lax.ppermute(value, axis, [(i, i ^ 1 << stride) for i in range(lax.axis_size(axis))])


def shifted_sum(lower_rows, padded, lower_index, upper_index, delays, halo_len, length):
    picked_low = jnp.take(lower_rows, lower_index, axis=0)
    picked_up = jnp.take(padded, upper_index, axis=0)

    def slide_row(row_values, amount):
        return lax.dynamic_slice_in_dim(row_values, halo_len - amount, length)

    moved_rows = jax.vmap(slide_row)(picked_up, delays)
    return picked_low + moved_rows


def box_best(centred, spread, widths, rim_values):
    row_count, length = centred.shape
    segment = min(256, TIME_DEV)
    block_count = length // segment
    extended = jnp.concatenate([rim_values, centred], axis=1)
    leading_rims = extended[:, :length].reshape(row_count, block_count, segment)[:, :, :MAXW]
    blocks = jnp.concatenate(
        [leading_rims, centred.reshape(row_count, block_count, segment)], axis=2
    )
    prefix = jnp.cumsum(blocks, axis=2)
    upper_sum = prefix[:, :, MAXW:]
    scale_rows = spread[:, None, None]

    def advance(which, running):
        box_width = widths[which]
        lower_sum = lax.dynamic_slice_in_dim(prefix, MAXW - box_width, segment, axis=2)
        scores = (upper_sum - lower_sum) / (scale_rows * jnp.sqrt(box_width.astype(jnp.float32)))
        return jnp.maximum(running, scores)

    start_best = jnp.full((row_count, block_count, segment), -jnp.inf, jnp.float32)
    running = lax.fori_loop(0, widths.shape[0], advance, start_best)
    return running.reshape(row_count, length)


def reverse_bits(value, bit_count):
    result = value * 0
    for bit_idx in range(bit_count):
        result = result + ((value >> bit_idx & 1) << bit_count - 1 - bit_idx)
    return result


def shards(spectra, lead_delay, tail_delay, widths):
    channels_dev, span_time = spectra.shape
    dev_freq = lax.axis_index("freq")
    dev_time = lax.axis_index("tm")
    n_freq = lax.axis_size("freq")
    total_time = span_time * lax.axis_size("tm")
    cross_count = n_freq.bit_length() - 1
    local_count = channels_dev.bit_length() - 1
    positions = jnp.arange(channels_dev, dtype=jnp.int32)
    current = spectra
    width_now = current.shape[1]
    paired = current.reshape(channels_dev // 2, 2, width_now)
    current = jnp.repeat(paired[:, 0] + paired[:, 1], 2, axis=0)
    for section_idx in range(1, local_count):
        rows_in = 2**section_idx
        halo_len = rows_in - 1
        leading = lax.dynamic_slice_in_dim(
            lead_delay[section_idx], dev_freq * channels_dev, channels_dev
        )
        trailing = lax.dynamic_slice_in_dim(
            tail_delay[section_idx], dev_freq * channels_dev, channels_dev
        )
        band_count = channels_dev // (2 * rows_in)
        halves = current.reshape(band_count, 2, rows_in, width_now)
        lower_rows = halves[:, 0].reshape(channels_dev // 2, width_now)
        upper_rows = halves[:, 1].reshape(channels_dev // 2, width_now)
        band_ids = positions // (2 * rows_in)
        lower_index = band_ids * rows_in + leading
        upper_index = band_ids * rows_in + trailing
        rim_values = shifted(upper_rows[:, width_now - halo_len :], "tm", 1)
        padded = jnp.concatenate([rim_values, upper_rows], axis=1)
        current = shifted_sum(
            lower_rows, padded, lower_index, upper_index, leading, halo_len, width_now
        )
    for level_idx in range(cross_count):
        section_idx = local_count + level_idx
        rows_in = channels_dev * 2**level_idx
        in_group = dev_freq % 2 ** (level_idx + 1)
        upper_side = in_group >> level_idx
        block_order = reverse_bits(in_group % 2**level_idx, level_idx)
        block_out = 2 * block_order + upper_side
        table_start = (dev_freq >> level_idx + 1) * (2 * rows_in) + channels_dev * block_out
        leading = lax.dynamic_slice_in_dim(lead_delay[section_idx], table_start, channels_dev)
        trailing = lax.dynamic_slice_in_dim(tail_delay[section_idx], table_start, channels_dev)
        partner = partner_2(current, "freq", level_idx)
        is_upper = upper_side == 1
        lower_rows = jnp.where(is_upper, partner, current)
        upper_rows = jnp.where(is_upper, current, partner)
        halo_len = rows_in
        rim_values = shifted(upper_rows[:, span_time - halo_len :], "tm", 1)
        padded = jnp.concatenate([rim_values, upper_rows], axis=1)
        lower_index = leading - channels_dev * block_order
        upper_index = trailing - channels_dev * block_order
        current = shifted_sum(
            lower_rows, padded, lower_index, upper_index, leading, halo_len, span_time
        )
    final_order = reverse_bits(dev_freq, cross_count)
    raw_rim = shifted(current[:, span_time - MAXW :], "tm", 1)
    totals = lax.psum(jnp.sum(current, axis=1), "tm")
    mean_row = totals / total_time
    centred = current - mean_row[:, None]
    squares = lax.psum(jnp.sum(centred * centred, axis=1), "tm")
    spread = jnp.sqrt(squares / total_time + eps_var)
    rim_values = jnp.where(dev_time > 0, raw_rim - mean_row[:, None], 0.0)
    running = box_best(centred, spread, widths, rim_values)
    best_snr = lax.pmax(jnp.max(running, axis=0), "freq")
    peak_local = jnp.max(running, axis=1)
    block_ids = jnp.arange(channels_dev * n_freq, dtype=jnp.int32) // channels_dev
    placed = jnp.where(block_ids == final_order, jnp.tile(peak_local, n_freq), -1e30)
    peak_all = lax.pmax(placed, ("freq", "tm"))
    trial_peak = lax.dynamic_slice_in_dim(peak_all, dev_freq * channels_dev, channels_dev)
    return (best_snr, trial_peak)


def solution(mesh):
    placed = (P("freq", "tm"), P(), P(), P())
    return jax.shard_map(
        shards, mesh=mesh, in_specs=placed, out_specs=(P("tm"), P("freq")), check_vma=False
    )
```

profile of v0, /device:TPU:0, one launch (start us, length us, event | category | flops | bytes accessed | tf_op | source)
XLA Modules:
  0.0 740.7 jit_solution(2071595765886541653)
XLA Ops:
  2.1 2.3 collective-permute-start
  8.3 67.0 %while.24 = (s32[]{:T(128)}, f32[32,1025]{1,0:T(8,128)S(1)}, s32[32,2]{0,1:T(2,128)S(1)}, f32[32,1024]{1,0:T(8,128)S(1)}, s32[]{:T(128)}, /*index=5*/s32[]{:T(128)}) while((s32[]{:T(128)}, f32[32,1025]{1,0:T(8,128)S(1)}, s32[32,2]{0,1:T(2,128)S(1)}, f32[32,1024]{1,0:T(8,128)S(1)}, s32[]{:T(128)}, /*index=5*/s32[]{:T(128)}) %tuple.207), condition=%wide.while_cond, body=%wide.while_body.sunk | while | flops 2 | bytes 16497 | solution.py:28
  78.6 67.7 %while.25 = (s32[]{:T(128)}, f32[32,1027]{1,0:T(8,128)S(1)}, s32[32,2]{0,1:T(2,128)S(1)}, f32[32,1024]{1,0:T(8,128)S(1)}, s32[]{:T(128)}, /*index=5*/s32[]{:T(128)}) while((s32[]{:T(128)}, f32[32,1027]{1,0:T(8,128)S(1)}, s32[32,2]{0,1:T(2,128)S(1)}, f32[32,1024]{1,0:T(8,128)S(1)}, s32[]{:T(128)}, /*index=5*/s32[]{:T(128)}) %tuple.210), condition=%wide.while_cond.1, body=%wide.while_body.1.sunk | while | flops 2 | bytes 16497 | solution.py:28
  81.4 1.4 dynamic-slice.67
  85.6 1.4 dynamic-slice.67
  89.8 1.4 dynamic-slice.67
  94.0 1.4 dynamic-slice.67
  98.3 1.4 dynamic-slice.67
  117.3 1.4 dynamic-slice.67
  121.5 1.4 dynamic-slice.67
  125.8 1.4 dynamic-slice.67
  130.0 1.4 dynamic-slice.67
  134.2 1.4 dynamic-slice.67
  138.4 1.4 dynamic-slice.67
  146.4 2.2 collective-permute-start.2
  150.3 67.7 %while.26 = (s32[]{:T(128)}, f32[32,1031]{1,0:T(8,128)S(1)}, s32[32,2]{0,1:T(2,128)S(1)}, f32[32,1024]{1,0:T(8,128)S(1)}, s32[]{:T(128)}, /*index=5*/s32[]{:T(128)}) while((s32[]{:T(128)}, f32[32,1031]{1,0:T(8,128)S(1)}, s32[32,2]{0,1:T(2,128)S(1)}, f32[32,1024]{1,0:T(8,128)S(1)}, s32[]{:T(128)}, /*index=5*/s32[]{:T(128)}) %tuple.213), condition=%wide.while_cond.2, body=%wide.while_body.2.sunk | while | flops 2 | bytes 16497 | solution.py:28
  151.0 1.4 dynamic-slice.69
  155.2 1.4 dynamic-slice.69
  159.4 1.4 dynamic-slice.69
  163.7 1.4 dynamic-slice.69
  167.9 1.4 dynamic-slice.69
  172.1 1.4 dynamic-slice.69
  191.1 1.4 dynamic-slice.69
  218.1 2.2 collective-permute-start.3
  222.0 67.7 %while.27 = (s32[]{:T(128)}, f32[32,1039]{1,0:T(8,128)S(1)}, s32[32,2]{0,1:T(2,128)S(1)}, f32[32,1024]{1,0:T(8,128)S(1)}, s32[]{:T(128)}, /*index=5*/s32[]{:T(128)}) while((s32[]{:T(128)}, f32[32,1039]{1,0:T(8,128)S(1)}, s32[32,2]{0,1:T(2,128)S(1)}, f32[32,1024]{1,0:T(8,128)S(1)}, s32[]{:T(128)}, /*index=5*/s32[]{:T(128)}) %tuple.216), condition=%wide.while_cond.3, body=%wide.while_body.3.sunk | while | flops 2 | bytes 16497 | solution.py:28
  289.8 2.4 collective-permute-start.4
  292.2 3.9 collective-permute-done.4
  296.3 1.8 collective-permute-start.5
  299.7 67.7 %while.28 = (s32[]{:T(128)}, f32[32,1056]{1,0:T(8,128)S(1)}, s32[32,2]{0,1:T(2,128)S(1)}, f32[32,1024]{1,0:T(8,128)S(1)}, s32[]{:T(128)}, /*index=5*/s32[]{:T(128)}) while((s32[]{:T(128)}, f32[32,1056]{1,0:T(8,128)S(1)}, s32[32,2]{0,1:T(2,128)S(1)}, f32[32,1024]{1,0:T(8,128)S(1)}, s32[]{:T(128)}, /*index=5*/s32[]{:T(128)}) %tuple.219), condition=%wide.while_cond.4, body=%wide.while_body.4.sunk | while | flops 2 | bytes 16497 | solution.py:28
  367.4 1.5 collective-permute-start.6
  369.0 4.2 collective-permute-done.6
  373.4 1.4 collective-permute-start.7
  376.5 67.7 %while.29 = (s32[]{:T(128)}, f32[32,1088]{1,0:T(8,128)S(1)}, s32[32,2]{0,1:T(2,128)S(1)}, f32[32,1024]{1,0:T(8,128)S(1)}, s32[]{:T(128)}, /*index=5*/s32[]{:T(128)}) while((s32[]{:T(128)}, f32[32,1088]{1,0:T(8,128)S(1)}, s32[32,2]{0,1:T(2,128)S(1)}, f32[32,1024]{1,0:T(8,128)S(1)}, s32[]{:T(128)}, /*index=5*/s32[]{:T(128)}) %tuple.222), condition=%wide.while_cond.5, body=%wide.while_body.5.sunk | while | flops 2 | bytes 16497 | solution.py:28
  444.2 1.6 collective-permute-start.8
  445.9 4.2 collective-permute-done.8
  450.1 1.4 collective-permute-start.9
  453.1 67.7 %while.30 = (s32[]{:T(128)}, f32[32,1152]{1,0:T(8,128)S(1)}, s32[32,2]{0,1:T(2,128)S(1)}, f32[32,1024]{1,0:T(8,128)S(1)}, s32[]{:T(128)}, /*index=5*/s32[]{:T(128)}) while((s32[]{:T(128)}, f32[32,1152]{1,0:T(8,128)S(1)}, s32[32,2]{0,1:T(2,128)S(1)}, f32[32,1024]{1,0:T(8,128)S(1)}, s32[]{:T(128)}, /*index=5*/s32[]{:T(128)}) %tuple.225), condition=%wide.while_cond.6, body=%wide.while_body.6.sunk | while | flops 2 | bytes 16497 | solution.py:28
  520.8 2.6 collective-permute-start.10
  523.5 6.9 collective-permute-done.10
  530.4 1.5 collective-permute-start.11
  533.5 67.0 %while.31 = (s32[]{:T(128)}, f32[32,1280]{1,0:T(8,128)S(1)}, s32[32,2]{0,1:T(2,128)S(1)}, f32[32,1024]{1,0:T(8,128)S(1)}, s32[]{:T(128)}, /*index=5*/s32[]{:T(128)}) while((s32[]{:T(128)}, f32[32,1280]{1,0:T(8,128)S(1)}, s32[32,2]{0,1:T(2,128)S(1)}, f32[32,1024]{1,0:T(8,128)S(1)}, s32[]{:T(128)}, /*index=5*/s32[]{:T(128)}) %tuple.228), condition=%wide.while_cond.7, body=%wide.while_body.7.sunk | while | flops 2 | bytes 16497 | solution.py:28
  600.7 2.3 collective-permute-start.12
  603.0 2.5 psum.14
  605.6 2.5 psum.15
  608.4 3.5 reduce-window.6
  612.9 46.1 %while.32 = (s32[]{:T(128)}, f32[32,4,256]{2,1,0:T(4,128)S(1)}, s32[16]{0:T(128)S(1)}, f32[32,4,384]{2,0,1:T(8,128)S(1)}, f32[32,4,256]{2,1,0:T(4,128)S(1)}, /*i...) while((s32[]{:T(128)}, f32[32,4,256]{2,1,0:T(4,128)S(1)}, ...), condition=%wide.region_7.10_spmd.clone, body=%wide.region_6.9_spmd.clone.sunk | while | flops 131112 | bytes 787009 | solution.py:54
  659.5 40.2 %pmax.15 = f32[512]{0:T(512)S(1)} all-reduce(f32[512]{0:T(512)S(1)} %fusion.4), channel_id=1, replica_groups=mesh['freq'=16,'tm'=2] {'freq','tm'}, use_global_device_ids=true, to_apply=%region_11.14 | all-reduce | flops 512 | bytes 4096 | tf_op jit(solution)/shard_map/pmax | solution.py:134
  700.3 40.4 %pmax.14 = f32[1024]{0:T(1024)} all-reduce(f32[1024]{0:T(1024)S(1)} %bitcast.231), channel_id=1, replica_groups=mesh['freq'=16,'tm'=2] {'freq'}, use_global_device_ids=true, to_apply=%region_9.12 | all-reduce | flops 1024 | bytes 8192 | tf_op jit(solution)/shard_map/pmax | solution.py:130
  (1232 shorter events, 544.9 us)
Async XLA Ops:
  2.1 5.4 collective-permute-start
  4.5 0.8 copy-start
  4.6 0.9 copy-start.1
  75.6 2.1 collective-permute-start.1
  146.4 3.1 collective-permute-start.2
  218.1 3.1 collective-permute-start.3
  289.8 6.4 collective-permute-start.4
  296.3 2.6 collective-permute-start.5
  367.4 5.8 collective-permute-start.6
  373.4 2.3 collective-permute-start.7
  444.2 5.8 collective-permute-start.8
  450.1 2.3 collective-permute-start.9
  520.8 9.5 %collective-permute-start.10 = (f32[32,1024]{1,0:T(8,128)S(1)}, f32[32,1024]{1,0:T(8,128)S(1)}, u32[]{:S(2)}, u32[]{:S(2)}) collective-permute-start(f32[32,1024]{1,0:T(8,128)S(1)} %select_add_fusion.1), channel_id=1, source_target_pairs={{0,16},{2,18},{4,20},{6,22},{8,24},{10,26},{12,28},{14,30},{16,0},... | collective-permute-start | bytes 393224 | tf_op jit(solution)/shard_map/ppermute | solution.py:20
  530.4 2.3 collective-permute-start.11
  600.7 7.4 %collective-permute-start.12 = (f32[32,128]{1,0:T(8,128)S(1)}, f32[32,128]{1,0:T(8,128)S(1)}, u32[]{:S(2)}, u32[]{:S(2)}) collective-permute-start(f32[32,128]{1,0:T(8,128)S(1)} %slice.298), channel_id=1, source_target_pairs={{0,1},{2,3},{4,5},{6,7},{8,9},{10,11},{12,13},{14,15},{16,17},{18,... | collective-permute-start | bytes 49160 | tf_op jit(solution)/shard_map/ppermute | solution.py:16
  612.3 0.7 copy-start.2
where the time goes:
time: 746 us; the launch traced here: 741 us
  local copies, waits for them, and re-layouts  559 us (75%)
  blocking collectives  85.5 us (11%)
  loops' own time  38.6 us (5%)
  starting transfers between devices  24.5 us (3%)
  waiting for transfers between devices  20 us (3%)
  other arithmetic  11.4 us (2%)
    gather x1024, local copies, waits for them, and re-layouts  534 us
    pmax x1, blocking collectives, shards(): best_snr = lax.pmax(jnp.max(running, axis=0), 'freq')  40.4 us
    pmax x1, blocking collectives, shards(): peak_all = lax.pmax(placed, ('freq', 'tm'))  40.2 us
    another operation x1, loops' own time, box_best(): running = lax.fori_loop(0, widths.shape[0], advance, start_best)  32.4 us
    ppermute x4, waiting for transfers between devices, partner_2(): lax.ppermute(value, axis, [(i, i ^ 1 << stride) for i in range(lax.axis_s...  19.1 us
    ppermute x9, starting transfers between devices, shifted(): return lax.ppermute(value, axis, pairs)  16.5 us
  transfers between devices with their start and end apart: 13, of which 11 were waited for; matrix products, arithmetic and copies ran while one was open for 1% of the time, Pallas kernels for 0%

commit v1 on v0

v1 whole, which is shorter than its diff:
```python
import functools

import jax
import jax.numpy as jnp
from jax import lax
from jax.experimental import pallas as pl
from jax.experimental.pallas import tpu as pltpu
from jax.sharding import PartitionSpec as P

MAXW = 128
LANES = 128
ROWS = 32
PAD = 8

eps_var = 1e-06
VMEM = pl.BlockSpec(memory_space=pltpu.VMEM)
SMEM = pl.BlockSpec(memory_space=pltpu.SMEM)


def xor_permute(value, axis, by):
    return lax.ppermute(value, axis, [(i, i ^ by) for i in range(lax.axis_size(axis))])


def shift_right(value, axis):
    count = lax.axis_size(axis)
    return lax.ppermute(value, axis, [(i, i + 1) for i in range(count - 1)])


def shifted_rows(src, starts, shifts, segs, lane):
    picked = []
    for start, shift in zip(starts, shifts):
        start = start - (shift >> 7)
        picked.append((src[pl.ds(start, segs), :], src[pl.ds(start - 1, segs), :]))
    out = []
    for (here, before), shift in zip(picked, shifts):
        part = shift & (LANES - 1)
        mixed = jnp.where(lane < LANES - part, here, before)
        out.append(pltpu.roll(mixed, part, axis=1))
    return out


def section_rows(src, src_segs, dst, dst_segs, table, rows, group=8):
    drop = src_segs - dst_segs
    lane = lax.broadcasted_iota(jnp.int32, (dst_segs, LANES), 1)

    def do_group(first):
        entries = [table(first + i) for i in range(group)]
        lower = [src[pl.ds(PAD + low * src_segs + drop, dst_segs), :] for low, _, _, _ in entries]
        upper = shifted_rows(
            src,
            [PAD + up * src_segs + drop for _, up, _, _ in entries],
            [delay for _, _, delay, _ in entries],
            dst_segs,
            lane,
        )
        for (_, _, _, to), a, b in zip(entries, lower, upper):
            dst[pl.ds(to, dst_segs), :] = a + b

    for first in range(0, rows, group):
        do_group(first)


def local_kernel(lead, tail, x, left, out, buf_a, buf_b, stage, *, sections, segs, out_segs, main_segs):
    channels = x.shape[0]
    halo = segs - main_segs
    column = lax.axis_index("freq") * channels
    pairs = channels // 2
    buf_a[pl.ds(0, PAD), :] = jnp.zeros((PAD, LANES), jnp.float32)
    buf_b[pl.ds(0, PAD), :] = jnp.zeros((PAD, LANES), jnp.float32)
    for seg in range(segs):
        source, at = (left, main_segs - halo + seg) if seg < halo else (x, seg - halo)
        stage[pl.ds(seg * channels, channels), :] = source[:, pl.ds(at * LANES, LANES)]
    for seg in range(segs):
        first = seg * channels
        summed = stage[pl.ds(first, pairs, stride=2), :] + stage[pl.ds(first + 1, pairs, stride=2), :]
        buf_a[pl.ds(PAD + seg, pairs, stride=segs), :] = summed
    src, dst = buf_a, buf_b
    for section in range(1, sections):
        rows_in = 2**section
        last = section == sections - 1

        def table(k, section=section, rows_in=rows_in, last=last):
            e = lead[section, column + k]
            h = tail[section, column + k]
            band = k // (2 * rows_in)
            if section == 1:
                low, up = 2 * band, 2 * band + 1
            else:
                low, up = 2 * band * rows_in + e, (2 * band + 1) * rows_in + h
            to = k * out_segs if last else PAD + k * segs
            return low, up, e, to

        section_rows(src, segs, out if last else dst, out_segs if last else segs, table, channels)
        src, dst = dst, src


def quad_kernel(lead, tail, own, one, two, three, out, buf_a, buf_b, *, section, segs, mid_segs, out_segs):
    freq = lax.axis_index("freq")
    place = freq % 4
    size = ROWS * segs
    for by, ref in enumerate((own, one, two, three)):
        to = pl.multiple_of(PAD + (place ^ by) * size, 8)
        buf_a[pl.ds(to, size), :] = ref[...]
    buf_a[pl.ds(0, PAD), :] = jnp.zeros((PAD, LANES), jnp.float32)
    buf_b[pl.ds(0, PAD), :] = jnp.zeros((PAD, LANES), jnp.float32)
    base = (freq // 4) * (4 * ROWS)
    half = place // 2

    def first(k):
        band, row = k // ROWS, k % ROWS
        column = base + 2 * ROWS * band + ROWS * half + row
        e = lead[section, column]
        h = tail[section, column]
        return 2 * band * ROWS + e, (2 * band + 1) * ROWS + h, e, PAD + k * mid_segs

    section_rows(buf_a, segs, buf_b, mid_segs, first, 2 * ROWS)

    def second(k):
        column = base + ROWS * place + k
        e = lead[section + 1, column]
        h = tail[section + 1, column]
        return e - ROWS * half, ROWS + h - ROWS * half, e, k * out_segs

    section_rows(buf_b, mid_segs, out, out_segs, second, ROWS)


def order_of(freq, level):
    order = freq % 4
    for bit in range(2, level):
        order = 2 * order + ((freq >> bit) & 1)
    return order


def pair_kernel(lead, tail, own, other, out, buf_a, *, level, section, segs, out_segs):
    freq = lax.axis_index("freq")
    side = (freq >> level) & 1
    order = order_of(freq, level)
    size = ROWS * segs
    buf_a[pl.ds(0, PAD), :] = jnp.zeros((PAD, LANES), jnp.float32)
    buf_a[pl.ds(pl.multiple_of(PAD + side * size, 8), size), :] = own[...]
    buf_a[pl.ds(pl.multiple_of(PAD + (1 - side) * size, 8), size), :] = other[...]
    base = (freq >> (level + 1)) * (2 * 2**section) + ROWS * (2 * order + side)

    def table(k):
        e = lead[section, base + k]
        h = tail[section, base + k]
        return e - ROWS * order, ROWS + h - ROWS * order, e, k * out_segs

    section_rows(buf_a, segs, out, out_segs, table, ROWS)


def final_kernel(lead, tail, widths, *refs, level, section, n_time, main_segs, trials, place_rows):
    own, other = refs[:n_time], refs[n_time : 2 * n_time]
    outs = refs[2 * n_time : 3 * n_time]
    buf, data, back, sums, scale = refs[3 * n_time :]
    freq = lax.axis_index("freq")
    tm = lax.axis_index("tm")
    side = (freq >> level) & 1
    order = order_of(freq, level)
    total_segs = n_time * main_segs
    stride = PAD + total_segs
    zeros = jnp.zeros((PAD, LANES), jnp.float32)
    for row in range(2 * ROWS):
        buf[pl.ds(row * stride, PAD), :] = zeros
    for which, group in ((side, own), (1 - side, other)):
        for by in range(n_time):
            start = which * (ROWS * stride) + PAD + (tm ^ by) * main_segs
            for row in range(ROWS):
                to = pl.multiple_of(start + row * stride, 8)
                buf[pl.ds(to, main_segs), :] = group[by][pl.ds(row * main_segs, main_segs), :]
    final = 2 * order + side
    first_trial = ROWS * final + trials * tm
    base = (freq >> (level + 1)) * (2 * 2**section) + first_trial
    lane = lax.broadcasted_iota(jnp.int32, (total_segs, LANES), 1)
    group = min(trials, 4)
    for start in range(0, trials, group):
        shifts, lows, ups = [], [], []
        for i in range(start, start + group):
            e = lead[section, base + i]
            h = tail[section, base + i]
            shifts.append(e)
            lows.append((e - ROWS * order) * stride + PAD)
            ups.append((ROWS + h - ROWS * order) * stride + PAD)
        lower = [buf[pl.ds(at, total_segs), :] for at in lows]
        upper = shifted_rows(buf, ups, shifts, total_segs, lane)
        for i, a, b in zip(range(start, start + group), lower, upper):
            value = a + b
            data[pl.ds(i * total_segs, total_segs), :] = value
            sums[pl.ds(i, 1), :] = jnp.sum(value, axis=0, keepdims=True)
    total_time = total_segs * LANES
    mean = jnp.sum(sums[...], axis=1, keepdims=True) / total_time
    sums[...] = jnp.broadcast_to(mean, sums.shape)
    for j in range(widths.shape[0]):
        scale[pl.ds(j, 1), :] = jnp.full((1, LANES), widths[j], jnp.int32).astype(jnp.float32)
    scale[...] = 1.0 / jnp.sqrt(scale[...])

    for start in range(0, trials, group):
        values = []
        for i in range(start, start + group):
            centred = data[pl.ds(i * total_segs, total_segs), :] - sums[pl.ds(i, 1), :]
            sums[pl.ds(i, 1), :] = jnp.sum(centred * centred, axis=0, keepdims=True)
            values.append(centred)
        step = 1
        while step < LANES:
            values = [v + jnp.where(lane >= step, pltpu.roll(v, step, axis=1), 0.0) for v in values]
            step *= 2
        for i, v in zip(range(start, start + group), values):
            data[pl.ds(i * total_segs, total_segs), :] = v
            back[pl.ds(i * stride, PAD), :] = zeros
            whole = jnp.broadcast_to(v[:, LANES - 1 :], v.shape)
            back[pl.ds(i * stride + PAD, total_segs), :] = v - whole
    squares = jnp.sum(sums[...], axis=1, keepdims=True)
    inverse = 1.0 / jnp.sqrt(squares / total_time + eps_var)
    sums[...] = jnp.broadcast_to(inverse, sums.shape)

    best_all = jnp.full((total_segs, LANES), -jnp.inf, jnp.float32)
    group = min(trials, 2)
    for start in range(0, trials, group):
        prefixes = [data[pl.ds(i * total_segs, total_segs), :] for i in range(start, start + group)]
        befores = [back[pl.ds(i * stride + PAD - 1, total_segs), :] for i in range(start, start + group)]
        best = [jnp.full((total_segs, LANES), -jnp.inf, jnp.float32)] * group
        for j in range(widths.shape[0]):
            width = widths[j]
            inv_root = scale[pl.ds(j, 1), :]
            mask = lane < LANES - width
            part = width & (LANES - 1)
            for n in range(group):
                ended = pltpu.roll(jnp.where(mask, prefixes[n], befores[n]), part, axis=1)
                best[n] = jnp.maximum(best[n], (prefixes[n] - ended) * inv_root)
        for n in range(group):
            i = start + n
            scores = best[n] * sums[pl.ds(i, 1), :]
            best_all = jnp.maximum(best_all, scores)
            sums[pl.ds(i, 1), :] = jnp.max(scores, axis=0, keepdims=True)
    peaks = jnp.max(sums[...], axis=1, keepdims=True)
    offset = first_trial % LANES
    shape = sums.shape
    spot = lax.broadcasted_iota(jnp.int32, shape, 1) == lax.broadcasted_iota(jnp.int32, shape, 0) + offset
    peak_row = jnp.max(jnp.where(spot, peaks, -jnp.inf), axis=0, keepdims=True)
    data[pl.ds(0, total_segs), :] = best_all
    for by in range(n_time):
        at = pl.multiple_of((tm ^ by) * main_segs, 8)
        outs[by][pl.ds(0, main_segs), :] = data[pl.ds(at, main_segs), :]
        outs[by][pl.ds(main_segs, place_rows), :] = jnp.full((place_rows, LANES), -jnp.inf, jnp.float32)
        outs[by][pl.ds(main_segs + first_trial // LANES, 1), :] = peak_row


def call(kernel, inputs, out_shapes, scratch, name):
    n_tables = 3 if name == "final" else 2
    specs = [SMEM] * n_tables + [VMEM] * (len(inputs) - n_tables)
    outs = [jax.ShapeDtypeStruct(shape, jnp.float32) for shape in out_shapes]
    used = sum(4 * s[0] * s[1] for s in scratch) + sum(4 * v.size for v in inputs) + sum(4 * o.size for o in outs)
    return pl.pallas_call(
        kernel,
        out_shape=outs,
        in_specs=specs,
        out_specs=[VMEM] * len(outs),
        scratch_shapes=[pltpu.VMEM(shape, jnp.float32) for shape in scratch],
        compiler_params=pltpu.CompilerParams(vmem_limit_bytes=used + (2 << 20)),
        name=name,
    )(*inputs)


def shards(spectra, lead_delay, tail_delay, widths):
    channels, span = spectra.shape
    n_freq = lax.axis_size("freq")
    n_time = lax.axis_size("tm")
    freq = lax.axis_index("freq")
    sections = lead_delay.shape[0]
    local = channels.bit_length() - 1
    cross = n_freq.bit_length() - 1
    main_segs = span // LANES
    last = sections - 1

    def segs_before(section):
        need = sum(2**s - 1 for s in range(section, last))
        return main_segs + -(-need // LANES)

    tables = (lead_delay, tail_delay)
    left = shift_right(spectra, "tm")
    segs = segs_before(1)
    out_segs = segs_before(local)
    (current,) = call(
        functools.partial(local_kernel, sections=local, segs=segs, out_segs=out_segs, main_segs=main_segs),
        (*tables, spectra, left),
        [(channels * out_segs, LANES)],
        [(PAD + channels * segs, LANES)] * 2 + [(channels * segs, LANES)],
        "local",
    )
    segs, mid_segs, out_segs = (segs_before(local + i) for i in range(3))
    others = [xor_permute(current, "freq", by) for by in (1, 2, 3)]
    (current,) = call(
        functools.partial(quad_kernel, section=local, segs=segs, mid_segs=mid_segs, out_segs=out_segs),
        (*tables, current, *others),
        [(ROWS * out_segs, LANES)],
        [(PAD + 4 * ROWS * segs, LANES), (PAD + 2 * ROWS * mid_segs, LANES)],
        "quad",
    )
    for level in range(2, cross - 1):
        section = local + level
        segs, out_segs = segs_before(section), segs_before(section + 1)
        other = xor_permute(current, "freq", 1 << level)
        (current,) = call(
            functools.partial(pair_kernel, level=level, section=section, segs=segs, out_segs=out_segs),
            (*tables, current, other),
            [(ROWS * out_segs, LANES)],
            [(PAD + 2 * ROWS * segs, LANES)],
            "pair",
        )
    level = cross - 1
    other = xor_permute(current, "freq", 1 << level)
    owns = [current] + [xor_permute(current, "tm", by) for by in range(1, n_time)]
    others = [other] + [xor_permute(other, "tm", by) for by in range(1, n_time)]
    trials = ROWS // n_time
    total_segs = n_time * main_segs
    stride = PAD + total_segs
    peak_rows = channels * n_freq // LANES
    place_rows = -(-peak_rows // 8) * 8
    chunk = (main_segs + place_rows, LANES)
    pieces = call(
        functools.partial(
            final_kernel,
            level=level,
            section=last,
            n_time=n_time,
            main_segs=main_segs,
            trials=trials,
            place_rows=place_rows,
        ),
        (*tables, widths, *owns, *others),
        [chunk] * n_time,
        [
            (2 * ROWS * stride, LANES),
            (trials * total_segs, LANES),
            (trials * stride, LANES),
            (trials, LANES),
            (widths.shape[0], LANES),
        ],
        "final",
    )
    merged = pieces[0]
    for by in range(1, n_time):
        merged = jnp.maximum(merged, xor_permute(pieces[by], "tm", by))
    level = 0
    while level < cross:
        span_bits = min(2, cross - level)
        received = [xor_permute(merged, "freq", by << level) for by in range(1, 1 << span_bits)]
        for value in received:
            merged = jnp.maximum(merged, value)
        level += span_bits
    best_snr = merged[:main_segs].reshape(span)
    peaks = merged[main_segs : main_segs + peak_rows].reshape(peak_rows * LANES)
    trial_peak = lax.dynamic_slice_in_dim(peaks, freq * channels, channels)
    return (best_snr, trial_peak)


def solution(mesh):
    placed = (P("freq", "tm"), P(), P(), P())
    return jax.shard_map(
        shards, mesh=mesh, in_specs=placed, out_specs=(P("tm"), P("freq")), check_vma=False
    )
```

time: 746 us -> 61.3 us (0.08)
  local copies, waits for them, and re-layouts: 559 us -> 3.61 us
  blocking collectives: 85.5 us -> 0 us
  loops' own time: 38.6 us -> 0 us
  other arithmetic: 11.4 us -> 0.01 us
  Pallas kernels: 0 us -> 9.62 us
  waiting for transfers between devices: 20 us -> 28.5 us
    gather x1040 -> x0, local copies, waits for them, and re-layouts: 544 us -> none
    pmax x2 -> x0, blocking collectives: 80.6 us -> none  [the longest x1 40.4 us: shards(): best_snr = lax.pmax(jnp.max(running, axis=0), 'freq')]
    another operation x9 -> x0, loops' own time: 38.6 us -> none  [the longest x1 32.4 us: box_best(): running = lax.fori_loop(0, widths.shape[0], advance, start_best)]
    dynamic_slice x33 -> x1, local copies, waits for them, and re-layouts: 11.6 us -> 0.58 us  [shards(): trial_peak = lax.dynamic_slice_in_dim(peaks, freq * channels, channels)]
    pallas_call x0 -> x4, Pallas kernels: none -> 9.62 us  [call(): pl.pallas_call(kernel, out_shape=outs, in_specs=specs, out_specs=[VMEM] *...]
    ppermute x13 -> x15, waiting for transfers between devices: 20 us -> 28.5 us  [the longest x14 27.3 us: xor_permute(): lax.ppermute(value, axis, [(i, i ^ by) for i in range(lax.axis_size(axis))])]
    ppermute x13 -> x15, starting transfers between devices: 24.5 us -> 18.6 us  [the longest x14 16.3 us: xor_permute(): lax.ppermute(value, axis, [(i, i ^ by) for i in range(lax.axis_size(axis))])]
  transfers between devices with their start and end apart: 13 -> 15, of which waited for: 11 -> 12; matrix products, arithmetic and copies ran while one was open for 1% -> 0% of each run, Pallas kernels for 0% -> 0%
where the time goes in v1:
time: 61.3 us; the launch traced here: 61.1 us
  waiting for transfers between devices  28.5 us (46%)
  starting transfers between devices  18.6 us (30%)
  Pallas kernels  9.62 us (16%)
  local copies, waits for them, and re-layouts  3.61 us (6%)
  between operations  0.67 us (1%)
    ppermute x14, waiting for transfers between devices, xor_permute(): lax.ppermute(value, axis, [(i, i ^ by) for i in range(lax.axis_size(axis))])  27.3 us
    ppermute x14, starting transfers between devices, xor_permute(): lax.ppermute(value, axis, [(i, i ^ by) for i in range(lax.axis_size(axis))])  16.3 us
    pallas_call x4, Pallas kernels, call(): pl.pallas_call(kernel, out_shape=outs, in_specs=specs, out_specs=[VMEM] *...  9.62 us
    unnamed x12, local copies, waits for them, and re-layouts  2.43 us
    ppermute x1, starting transfers between devices, shift_right(): return lax.ppermute(value, axis, [(i, i + 1) for i in range(count - 1)])  2.36 us
  transfers between devices with their start and end apart: 15, of which 12 were waited for; matrix products, arithmetic and copies ran while one was open for 0% of the time, Pallas kernels for 0%

profile of v1, /device:TPU:0, one launch (start us, length us, event | category | flops | bytes accessed | tf_op | source)
XLA Modules:
  0.0 61.1 jit_solution(12007968278470761757)
XLA Ops:
  0.6 2.4 %collective-permute-start = (f32[32,1024]{1,0:T(8,128)}, f32[32,1024]{1,0:T(8,128)S(1)}, u32[]{:S(2)}, u32[]{:S(2)}) collective-permute-start(f32[32,1024]{1,0:T(8,128)} %x.1), channel_id=1, source_target_pairs={{0,1},{2,3},{4,5},{6,7},{8,9},{10,11},{12,13},{14,15},{16,17},{18,... | collective-permute-start | bytes 393224 | tf_op jit(solution)/shard_map/ppermute | solution.py:26
  3.0 1.2 %collective-permute-done.left = f32[32,1024]{1,0:T(8,128)S(1)} collective-permute-done((f32[32,1024]{1,0:T(8,128)}, f32[32,1024]{1,0:T(8,128)S(1)}, u32[]{:S(2)}, u32[]{:S(2)}) %collective-permute-start) | collective-permute-done | bytes 131104 | tf_op jit(solution)/shard_map/ppermute | solution.py:26
  4.2 0.0 copy-start
  4.2 0.8 %copy-done = s32[9,512]{1,0:T(8,128)S(1)} copy-done((s32[9,512]{1,0:T(8,128)S(1)}, s32[9,512]{1,0:T(8,128)}, u32[]{:S(2)}) %copy-start) | copy-done | bytes 18456
  4.9 0.0 copy-start.2
  4.9 0.8 %copy-done.2 = s32[9,512]{1,0:T(8,128)S(1)} copy-done((s32[9,512]{1,0:T(8,128)S(1)}, s32[9,512]{1,0:T(8,128)}, u32[]{:S(2)}) %copy-start.2) | copy-done | bytes 18456
  5.7 0.0 copy-start.4
  5.7 0.9 %copy-done.4 = f32[32,1024]{1,0:T(8,128)S(1)} copy-done((f32[32,1024]{1,0:T(8,128)S(1)}, f32[32,1024]{1,0:T(8,128)}, u32[]{:S(2)}) %copy-start.4) | copy-done | bytes 131096
  6.6 0.0 copy-start.1
  6.6 0.0 copy-start.3
  6.6 2.3 %local.1.own = f32[320,128]{1,0:T(8,128)S(1)} custom-call(s32[9,512]{1,0:T(8,128)S(1)} %copy-done, s32[9,512]{1,0:T(8,128)S(1)} %copy-done.2, f32[32,1024]{1,0:T(8,128)S(1)} %copy-done.4, f32[32,1024]{1,0:T(8,128)S(1)} %collective-permute-done.left), custom_call_target="tpu_custom_call" | custom-call | tf_op jit(solution)/shard_map/local/pallas_call | solution.py:253
  8.9 2.4 %collective-permute-start.1 = (f32[320,128]{1,0:T(8,128)S(1)}, f32[320,128]{1,0:T(8,128)S(1)}, u32[]{:S(2)}, u32[]{:S(2)}) collective-permute-start(f32[320,128]{1,0:T(8,128)S(1)} %local.1.own), channel_id=1, source_target_pairs={{0,2},{2,0},{4,6},{6,4},{8,10},{10,8},{12,14},{14,12},{16,18},{18,... | collective-permute-start | bytes 491528 | tf_op jit(solution)/shard_map/ppermute | solution.py:21
  11.3 1.5 %collective-permute-start.2 = (f32[320,128]{1,0:T(8,128)S(1)}, f32[320,128]{1,0:T(8,128)S(1)}, u32[]{:S(2)}, u32[]{:S(2)}) collective-permute-start(f32[320,128]{1,0:T(8,128)S(1)} %local.1.own), channel_id=1, source_target_pairs={{0,4},{2,6},{4,0},{6,2},{8,12},{10,14},{12,8},{14,10},{16,20},{18,... | collective-permute-start | bytes 491528 | tf_op jit(solution)/shard_map/ppermute | solution.py:21
  12.9 0.0 collective-permute-start.3
  12.9 3.5 %collective-permute-done.1.one = f32[320,128]{1,0:T(8,128)S(1)} collective-permute-done((f32[320,128]{1,0:T(8,128)S(1)}, f32[320,128]{1,0:T(8,128)S(1)}, u32[]{:S(2)}, u32[]{:S(2)}) %collective-permute-start.1) | collective-permute-done | bytes 163872 | tf_op jit(solution)/shard_map/ppermute | solution.py:21
  16.4 4.6 %collective-permute-done.2.two = f32[320,128]{1,0:T(8,128)S(1)} collective-permute-done((f32[320,128]{1,0:T(8,128)S(1)}, f32[320,128]{1,0:T(8,128)S(1)}, u32[]{:S(2)}, u32[]{:S(2)}) %collective-permute-start.2) | collective-permute-done | bytes 163872 | tf_op jit(solution)/shard_map/ppermute | solution.py:21
  21.0 0.0 collective-permute-done.3.three
  21.0 0.0 copy-done.1
  21.0 0.0 copy-done.3
  21.0 2.2 %quad.1.own = f32[288,128]{1,0:T(8,128)S(1)} custom-call(s32[9,512]{1,0:T(8,128)S(1)} %copy-done.1, s32[9,512]{1,0:T(8,128)S(1)} %copy-done.3, f32[320,128]{1,0:T(8,128)S(1)} %local.1.own, f32[320,128]{1,0:T(8,128)S(1)} %collective-permute-done.1.one, f32[320,128]{1,0:T(8,128)S(1)} %collective-permute-done.2.two, f32[320,128]{1,0:T(8,128)S(1)} %collective-permute-done.3.three), custom_call_target="tpu_custom_call" | custom-call | tf_op jit(solution)/shard_map/quad/pallas_call | solution.py:253
  23.3 0.0 copy-start.5
  23.3 1.6 %collective-permute-start.4 = (f32[288,128]{1,0:T(8,128)S(1)}, f32[288,128]{1,0:T(8,128)S(1)}, u32[]{:S(2)}, u32[]{:S(2)}) collective-permute-start(f32[288,128]{1,0:T(8,128)S(1)} %quad.1.own), channel_id=1, source_target_pairs={{0,8},{2,10},{4,12},{6,14},{8,0},{10,2},{12,4},{14,6},{16,24},{18,... | collective-permute-start | bytes 442376 | tf_op jit(solution)/shard_map/ppermute | solution.py:21
  24.9 3.6 %collective-permute-done.4.other = f32[288,128]{1,0:T(8,128)S(1)} collective-permute-done((f32[288,128]{1,0:T(8,128)S(1)}, f32[288,128]{1,0:T(8,128)S(1)}, u32[]{:S(2)}, u32[]{:S(2)}) %collective-permute-start.4) | collective-permute-done | bytes 147488 | tf_op jit(solution)/shard_map/ppermute | solution.py:21
  28.5 1.9 %pair.1.refs_0_ = f32[256,128]{1,0:T(8,128)S(1)} custom-call(s32[9,512]{1,0:T(8,128)S(1)} %copy-done.1, s32[9,512]{1,0:T(8,128)S(1)} %copy-done.3, f32[288,128]{1,0:T(8,128)S(1)} %quad.1.own, f32[288,128]{1,0:T(8,128)S(1)} %collective-permute-done.4.other), custom_call_target="tpu_custom_call" | custom-call | tf_op jit(solution)/shard_map/pair/pallas_call | solution.py:253
  30.3 2.6 %collective-permute-start.6 = (f32[256,128]{1,0:T(8,128)S(1)}, f32[256,128]{1,0:T(8,128)S(1)}, u32[]{:S(2)}, u32[]{:S(2)}) collective-permute-start(f32[256,128]{1,0:T(8,128)S(1)} %pair.1.refs_0_), channel_id=1, source_target_pairs={{0,16},{2,18},{4,20},{6,22},{8,24},{10,26},{12,28},{14,30},{16,0},... | collective-permute-start | bytes 393224 | tf_op jit(solution)/shard_map/ppermute | solution.py:21
  33.0 0.0 collective-permute-start.5
  33.0 4.7 %collective-permute-done.6.refs_2_ = f32[256,128]{1,0:T(8,128)S(1)} collective-permute-done((f32[256,128]{1,0:T(8,128)S(1)}, f32[256,128]{1,0:T(8,128)S(1)}, u32[]{:S(2)}, u32[]{:S(2)}) %collective-permute-start.6) | collective-permute-done | bytes 131104 | tf_op jit(solution)/shard_map/ppermute | solution.py:21
  37.7 0.0 collective-permute-start.7
  37.7 0.0 collective-permute-done.5.refs_1_
  37.7 1.3 %collective-permute-done.7.refs_3_ = f32[256,128]{1,0:T(8,128)S(1)} collective-permute-done((f32[256,128]{1,0:T(8,128)S(1)}, f32[256,128]{1,0:T(8,128)S(1)}, u32[]{:S(2)}, u32[]{:S(2)}) %collective-permute-start.7) | collective-permute-done | bytes 131104 | tf_op jit(solution)/shard_map/ppermute | solution.py:21
  39.0 0.0 copy-done.5
  39.0 3.2 %final.1 = (f32[16,128]{1,0:T(8,128)S(1)}, f32[16,128]{1,0:T(8,128)S(1)}) custom-call(s32[9,512]{1,0:T(8,128)S(1)} %copy-done.1, s32[9,512]{1,0:T(8,128)S(1)} %copy-done.3, s32[16]{0:T(128)S(1)} %copy-done.5, f32[256,128]{1,0:T(8,128)S(1)} %pair.1.refs_0_, f32[256,128]{1,0:T(8,128)S(1)} %collective-permute-done.5.refs_1_, ...), custom_call_target="tpu_custom_call" | custom-call | tf_op jit(solution)/shard_map/final/pallas_call | solution.py:253
  42.2 0.2 collective-permute-start.8
  42.4 1.0 %collective-permute-done.8 = f32[16,128]{1,0:T(8,128)S(1)} collective-permute-done((f32[16,128]{1,0:T(8,128)S(1)}, f32[16,128]{1,0:T(8,128)S(1)}, u32[]{:S(2)}, u32[]{:S(2)}) %collective-permute-start.8) | collective-permute-done | bytes 8224 | tf_op jit(solution)/shard_map/ppermute | solution.py:21
  43.4 1.5 %collective-permute-start.10 = (f32[16,128]{1,0:T(8,128)S(1)}, f32[16,128]{1,0:T(8,128)S(1)}, u32[]{:S(2)}, u32[]{:S(2)}) collective-permute-start(f32[16,128]{1,0:T(8,128)S(1)} %max.21), channel_id=1, source_target_pairs={{0,4},{2,6},{4,0},{6,2},{8,12},{10,14},{12,8},{14,10},{16,20},{18,... | collective-permute-start | bytes 24584 | tf_op jit(solution)/shard_map/ppermute | solution.py:21
  44.9 1.8 %collective-permute-start.11 = (f32[16,128]{1,0:T(8,128)S(1)}, f32[16,128]{1,0:T(8,128)S(1)}, u32[]{:S(2)}, u32[]{:S(2)}) collective-permute-start(f32[16,128]{1,0:T(8,128)S(1)} %max.21), channel_id=1, source_target_pairs={{0,6},{2,4},{4,2},{6,0},{8,14},{10,12},{12,10},{14,8},{16,22},{18,... | collective-permute-start | bytes 24584 | tf_op jit(solution)/shard_map/ppermute | solution.py:21
  46.7 0.2 collective-permute-start.9
  46.9 0.2 collective-permute-done.10
  47.1 2.4 %collective-permute-done.11 = f32[16,128]{1,0:T(8,128)S(1)} collective-permute-done((f32[16,128]{1,0:T(8,128)S(1)}, f32[16,128]{1,0:T(8,128)S(1)}, u32[]{:S(2)}, u32[]{:S(2)}) %collective-permute-start.11) | collective-permute-done | bytes 8224 | tf_op jit(solution)/shard_map/ppermute | solution.py:21
  49.5 0.9 %collective-permute-done.9 = f32[16,128]{1,0:T(8,128)S(1)} collective-permute-done((f32[16,128]{1,0:T(8,128)S(1)}, f32[16,128]{1,0:T(8,128)S(1)}, u32[]{:S(2)}, u32[]{:S(2)}) %collective-permute-start.9) | collective-permute-done | bytes 8224 | tf_op jit(solution)/shard_map/ppermute | solution.py:21
  50.4 0.7 %collective-permute-start.12 = (f32[16,128]{1,0:T(8,128)S(1)}, f32[16,128]{1,0:T(8,128)S(1)}, u32[]{:S(2)}, u32[]{:S(2)}) collective-permute-start(f32[16,128]{1,0:T(8,128)S(1)} %maximum_maximum_fusion.1), channel_id=1, source_target_pairs={{0,8},{2,10},{4,12},{6,14},{8,0},{10,2},{12,4},{14,6},{16,24},{18,... | collective-permute-start | bytes 24584 | tf_op jit(solution)/shard_map/ppermute | solution.py:21
  51.0 3.4 %collective-permute-start.13 = (f32[16,128]{1,0:T(8,128)S(1)}, f32[16,128]{1,0:T(8,128)S(1)}, u32[]{:S(2)}, u32[]{:S(2)}) collective-permute-start(f32[16,128]{1,0:T(8,128)S(1)} %maximum_maximum_fusion.1), channel_id=1, source_target_pairs={{0,16},{2,18},{4,20},{6,22},{8,24},{10,26},{12,28},{14,30},{16,0},... | collective-permute-start | bytes 24584 | tf_op jit(solution)/shard_map/ppermute | solution.py:21
  54.4 0.3 collective-permute-start.14
  54.8 0.0 collective-permute-done.12
  54.8 1.3 %collective-permute-done.13 = f32[16,128]{1,0:T(8,128)S(1)} collective-permute-done((f32[16,128]{1,0:T(8,128)S(1)}, f32[16,128]{1,0:T(8,128)S(1)}, u32[]{:S(2)}, u32[]{:S(2)}) %collective-permute-start.13) | collective-permute-done | bytes 8224 | tf_op jit(solution)/shard_map/ppermute | solution.py:21
  56.0 3.8 %collective-permute-done.14 = f32[16,128]{1,0:T(8,128)S(1)} collective-permute-done((f32[16,128]{1,0:T(8,128)S(1)}, f32[16,128]{1,0:T(8,128)S(1)}, u32[]{:S(2)}, u32[]{:S(2)}) %collective-permute-start.14) | collective-permute-done | bytes 8224 | tf_op jit(solution)/shard_map/ppermute | solution.py:21
  59.9 0.6 slice_bitcast_fusion
  60.5 0.6 dynamic_slice.3
  (4 shorter events, 0.0 us)
Async XLA Ops:
  0.6 3.5 %collective-permute-start = (f32[32,1024]{1,0:T(8,128)}, f32[32,1024]{1,0:T(8,128)S(1)}, u32[]{:S(2)}, u32[]{:S(2)}) collective-permute-start(f32[32,1024]{1,0:T(8,128)} %x.1), channel_id=1, source_target_pairs={{0,1},{2,3},{4,5},{6,7},{8,9},{10,11},{12,13},{14,15},{16,17},{18,... | collective-permute-start | bytes 393224 | tf_op jit(solution)/shard_map/ppermute | solution.py:26
  4.2 0.8 %copy-start = (s32[9,512]{1,0:T(8,128)S(1)}, s32[9,512]{1,0:T(8,128)}, u32[]{:S(2)}) copy-start(s32[9,512]{1,0:T(8,128)} %lead.7) | copy-start | bytes 55300
  4.9 0.8 %copy-start.2 = (s32[9,512]{1,0:T(8,128)S(1)}, s32[9,512]{1,0:T(8,128)}, u32[]{:S(2)}) copy-start(s32[9,512]{1,0:T(8,128)} %tail.7) | copy-start | bytes 55300
  5.7 0.9 %copy-start.4 = (f32[32,1024]{1,0:T(8,128)S(1)}, f32[32,1024]{1,0:T(8,128)}, u32[]{:S(2)}) copy-start(f32[32,1024]{1,0:T(8,128)} %x.1) | copy-start | bytes 393220
  6.6 14.4 %copy-start.1 = (s32[9,512]{1,0:T(8,128)S(1)}, s32[9,512]{1,0:T(8,128)}, u32[]{:S(2)}) copy-start(s32[9,512]{1,0:T(8,128)} %lead.7) | copy-start | bytes 55300
  6.6 14.4 %copy-start.3 = (s32[9,512]{1,0:T(8,128)S(1)}, s32[9,512]{1,0:T(8,128)}, u32[]{:S(2)}) copy-start(s32[9,512]{1,0:T(8,128)} %tail.7) | copy-start | bytes 55300
  8.9 7.4 %collective-permute-start.1 = (f32[320,128]{1,0:T(8,128)S(1)}, f32[320,128]{1,0:T(8,128)S(1)}, u32[]{:S(2)}, u32[]{:S(2)}) collective-permute-start(f32[320,128]{1,0:T(8,128)S(1)} %local.1.own), channel_id=1, source_target_pairs={{0,2},{2,0},{4,6},{6,4},{8,10},{10,8},{12,14},{14,12},{16,18},{18,... | collective-permute-start | bytes 491528 | tf_op jit(solution)/shard_map/ppermute | solution.py:21
  11.3 9.7 %collective-permute-start.2 = (f32[320,128]{1,0:T(8,128)S(1)}, f32[320,128]{1,0:T(8,128)S(1)}, u32[]{:S(2)}, u32[]{:S(2)}) collective-permute-start(f32[320,128]{1,0:T(8,128)S(1)} %local.1.own), channel_id=1, source_target_pairs={{0,4},{2,6},{4,0},{6,2},{8,12},{10,14},{12,8},{14,10},{16,20},{18,... | collective-permute-start | bytes 491528 | tf_op jit(solution)/shard_map/ppermute | solution.py:21
  12.9 8.2 %collective-permute-start.3 = (f32[320,128]{1,0:T(8,128)S(1)}, f32[320,128]{1,0:T(8,128)S(1)}, u32[]{:S(2)}, u32[]{:S(2)}) collective-permute-start(f32[320,128]{1,0:T(8,128)S(1)} %local.1.own), channel_id=1, source_target_pairs={{0,6},{2,4},{4,2},{6,0},{8,14},{10,12},{12,10},{14,8},{16,22},{18,... | collective-permute-start | bytes 491528 | tf_op jit(solution)/shard_map/ppermute | solution.py:21
  23.3 15.8 %copy-start.5 = (s32[16]{0:T(128)S(1)}, s32[16]{0:T(128)}, u32[]{:S(2)}) copy-start(s32[16]{0:T(128)} %widths.1) | copy-start | bytes 196
  23.3 5.2 %collective-permute-start.4 = (f32[288,128]{1,0:T(8,128)S(1)}, f32[288,128]{1,0:T(8,128)S(1)}, u32[]{:S(2)}, u32[]{:S(2)}) collective-permute-start(f32[288,128]{1,0:T(8,128)S(1)} %quad.1.own), channel_id=1, source_target_pairs={{0,8},{2,10},{4,12},{6,14},{8,0},{10,2},{12,4},{14,6},{16,24},{18,... | collective-permute-start | bytes 442376 | tf_op jit(solution)/shard_map/ppermute | solution.py:21
  30.3 7.3 %collective-permute-start.6 = (f32[256,128]{1,0:T(8,128)S(1)}, f32[256,128]{1,0:T(8,128)S(1)}, u32[]{:S(2)}, u32[]{:S(2)}) collective-permute-start(f32[256,128]{1,0:T(8,128)S(1)} %pair.1.refs_0_), channel_id=1, source_target_pairs={{0,16},{2,18},{4,20},{6,22},{8,24},{10,26},{12,28},{14,30},{16,0},... | collective-permute-start | bytes 393224 | tf_op jit(solution)/shard_map/ppermute | solution.py:21
  33.0 4.7 %collective-permute-start.5 = (f32[256,128]{1,0:T(8,128)S(1)}, f32[256,128]{1,0:T(8,128)S(1)}, u32[]{:S(2)}, u32[]{:S(2)}) collective-permute-start(f32[256,128]{1,0:T(8,128)S(1)} %pair.1.refs_0_), channel_id=1, source_target_pairs={{0,1},{1,0},{2,3},{3,2},{4,5},{5,4},{6,7},{7,6},{8,9},{9,8},{10,11... | collective-permute-start | bytes 393224 | tf_op jit(solution)/shard_map/ppermute | solution.py:21
  37.7 1.3 %collective-permute-start.7 = (f32[256,128]{1,0:T(8,128)S(1)}, f32[256,128]{1,0:T(8,128)S(1)}, u32[]{:S(2)}, u32[]{:S(2)}) collective-permute-start(f32[256,128]{1,0:T(8,128)S(1)} %collective-permute-done.6.refs_2_), channel_id=1, source_target_pairs={{0,1},{1,0},{2,3},{3,2},{4,5},{5,4},{6,7},{7,6},{8,9},{9,8},{10,11... | collective-permute-start | bytes 393224 | tf_op jit(solution)/shard_map/ppermute | solution.py:21
  42.2 1.2 %collective-permute-start.8 = (f32[16,128]{1,0:T(8,128)S(1)}, f32[16,128]{1,0:T(8,128)S(1)}, u32[]{:S(2)}, u32[]{:S(2)}) collective-permute-start(f32[16,128]{1,0:T(8,128)S(1)} %get-tuple-element.5), channel_id=1, source_target_pairs={{0,1},{1,0},{2,3},{3,2},{4,5},{5,4},{6,7},{7,6},{8,9},{9,8},{10,11... | collective-permute-start | bytes 24584 | tf_op jit(solution)/shard_map/ppermute | solution.py:21
  43.4 3.7 %collective-permute-start.10 = (f32[16,128]{1,0:T(8,128)S(1)}, f32[16,128]{1,0:T(8,128)S(1)}, u32[]{:S(2)}, u32[]{:S(2)}) collective-permute-start(f32[16,128]{1,0:T(8,128)S(1)} %max.21), channel_id=1, source_target_pairs={{0,4},{2,6},{4,0},{6,2},{8,12},{10,14},{12,8},{14,10},{16,20},{18,... | collective-permute-start | bytes 24584 | tf_op jit(solution)/shard_map/ppermute | solution.py:21
  44.9 4.5 %collective-permute-start.11 = (f32[16,128]{1,0:T(8,128)S(1)}, f32[16,128]{1,0:T(8,128)S(1)}, u32[]{:S(2)}, u32[]{:S(2)}) collective-permute-start(f32[16,128]{1,0:T(8,128)S(1)} %max.21), channel_id=1, source_target_pairs={{0,6},{2,4},{4,2},{6,0},{8,14},{10,12},{12,10},{14,8},{16,22},{18,... | collective-permute-start | bytes 24584 | tf_op jit(solution)/shard_map/ppermute | solution.py:21
  46.7 3.7 %collective-permute-start.9 = (f32[16,128]{1,0:T(8,128)S(1)}, f32[16,128]{1,0:T(8,128)S(1)}, u32[]{:S(2)}, u32[]{:S(2)}) collective-permute-start(f32[16,128]{1,0:T(8,128)S(1)} %max.21), channel_id=1, source_target_pairs={{0,2},{2,0},{4,6},{6,4},{8,10},{10,8},{12,14},{14,12},{16,18},{18,... | collective-permute-start | bytes 24584 | tf_op jit(solution)/shard_map/ppermute | solution.py:21
  50.4 4.4 %collective-permute-start.12 = (f32[16,128]{1,0:T(8,128)S(1)}, f32[16,128]{1,0:T(8,128)S(1)}, u32[]{:S(2)}, u32[]{:S(2)}) collective-permute-start(f32[16,128]{1,0:T(8,128)S(1)} %maximum_maximum_fusion.1), channel_id=1, source_target_pairs={{0,8},{2,10},{4,12},{6,14},{8,0},{10,2},{12,4},{14,6},{16,24},{18,... | collective-permute-start | bytes 24584 | tf_op jit(solution)/shard_map/ppermute | solution.py:21
  51.0 5.0 %collective-permute-start.13 = (f32[16,128]{1,0:T(8,128)S(1)}, f32[16,128]{1,0:T(8,128)S(1)}, u32[]{:S(2)}, u32[]{:S(2)}) collective-permute-start(f32[16,128]{1,0:T(8,128)S(1)} %maximum_maximum_fusion.1), channel_id=1, source_target_pairs={{0,16},{2,18},{4,20},{6,22},{8,24},{10,26},{12,28},{14,30},{16,0},... | collective-permute-start | bytes 24584 | tf_op jit(solution)/shard_map/ppermute | solution.py:21
  54.4 5.4 %collective-permute-start.14 = (f32[16,128]{1,0:T(8,128)S(1)}, f32[16,128]{1,0:T(8,128)S(1)}, u32[]{:S(2)}, u32[]{:S(2)}) collective-permute-start(f32[16,128]{1,0:T(8,128)S(1)} %maximum_maximum_fusion.1), channel_id=1, source_target_pairs={{0,24},{2,26},{4,28},{6,30},{8,16},{10,18},{12,20},{14,22},{16,8},... | collective-permute-start | bytes 24584 | tf_op jit(solution)/shard_map/ppermute | solution.py:21

commit v2 on v0

v2 whole, which is shorter than its diff:
```python
import functools

import jax
import jax.numpy as jnp
from jax import lax
from jax.experimental import pallas as pl
from jax.experimental.pallas import tpu as pltpu
from jax.sharding import PartitionSpec as P

LANES = 128
ROWS = 32
PAD = 8

eps_var = 1e-06
VMEM = pl.BlockSpec(memory_space=pltpu.VMEM)
ANY = pl.BlockSpec(memory_space=pl.ANY)


def xor_permute(value, axis, by):
    return lax.ppermute(value, axis, [(i, i ^ by) for i in range(lax.axis_size(axis))])


def shift_right(value, axis):
    count = lax.axis_size(axis)
    return lax.ppermute(value, axis, [(i, i + 1) for i in range(count - 1)])


def section_rows(src, src_row, dst, dst_row, segs, rows, table, far, group=16):
    lane = lax.broadcasted_iota(jnp.int32, (segs, LANES), 1)
    for first in range(0, rows, group):
        picked = []
        for k in range(first, min(first + group, rows)):
            low, up, delay = table(k)
            start = src_row(up)
            if far:
                start = start - (delay >> 7)
                delay = delay & (LANES - 1)
            lower = src[pl.ds(src_row(low), segs), :]
            picked.append((k, delay, lower, src[pl.ds(start, segs), :], src[pl.ds(start - 1, segs), :]))
        for k, delay, lower, here, before in picked:
            mixed = jnp.where(lane < LANES - delay, here, before)
            dst[pl.ds(dst_row(k), segs), :] = lower + pltpu.roll(mixed, delay, axis=1)


def window(start):
    return pl.multiple_of((start // LANES) * LANES, LANES)


def order_of(freq, stage):
    order = 0
    for n in range(stage):
        order = 4 * order + ((freq >> (2 * n)) & 3)
    return order


def pair_kernel(x, out, tip, stage, *, halo):
    channels, span = x.shape
    segs = span // LANES
    for seg in range(segs):
        stage[pl.ds(seg * channels, channels), :] = x[:, pl.ds(seg * LANES, LANES)]
    for seg in range(segs):
        first = seg * channels
        half = channels // 2
        summed = stage[pl.ds(first, half, stride=2), :] + stage[pl.ds(first + 1, half, stride=2), :]
        out[pl.ds(seg, half, stride=segs), :] = summed
        if seg >= segs - halo:
            if halo == 1:
                tip[...] = summed
            else:
                tip[pl.ds(seg - segs + halo, half, stride=halo), :] = summed


def join_kernel(main, tip, out, *, segs, main_segs):
    halo = segs - main_segs
    for row in range(main.shape[0] // main_segs):
        out[pl.ds(row * segs, halo), :] = tip[pl.ds(row * halo, halo), :]
        out[pl.ds(row * segs + halo, main_segs), :] = main[pl.ds(row * main_segs, main_segs), :]


def quad_kernel(lead_all, tail_all, *refs, stage, section, local, segs_of):
    inputs, out = refs[:4], refs[4]
    buf_a, buf_b, lead, tail, sems = refs[5:]
    freq = lax.axis_index("freq")
    place = (freq >> (2 * stage)) & 3
    order = order_of(freq, stage)
    rows_in = 2**section
    base = (freq >> (2 * stage + 2)) * (4 * rows_in)
    half_order = 2 * order + place // 2
    starts = [base + ROWS * half_order, base + 2 * rows_in + ROWS * half_order]
    last_start = base + ROWS * (4 * order + place)
    wheres = [base] if local else [*starts, last_start]
    copies = []
    for n, where in enumerate(wheres):
        for table, to in ((lead_all, lead), (tail_all, tail)):
            copies.append(
                pltpu.make_async_copy(table.at[:, pl.ds(window(where), LANES)], to.at[n], sems.at[len(copies)])
            )
    for copy in copies:
        copy.start()
    segs = segs_of(1) if local else segs_of(section)
    size = inputs[0].shape[0]
    buf_a[pl.ds(0, PAD), :] = jnp.zeros((PAD, LANES), jnp.float32)
    buf_b[pl.ds(0, PAD), :] = jnp.zeros((PAD, LANES), jnp.float32)
    for by, ref in enumerate(inputs):
        to = pl.multiple_of(PAD + (place ^ by) * size, 8)
        buf_a[pl.ds(to, size), :] = ref[...]
    for copy in copies:
        copy.wait()
    src, dst = buf_a, buf_b
    for now in range(1, local):
        reach = 2**now

        def local_table(k, now=now, reach=reach):
            e, h = lead[0, now, k], tail[0, now, k]
            band = k // (2 * reach)
            if now == 1:
                return 2 * band, 2 * band + 1, e
            return 2 * band * reach + e, (2 * band + 1) * reach + h, e

        def at_row(row):
            return PAD + row * segs

        section_rows(src, at_row, dst, at_row, segs, 4 * ROWS, local_table, False)
        src, dst = dst, src
    in_segs = segs
    mid_segs, out_segs = segs_of(section + 1), segs_of(section + 2)

    def mid_table(k):
        band = k // ROWS
        if local:
            slot, column = 0, 2 * ROWS * band + ROWS * half_order + k % ROWS
        else:
            slot, column = band, starts[band] % LANES + k % ROWS
        e, h = lead[slot, section, column], tail[slot, section, column]
        return 2 * band * ROWS + e - ROWS * order, (2 * band + 1) * ROWS + h - ROWS * order, e

    section_rows(
        src,
        lambda row: PAD + row * in_segs + in_segs - mid_segs,
        dst,
        lambda row: PAD + row * mid_segs,
        mid_segs,
        2 * ROWS,
        mid_table,
        rows_in > LANES,
    )

    def last_table(k):
        slot = 0 if local else 2
        column = last_start % LANES + k
        e, h = lead[slot, section + 1, column], tail[slot, section + 1, column]
        return e - ROWS * half_order, ROWS + h - ROWS * half_order, e

    section_rows(
        dst,
        lambda row: PAD + row * mid_segs + mid_segs - out_segs,
        out,
        lambda row: row * out_segs,
        out_segs,
        ROWS,
        last_table,
        2 * rows_in > LANES,
    )


def final_kernel(lead_all, tail_all, widths_all, *refs, stage, section, n_time, main_segs, trials, place_rows):
    own, moved = refs[:4], refs[4 : 3 + n_time]
    outs = refs[3 + n_time : 3 + 2 * n_time]
    buf, mid, data, edges, over, scale, lead, tail, widths, sems = refs[3 + 2 * n_time :]
    freq = lax.axis_index("freq")
    tm = lax.axis_index("tm")
    place = (freq >> (2 * stage)) & 3
    order = order_of(freq, stage)
    rows_in = 2**section
    first_trial = 4 * ROWS * order + trials * tm
    half_order = first_trial // (2 * ROWS)
    starts = [ROWS * half_order, 2 * rows_in + ROWS * half_order, first_trial]
    copies = [pltpu.make_async_copy(widths_all, widths, sems.at[0])]
    for n, (where, row) in enumerate(zip(starts, (section, section, section + 1))):
        for table, to in ((lead_all, lead), (tail_all, tail)):
            part = table.at[pl.ds(row, 1), pl.ds(window(where), LANES)]
            copies.append(pltpu.make_async_copy(part, to.at[pl.ds(n, 1)], sems.at[len(copies)]))
    for copy in copies:
        copy.start()
    total_segs = n_time * main_segs
    total_time = total_segs * LANES
    stride = PAD + total_segs
    zeros = jnp.zeros((PAD, LANES), jnp.float32)
    for row in range(4 * ROWS):
        buf[pl.ds(row * stride, PAD), :] = zeros
    for row in range(2 * ROWS):
        mid[pl.ds(row * stride, PAD), :] = zeros
    size = ROWS * main_segs
    for by_band in range(4):
        for by_time in range(n_time):
            start = (place ^ by_band) * (ROWS * stride) + PAD + (tm ^ by_time) * main_segs
            ref, at = (own[by_band], 0) if by_time == 0 else (moved[by_time - 1], by_band * size)
            for row in range(ROWS):
                to = pl.multiple_of(start + row * stride, 8)
                buf[pl.ds(to, main_segs), :] = ref[pl.ds(at + row * main_segs, main_segs), :]
    for copy in copies:
        copy.wait()

    def at_row(row):
        return row * stride + PAD

    def mid_table(k):
        band = k // ROWS
        column = starts[0] % LANES + k % ROWS
        e, h = lead[band, column], tail[band, column]
        return 2 * band * ROWS + e - ROWS * order, (2 * band + 1) * ROWS + h - ROWS * order, e

    section_rows(buf, at_row, mid, at_row, total_segs, 2 * ROWS, mid_table, rows_in > LANES)

    def last_table(k):
        column = first_trial % LANES + k
        e, h = lead[2, column], tail[2, column]
        return e - ROWS * half_order, ROWS + h - ROWS * half_order, e

    def data_row(row):
        return row * total_segs

    section_rows(mid, at_row, data, data_row, total_segs, trials, last_table, 2 * rows_in > LANES)

    def samples(seg):
        return data[pl.ds(seg, trials, stride=total_segs), :]

    total = samples(0)
    for seg in range(1, total_segs):
        total = total + samples(seg)
    mean = jnp.sum(total, axis=1, keepdims=True) / total_time

    row_at = lax.broadcasted_iota(jnp.int32, (2 * LANES, LANES), 0)
    column_at = lax.broadcasted_iota(jnp.int32, (2 * LANES, LANES), 1)
    after = jnp.where(column_at > row_at, -1.0, 0.0)
    upto = jnp.where(column_at <= row_at - LANES, 1.0, 0.0)
    ones = jnp.where(row_at < LANES, after, upto).astype(jnp.bfloat16)
    ones = jnp.concatenate([ones] * 3, axis=1)
    squares = jnp.zeros((trials, LANES), jnp.float32)
    for seg in range(-1, main_segs):
        parts = []
        for part in range(n_time):
            at = part * main_segs + seg
            centred = samples(at) - mean if at >= 0 else jnp.zeros((trials, LANES), jnp.float32)
            if seg >= 0:
                squares = squares + centred * centred
            parts.append(centred)
        values = jnp.concatenate(parts, axis=0)
        terms = []
        for _ in range(3):
            term = values.astype(jnp.bfloat16)
            terms.append(term)
            values = values - term.astype(jnp.float32)
        both = lax.dot_general(
            ones,
            jnp.concatenate(terms, axis=1),
            (((1,), (1,)), ((), ())),
            preferred_element_type=jnp.float32,
        )
        if seg + 1 < main_segs:
            edges[pl.ds((seg + 1) * 2 * LANES, LANES), :] = both[:LANES]
        if seg >= 0:
            edges[pl.ds(seg * 2 * LANES + LANES, LANES), :] = both[LANES:]
    squares = jnp.sum(squares, axis=1, keepdims=True)
    inverse = 1.0 / jnp.sqrt(squares / total_time + eps_var)
    inverse = jnp.concatenate([jnp.broadcast_to(inverse, (trials, LANES))] * n_time, axis=0).T[:8]

    count = widths.shape[0]
    for j in range(count):
        scale[pl.ds(j * 8, 8), :] = jnp.full((8, LANES), widths[j], jnp.int32).astype(jnp.float32)
    scale[...] = 1.0 / jnp.sqrt(scale[...])
    tall = 64

    def spread_rows(value):
        return jnp.concatenate([value] * (tall // 8), axis=0)

    def fold(value):
        out = value[:8]
        for n in range(8, value.shape[0], 8):
            out = jnp.maximum(out, value[n : n + 8])
        return out

    peaks = jnp.full((8, LANES), -jnp.inf, jnp.float32)
    for seg in range(main_segs):
        blocks = []
        for first in range(0, LANES, tall):
            at = seg * 2 * LANES + LANES + first
            ends = edges[pl.ds(at, tall), :]
            best = None
            for j in range(count):
                score = (ends - edges[pl.ds(at - widths[j], tall), :]) * spread_rows(scale[pl.ds(j * 8, 8), :])
                best = score if j == 0 else jnp.maximum(best, score)
            best = best * spread_rows(inverse)
            peaks = jnp.maximum(peaks, fold(best))
            blocks.append(best)
        turned = jnp.concatenate(blocks, axis=0).T
        for part in range(n_time):
            over[pl.ds((part * main_segs + seg) * 8, 8), :] = fold(turned[part * trials : (part + 1) * trials])
    best_all = over[pl.ds(0, total_segs, stride=8), :]
    for n in range(1, 8):
        best_all = jnp.maximum(best_all, over[pl.ds(n, total_segs, stride=8), :])
    buf[pl.ds(0, total_segs), :] = best_all
    peak_row = jnp.max(peaks, axis=0, keepdims=True)
    step = trials
    while step < LANES:
        peak_row = jnp.maximum(peak_row, pltpu.roll(peak_row, step, axis=1))
        step *= 2
    offset = first_trial % LANES
    lane = lax.broadcasted_iota(jnp.int32, (1, LANES), 1)
    peak_row = jnp.where((lane >= offset) & (lane < offset + trials), peak_row, -jnp.inf)
    for by in range(n_time):
        at = pl.multiple_of((tm ^ by) * main_segs, 8)
        outs[by][pl.ds(0, main_segs), :] = buf[pl.ds(at, main_segs), :]
        outs[by][pl.ds(main_segs, place_rows), :] = jnp.full((place_rows, LANES), -jnp.inf, jnp.float32)
        outs[by][pl.ds(main_segs + first_trial // LANES, 1), :] = peak_row


def call(kernel, name, inputs, out_shapes, scratch=(), tables=()):
    outs = [jax.ShapeDtypeStruct(shape, jnp.float32) for shape in out_shapes]
    used = sum(4 * v.size for v in inputs) + sum(4 * o.size for o in outs)
    used += sum(4 * s.shape[0] * s.shape[1] for s in scratch if len(s.shape) == 2)
    return pl.pallas_call(
        kernel,
        out_shape=outs,
        in_specs=[ANY] * len(tables) + [VMEM] * len(inputs),
        out_specs=[VMEM] * len(outs),
        scratch_shapes=list(scratch),
        compiler_params=pltpu.CompilerParams(vmem_limit_bytes=used + (2 << 20)),
        name=name,
    )(*tables, *inputs)


def floats(rows):
    return pltpu.VMEM((rows, LANES), jnp.float32)


def shards(spectra, lead_delay, tail_delay, widths):
    channels, span = spectra.shape
    n_freq = lax.axis_size("freq")
    n_time = lax.axis_size("tm")
    freq = lax.axis_index("freq")
    sections = lead_delay.shape[0]
    local = channels.bit_length() - 1
    stages = (n_freq.bit_length() - 1) // 2
    main_segs = span // LANES
    full_time = sections - 2

    def segs_of(section):
        need = sum(2**s - 1 for s in range(section, full_time))
        return main_segs + -(-need // LANES)

    def smem_windows(count):
        return [pltpu.SMEM((count, sections, LANES), jnp.int32)] * 2

    tables = (lead_delay, tail_delay)
    pairs = channels // 2
    segs = segs_of(1)
    halo = segs - main_segs
    main, tip = call(
        functools.partial(pair_kernel, halo=halo),
        "pairs",
        [spectra],
        [(pairs * main_segs, LANES), (pairs * halo, LANES)],
        [floats(channels * main_segs)],
    )
    (current,) = call(
        functools.partial(join_kernel, segs=segs, main_segs=main_segs),
        "join",
        [main, shift_right(tip, "tm")],
        [(pairs * segs, LANES)],
    )
    for stage in range(stages - 1):
        section = local + 2 * stage
        others = [xor_permute(current, "freq", by << (2 * stage)) for by in (1, 2, 3)]
        windows = 1 if stage == 0 else 3
        rows = 4 * ROWS * (segs_of(1) if stage == 0 else segs_of(section))
        (current,) = call(
            functools.partial(
                quad_kernel,
                stage=stage,
                section=section,
                local=local if stage == 0 else 0,
                segs_of=segs_of,
            ),
            "quad",
            [current, *others],
            [(ROWS * segs_of(section + 2), LANES)],
            [floats(PAD + rows), floats(PAD + rows), *smem_windows(windows), pltpu.SemaphoreType.DMA((2 * windows,))],
            tables,
        )
    stage = stages - 1
    bands = [current] + [xor_permute(current, "freq", by << (2 * stage)) for by in (1, 2, 3)]
    stacked = jnp.concatenate(bands, axis=0)
    arrays = bands + [xor_permute(stacked, "tm", by) for by in range(1, n_time)]
    trials = 4 * ROWS // n_time
    total_segs = n_time * main_segs
    stride = PAD + total_segs
    peak_rows = channels * n_freq // LANES
    place_rows = -(-peak_rows // 8) * 8
    pieces = call(
        functools.partial(
            final_kernel,
            stage=stage,
            section=full_time,
            n_time=n_time,
            main_segs=main_segs,
            trials=trials,
            place_rows=place_rows,
        ),
        "final",
        arrays,
        [(main_segs + place_rows, LANES)] * n_time,
        [
            floats(4 * ROWS * stride),
            floats(2 * ROWS * stride),
            floats(trials * total_segs),
            floats(2 * LANES * main_segs),
            floats(8 * total_segs),
            floats(widths.shape[0] * 8),
            *[pltpu.SMEM((3, LANES), jnp.int32)] * 2,
            pltpu.SMEM(widths.shape, jnp.int32),
            pltpu.SemaphoreType.DMA((7,)),
        ],
        (*tables, widths),
    )
    merged = pieces[0]
    for by in range(1, n_time):
        merged = jnp.maximum(merged, xor_permute(pieces[by], "tm", by))
    for stage in range(stages - 1):
        received = [xor_permute(merged, "freq", by << (2 * stage)) for by in (1, 2, 3)]
        for value in received:
            merged = jnp.maximum(merged, value)
    best_snr = merged[:main_segs].reshape(span)
    peaks = merged[main_segs : main_segs + peak_rows].reshape(peak_rows * LANES)
    trial_peak = lax.dynamic_slice_in_dim(peaks, freq * channels, channels)
    return (best_snr, trial_peak)


def solution(mesh):
    placed = (P("freq", "tm"), P(), P(), P())
    return jax.shard_map(
        shards, mesh=mesh, in_specs=placed, out_specs=(P("tm"), P("freq")), check_vma=False
    )
```

time: 746 us -> 43.8 us (0.06)
  local copies, waits for them, and re-layouts: 559 us -> 2.09 us
  blocking collectives: 85.5 us -> 0 us
  loops' own time: 38.6 us -> 0 us
  other arithmetic: 11.4 us -> 0.04 us
  starting transfers between devices: 24.5 us -> 14.5 us
    gather x1040 -> x0, local copies, waits for them, and re-layouts: 544 us -> none
    pmax x2 -> x0, blocking collectives: 80.6 us -> none  [the longest x1 40.4 us: shards(): best_snr = lax.pmax(jnp.max(running, axis=0), 'freq')]
    another operation x9 -> x0, loops' own time: 38.6 us -> none  [the longest x1 32.4 us: box_best(): running = lax.fori_loop(0, widths.shape[0], advance, start_best)]
    dynamic_slice x33 -> x1, local copies, waits for them, and re-layouts: 11.6 us -> 0.58 us  [shards(): trial_peak = lax.dynamic_slice_in_dim(peaks, freq * channels, channels)]
    ppermute x13 -> x12, starting transfers between devices: 24.5 us -> 14.5 us  [the longest x11 12.1 us: xor_permute(): lax.ppermute(value, axis, [(i, i ^ by) for i in range(lax.axis_size(axis))])]
    ppermute x13 -> x12, waiting for transfers between devices: 20 us -> 20.2 us  [the longest x11 19.4 us: xor_permute(): lax.ppermute(value, axis, [(i, i ^ by) for i in range(lax.axis_size(axis))])]
  transfers between devices with their start and end apart: 13 -> 12, of which waited for: 11 -> 11; matrix products, arithmetic and copies ran while one was open for 1% -> 0% of each run, Pallas kernels for 0% -> 0%
where the time goes in v2:
time: 43.8 us; the launch traced here: 43.7 us
  waiting for transfers between devices  20.2 us (46%)
  starting transfers between devices  14.5 us (33%)
  Pallas kernels  6.19 us (14%)
  local copies, waits for them, and re-layouts  2.09 us (5%)
  between operations  0.7 us (2%)
    ppermute x11, waiting for transfers between devices, xor_permute(): lax.ppermute(value, axis, [(i, i ^ by) for i in range(lax.axis_size(axis))])  19.4 us
    ppermute x11, starting transfers between devices, xor_permute(): lax.ppermute(value, axis, [(i, i ^ by) for i in range(lax.axis_size(axis))])  12.1 us
    pallas_call x4, Pallas kernels, call(): pl.pallas_call(kernel, out_shape=outs, in_specs=[ANY] * len(tables) + [VM...  6.19 us
    ppermute x1, starting transfers between devices, shift_right(): return lax.ppermute(value, axis, [(i, i + 1) for i in range(count - 1)])  2.36 us
    unnamed x8, local copies, waits for them, and re-layouts  0.91 us
  transfers between devices with their start and end apart: 12, of which 11 were waited for; matrix products, arithmetic and copies ran while one was open for 0% of the time, Pallas kernels for 0%

profile of v2, /device:TPU:0, one launch (start us, length us, event | category | flops | bytes accessed | tf_op | source)
XLA Modules:
  0.0 43.7 jit_solution(4566545068209398173)
XLA Ops:
  0.6 0.0 copy-start
  0.6 0.9 %copy-done = f32[32,1024]{1,0:T(8,128)S(1)} copy-done((f32[32,1024]{1,0:T(8,128)S(1)}, f32[32,1024]{1,0:T(8,128)}, u32[]{:S(2)}) %copy-start) | copy-done | bytes 131096
  1.6 2.4 %collective-permute-start = (f32[16,128]{1,0:T(8,128)S(1)}, f32[16,128]{1,0:T(8,128)S(1)}, u32[]{:S(2)}, u32[]{:S(2)}) collective-permute-start(f32[16,128]{1,0:T(8,128)S(1)} %get-tuple-element.7), channel_id=1, source_target_pairs={{0,1},{2,3},{4,5},{6,7},{8,9},{10,11},{12,13},{14,15},{16,17},{18,... | collective-permute-start | bytes 24584 | tf_op jit(solution)/shard_map/ppermute | solution.py:25
  3.9 0.8 %collective-permute-done.tip = f32[16,128]{1,0:T(8,128)S(1)} collective-permute-done((f32[16,128]{1,0:T(8,128)S(1)}, f32[16,128]{1,0:T(8,128)S(1)}, u32[]{:S(2)}, u32[]{:S(2)}) %collective-permute-start) | collective-permute-done | bytes 8224 | tf_op jit(solution)/shard_map/ppermute | solution.py:25
  4.7 0.0 copy-start.1
  4.7 0.0 copy-start.2
  4.8 2.4 %collective-permute-start.1 = (f32[144,128]{1,0:T(8,128)S(1)}, f32[144,128]{1,0:T(8,128)S(1)}, u32[]{:S(2)}, u32[]{:S(2)}) collective-permute-start(f32[144,128]{1,0:T(8,128)S(1)} %join.1.refs_0_), channel_id=1, source_target_pairs={{0,2},{2,0},{4,6},{6,4},{8,10},{10,8},{12,14},{14,12},{16,18},{18,... | collective-permute-start | bytes 221192 | tf_op jit(solution)/shard_map/ppermute | solution.py:20
  7.1 1.5 %collective-permute-start.2 = (f32[144,128]{1,0:T(8,128)S(1)}, f32[144,128]{1,0:T(8,128)S(1)}, u32[]{:S(2)}, u32[]{:S(2)}) collective-permute-start(f32[144,128]{1,0:T(8,128)S(1)} %join.1.refs_0_), channel_id=1, source_target_pairs={{0,4},{2,6},{4,0},{6,2},{8,12},{10,14},{12,8},{14,10},{16,20},{18,... | collective-permute-start | bytes 221192 | tf_op jit(solution)/shard_map/ppermute | solution.py:20
  8.7 0.0 collective-permute-start.3
  8.7 1.2 %collective-permute-done.1.refs_1_ = f32[144,128]{1,0:T(8,128)S(1)} collective-permute-done((f32[144,128]{1,0:T(8,128)S(1)}, f32[144,128]{1,0:T(8,128)S(1)}, u32[]{:S(2)}, u32[]{:S(2)}) %collective-permute-start.1) | collective-permute-done | bytes 73760 | tf_op jit(solution)/shard_map/ppermute | solution.py:20
  9.9 1.6 %collective-permute-done.2.refs_2_ = f32[144,128]{1,0:T(8,128)S(1)} collective-permute-done((f32[144,128]{1,0:T(8,128)S(1)}, f32[144,128]{1,0:T(8,128)S(1)}, u32[]{:S(2)}, u32[]{:S(2)}) %collective-permute-start.2) | collective-permute-done | bytes 73760 | tf_op jit(solution)/shard_map/ppermute | solution.py:20
  11.5 2.4 %collective-permute-done.3.refs_3_ = f32[144,128]{1,0:T(8,128)S(1)} collective-permute-done((f32[144,128]{1,0:T(8,128)S(1)}, f32[144,128]{1,0:T(8,128)S(1)}, u32[]{:S(2)}, u32[]{:S(2)}) %collective-permute-start.3) | collective-permute-done | bytes 73760 | tf_op jit(solution)/shard_map/ppermute | solution.py:20
  13.9 0.0 copy-done.1
  13.9 0.0 copy-done.2
  13.9 2.7 %quad.1.refs_0_ = f32[256,128]{1,0:T(8,128)S(1)} custom-call(s32[9,512]{1,0:T(8,128)S(1)} %copy-done.1, s32[9,512]{1,0:T(8,128)S(1)} %copy-done.2, f32[144,128]{1,0:T(8,128)S(1)} %join.1.refs_0_, f32[144,128]{1,0:T(8,128)S(1)} %collective-permute-done.1.refs_1_, f32[144,128]{1,0:T(8,128)S(1)} %collective-permute-done.2.refs_2_, ...), custom_call_target="tpu_custom_call" | custom-call | tf_op jit(solution)/shard_map/quad/pallas_call | solution.py:322
  16.6 0.0 copy-start.3
  16.6 1.6 %collective-permute-start.4 = (f32[256,128]{1,0:T(8,128)S(1)}, f32[256,128]{1,0:T(8,128)S(1)}, u32[]{:S(2)}, u32[]{:S(2)}) collective-permute-start(f32[256,128]{1,0:T(8,128)S(1)} %quad.1.refs_0_), channel_id=1, source_target_pairs={{0,8},{2,10},{4,12},{6,14},{8,0},{10,2},{12,4},{14,6},{16,24},{18,... | collective-permute-start | bytes 393224 | tf_op jit(solution)/shard_map/ppermute | solution.py:20
  18.2 2.6 %collective-permute-start.5 = (f32[256,128]{1,0:T(8,128)S(1)}, f32[256,128]{1,0:T(8,128)S(1)}, u32[]{:S(2)}, u32[]{:S(2)}) collective-permute-start(f32[256,128]{1,0:T(8,128)S(1)} %quad.1.refs_0_), channel_id=1, source_target_pairs={{0,16},{2,18},{4,20},{6,22},{8,24},{10,26},{12,28},{14,30},{16,0},... | collective-permute-start | bytes 393224 | tf_op jit(solution)/shard_map/ppermute | solution.py:20
  20.8 0.2 collective-permute-start.6
  21.0 1.9 %collective-permute-done.4.refs_1_ = f32[256,128]{1,0:T(8,128)S(1)} collective-permute-done((f32[256,128]{1,0:T(8,128)S(1)}, f32[256,128]{1,0:T(8,128)S(1)}, u32[]{:S(2)}, u32[]{:S(2)}) %collective-permute-start.4) | collective-permute-done | bytes 131104 | tf_op jit(solution)/shard_map/ppermute | solution.py:20
  22.9 7.0 %collective-permute-done.5.refs_2_ = f32[256,128]{1,0:T(8,128)S(1)} collective-permute-done((f32[256,128]{1,0:T(8,128)S(1)}, f32[256,128]{1,0:T(8,128)S(1)}, u32[]{:S(2)}, u32[]{:S(2)}) %collective-permute-start.5) | collective-permute-done | bytes 131104 | tf_op jit(solution)/shard_map/ppermute | solution.py:20
  29.9 0.0 collective-permute-done.6.refs_3_
  30.0 0.1 collective-permute-start.7
  30.0 1.9 %collective-permute-done.7.refs_4_ = f32[1024,128]{1,0:T(8,128)S(1)} collective-permute-done((f32[1024,128]{1,0:T(8,128)S(1)}, f32[1024,128]{1,0:T(8,128)S(1)}, u32[]{:S(2)}, u32[]{:S(2)}) %collective-permute-start.7) | collective-permute-done | bytes 524320 | tf_op jit(solution)/shard_map/ppermute | solution.py:20
  31.9 0.0 copy-done.3
  31.9 3.5 %final.1 = (f32[16,128]{1,0:T(8,128)S(1)}, f32[16,128]{1,0:T(8,128)S(1)}) custom-call(s32[9,512]{1,0:T(8,128)S(1)} %copy-done.1, s32[9,512]{1,0:T(8,128)S(1)} %copy-done.2, s32[16]{0:T(128)S(1)} %copy-done.3, f32[256,128]{1,0:T(8,128)S(1)} %quad.1.refs_0_, f32[256,128]{1,0:T(8,128)S(1)} %collective-permute-done.4.refs_1_, ...), custom_call_target="tpu_custom_call" | custom-call | tf_op jit(solution)/shard_map/final/pallas_call | solution.py:322
  35.4 0.2 collective-permute-start.8
  35.6 1.0 %collective-permute-done.8 = f32[16,128]{1,0:T(8,128)S(1)} collective-permute-done((f32[16,128]{1,0:T(8,128)S(1)}, f32[16,128]{1,0:T(8,128)S(1)}, u32[]{:S(2)}, u32[]{:S(2)}) %collective-permute-start.8) | collective-permute-done | bytes 8224 | tf_op jit(solution)/shard_map/ppermute | solution.py:20
  36.7 0.6 %collective-permute-start.10 = (f32[16,128]{1,0:T(8,128)S(1)}, f32[16,128]{1,0:T(8,128)S(1)}, u32[]{:S(2)}, u32[]{:S(2)}) collective-permute-start(f32[16,128]{1,0:T(8,128)S(1)} %max.12), channel_id=1, source_target_pairs={{0,4},{2,6},{4,0},{6,2},{8,12},{10,14},{12,8},{14,10},{16,20},{18,... | collective-permute-start | bytes 24584 | tf_op jit(solution)/shard_map/ppermute | solution.py:20
  37.3 1.6 %collective-permute-start.11 = (f32[16,128]{1,0:T(8,128)S(1)}, f32[16,128]{1,0:T(8,128)S(1)}, u32[]{:S(2)}, u32[]{:S(2)}) collective-permute-start(f32[16,128]{1,0:T(8,128)S(1)} %max.12), channel_id=1, source_target_pairs={{0,6},{2,4},{4,2},{6,0},{8,14},{10,12},{12,10},{14,8},{16,22},{18,... | collective-permute-start | bytes 24584 | tf_op jit(solution)/shard_map/ppermute | solution.py:20
  38.9 1.3 %collective-permute-start.9 = (f32[16,128]{1,0:T(8,128)S(1)}, f32[16,128]{1,0:T(8,128)S(1)}, u32[]{:S(2)}, u32[]{:S(2)}) collective-permute-start(f32[16,128]{1,0:T(8,128)S(1)} %max.12), channel_id=1, source_target_pairs={{0,2},{2,0},{4,6},{6,4},{8,10},{10,8},{12,14},{14,12},{16,18},{18,... | collective-permute-start | bytes 24584 | tf_op jit(solution)/shard_map/ppermute | solution.py:20
  40.2 0.2 collective-permute-done.10
  40.3 1.5 %collective-permute-done.11 = f32[16,128]{1,0:T(8,128)S(1)} collective-permute-done((f32[16,128]{1,0:T(8,128)S(1)}, f32[16,128]{1,0:T(8,128)S(1)}, u32[]{:S(2)}, u32[]{:S(2)}) %collective-permute-start.11) | collective-permute-done | bytes 8224 | tf_op jit(solution)/shard_map/ppermute | solution.py:20
  41.9 0.7 %collective-permute-done.9 = f32[16,128]{1,0:T(8,128)S(1)} collective-permute-done((f32[16,128]{1,0:T(8,128)S(1)}, f32[16,128]{1,0:T(8,128)S(1)}, u32[]{:S(2)}, u32[]{:S(2)}) %collective-permute-start.9) | collective-permute-done | bytes 8224 | tf_op jit(solution)/shard_map/ppermute | solution.py:20
  42.5 0.6 %slice_bitcast_fusion = f32[1024]{0:T(1024)} fusion(f32[16,128]{1,0:T(8,128)S(1)} %maximum_maximum_fusion), kind=kLoop, calls=%fused_computation.2 | loop fusion | bytes 8192 | tf_op jit(solution)/shard_map/reshape | solution.py:433
  43.1 0.6 %dynamic_slice.3 = f32[32]{0:T(128)} dynamic-slice(f32[512]{0:T(512)S(1)} %slice_bitcast_fusion.1, s32[]{:T(128)S(6)} %select_n.3), dynamic_slice_sizes={32} | dynamic-slice | bytes 260 | tf_op jit(solution)/shard_map/dynamic_slice | solution.py:435
  (6 shorter events, 0.1 us)
Async XLA Ops:
  0.6 0.9 %copy-start = (f32[32,1024]{1,0:T(8,128)S(1)}, f32[32,1024]{1,0:T(8,128)}, u32[]{:S(2)}) copy-start(f32[32,1024]{1,0:T(8,128)} %x.1) | copy-start | bytes 393220
  1.6 3.2 %collective-permute-start = (f32[16,128]{1,0:T(8,128)S(1)}, f32[16,128]{1,0:T(8,128)S(1)}, u32[]{:S(2)}, u32[]{:S(2)}) collective-permute-start(f32[16,128]{1,0:T(8,128)S(1)} %get-tuple-element.7), channel_id=1, source_target_pairs={{0,1},{2,3},{4,5},{6,7},{8,9},{10,11},{12,13},{14,15},{16,17},{18,... | collective-permute-start | bytes 24584 | tf_op jit(solution)/shard_map/ppermute | solution.py:25
  4.7 9.2 %copy-start.1 = (s32[9,512]{1,0:T(8,128)S(1)}, s32[9,512]{1,0:T(8,128)}, u32[]{:S(2)}) copy-start(s32[9,512]{1,0:T(8,128)} %lead_all.3) | copy-start | bytes 55300
  4.7 9.2 %copy-start.2 = (s32[9,512]{1,0:T(8,128)S(1)}, s32[9,512]{1,0:T(8,128)}, u32[]{:S(2)}) copy-start(s32[9,512]{1,0:T(8,128)} %tail_all.3) | copy-start | bytes 55300
  4.8 5.2 %collective-permute-start.1 = (f32[144,128]{1,0:T(8,128)S(1)}, f32[144,128]{1,0:T(8,128)S(1)}, u32[]{:S(2)}, u32[]{:S(2)}) collective-permute-start(f32[144,128]{1,0:T(8,128)S(1)} %join.1.refs_0_), channel_id=1, source_target_pairs={{0,2},{2,0},{4,6},{6,4},{8,10},{10,8},{12,14},{14,12},{16,18},{18,... | collective-permute-start | bytes 221192 | tf_op jit(solution)/shard_map/ppermute | solution.py:20
  7.1 4.4 %collective-permute-start.2 = (f32[144,128]{1,0:T(8,128)S(1)}, f32[144,128]{1,0:T(8,128)S(1)}, u32[]{:S(2)}, u32[]{:S(2)}) collective-permute-start(f32[144,128]{1,0:T(8,128)S(1)} %join.1.refs_0_), channel_id=1, source_target_pairs={{0,4},{2,6},{4,0},{6,2},{8,12},{10,14},{12,8},{14,10},{16,20},{18,... | collective-permute-start | bytes 221192 | tf_op jit(solution)/shard_map/ppermute | solution.py:20
  8.7 5.3 %collective-permute-start.3 = (f32[144,128]{1,0:T(8,128)S(1)}, f32[144,128]{1,0:T(8,128)S(1)}, u32[]{:S(2)}, u32[]{:S(2)}) collective-permute-start(f32[144,128]{1,0:T(8,128)S(1)} %join.1.refs_0_), channel_id=1, source_target_pairs={{0,6},{2,4},{4,2},{6,0},{8,14},{10,12},{12,10},{14,8},{16,22},{18,... | collective-permute-start | bytes 221192 | tf_op jit(solution)/shard_map/ppermute | solution.py:20
  16.6 15.4 %copy-start.3 = (s32[16]{0:T(128)S(1)}, s32[16]{0:T(128)}, u32[]{:S(2)}) copy-start(s32[16]{0:T(128)} %widths_all.1) | copy-start | bytes 196
  16.6 6.3 %collective-permute-start.4 = (f32[256,128]{1,0:T(8,128)S(1)}, f32[256,128]{1,0:T(8,128)S(1)}, u32[]{:S(2)}, u32[]{:S(2)}) collective-permute-start(f32[256,128]{1,0:T(8,128)S(1)} %quad.1.refs_0_), channel_id=1, source_target_pairs={{0,8},{2,10},{4,12},{6,14},{8,0},{10,2},{12,4},{14,6},{16,24},{18,... | collective-permute-start | bytes 393224 | tf_op jit(solution)/shard_map/ppermute | solution.py:20
  18.2 11.7 %collective-permute-start.5 = (f32[256,128]{1,0:T(8,128)S(1)}, f32[256,128]{1,0:T(8,128)S(1)}, u32[]{:S(2)}, u32[]{:S(2)}) collective-permute-start(f32[256,128]{1,0:T(8,128)S(1)} %quad.1.refs_0_), channel_id=1, source_target_pairs={{0,16},{2,18},{4,20},{6,22},{8,24},{10,26},{12,28},{14,30},{16,0},... | collective-permute-start | bytes 393224 | tf_op jit(solution)/shard_map/ppermute | solution.py:20
  20.8 9.1 %collective-permute-start.6 = (f32[256,128]{1,0:T(8,128)S(1)}, f32[256,128]{1,0:T(8,128)S(1)}, u32[]{:S(2)}, u32[]{:S(2)}) collective-permute-start(f32[256,128]{1,0:T(8,128)S(1)} %quad.1.refs_0_), channel_id=1, source_target_pairs={{0,24},{2,26},{4,28},{6,30},{8,16},{10,18},{12,20},{14,22},{16,8},... | collective-permute-start | bytes 393224 | tf_op jit(solution)/shard_map/ppermute | solution.py:20
  30.0 2.0 %collective-permute-start.7 = (f32[1024,128]{1,0:T(8,128)S(1)}, f32[1024,128]{1,0:T(8,128)S(1)}, u32[]{:S(2)}, u32[]{:S(2)}) collective-permute-start(f32[1024,128]{1,0:T(8,128)S(1)} %pad_maximum_fusion), channel_id=1, source_target_pairs={{0,1},{1,0},{2,3},{3,2},{4,5},{5,4},{6,7},{7,6},{8,9},{9,8},{10,11... | collective-permute-start | bytes 1572872 | tf_op jit(solution)/shard_map/ppermute | solution.py:20
  35.4 1.2 %collective-permute-start.8 = (f32[16,128]{1,0:T(8,128)S(1)}, f32[16,128]{1,0:T(8,128)S(1)}, u32[]{:S(2)}, u32[]{:S(2)}) collective-permute-start(f32[16,128]{1,0:T(8,128)S(1)} %get-tuple-element.9), channel_id=1, source_target_pairs={{0,1},{1,0},{2,3},{3,2},{4,5},{5,4},{6,7},{7,6},{8,9},{9,8},{10,11... | collective-permute-start | bytes 24584 | tf_op jit(solution)/shard_map/ppermute | solution.py:20
  36.7 3.7 %collective-permute-start.10 = (f32[16,128]{1,0:T(8,128)S(1)}, f32[16,128]{1,0:T(8,128)S(1)}, u32[]{:S(2)}, u32[]{:S(2)}) collective-permute-start(f32[16,128]{1,0:T(8,128)S(1)} %max.12), channel_id=1, source_target_pairs={{0,4},{2,6},{4,0},{6,2},{8,12},{10,14},{12,8},{14,10},{16,20},{18,... | collective-permute-start | bytes 24584 | tf_op jit(solution)/shard_map/ppermute | solution.py:20
  37.3 4.5 %collective-permute-start.11 = (f32[16,128]{1,0:T(8,128)S(1)}, f32[16,128]{1,0:T(8,128)S(1)}, u32[]{:S(2)}, u32[]{:S(2)}) collective-permute-start(f32[16,128]{1,0:T(8,128)S(1)} %max.12), channel_id=1, source_target_pairs={{0,6},{2,4},{4,2},{6,0},{8,14},{10,12},{12,10},{14,8},{16,22},{18,... | collective-permute-start | bytes 24584 | tf_op jit(solution)/shard_map/ppermute | solution.py:20
  38.9 3.7 %collective-permute-start.9 = (f32[16,128]{1,0:T(8,128)S(1)}, f32[16,128]{1,0:T(8,128)S(1)}, u32[]{:S(2)}, u32[]{:S(2)}) collective-permute-start(f32[16,128]{1,0:T(8,128)S(1)} %max.12), channel_id=1, source_target_pairs={{0,2},{2,0},{4,6},{6,4},{8,10},{10,8},{12,14},{14,12},{16,18},{18,... | collective-permute-start | bytes 24584 | tf_op jit(solution)/shard_map/ppermute | solution.py:20

commit v3 on v2

v3 whole, which is shorter than its diff:
```python
import functools

import jax
import jax.numpy as jnp
from jax import lax
from jax.experimental import pallas as pl
from jax.experimental.pallas import tpu as pltpu
from jax.sharding import PartitionSpec as P

LANES = 128
ROWS = 32
PAD = 8

eps_var = 1e-06
VMEM = pl.BlockSpec(memory_space=pltpu.VMEM)
ANY = pl.BlockSpec(memory_space=pl.ANY)


def xor_permute(value, axis, by):
    return lax.ppermute(value, axis, [(i, i ^ by) for i in range(lax.axis_size(axis))])


def rotate_right(value, axis):
    count = lax.axis_size(axis)
    return lax.ppermute(value, axis, [(i, (i + 1) % count) for i in range(count)])


def section_rows(src, dst, dst_row, segs, rows, table, entry, group=16):
    lane = lax.broadcasted_iota(jnp.int32, (segs, LANES), 1)
    for first in range(0, rows, group):
        picked = []
        for k in range(first, min(first + group, rows)):
            at, column = entry(k)
            start, delay = table[at + 1, column], table[at + 2, column]
            lower = src[pl.ds(table[at, column], segs), :]
            picked.append((k, delay, lower, src[pl.ds(start, segs), :], src[pl.ds(start - 1, segs), :]))
        for k, delay, lower, here, before in picked:
            mixed = jnp.where(lane < LANES - delay, here, before)
            dst[pl.ds(dst_row(k), segs), :] = lower + pltpu.roll(mixed, delay, axis=1)


def window(start):
    return pl.multiple_of((start // LANES) * LANES, LANES)


def order_of(freq, stage):
    order = 0
    for n in range(stage):
        order = 4 * order + ((freq >> (2 * n)) & 3)
    return order


def pair_kernel(x, out, stage):
    channels, span = x.shape
    segs = span // LANES
    half = channels // 2
    for seg in range(segs):
        stage[pl.ds(seg * channels, channels), :] = x[:, pl.ds(seg * LANES, LANES)]
    for seg in range(segs):
        first = seg * channels
        summed = stage[pl.ds(first, half, stride=2), :] + stage[pl.ds(first + 1, half, stride=2), :]
        out[pl.ds(seg, half, stride=segs), :] = summed


def tips_kernel(*refs, main_segs, halo):
    *inputs, out = refs
    rows = inputs[0].shape[0] // main_segs
    for n, ref in enumerate(inputs):
        for seg in range(halo):
            to = (n * halo + seg) * rows
            out[pl.ds(to, rows), :] = ref[pl.ds(main_segs - halo + seg, rows, stride=main_segs), :]


def stage_places(stage, section, freq, trials_first=None):
    order = order_of(freq, stage)
    place = (freq >> (2 * stage)) & 3
    rows_in = 2**section
    base = (freq >> (2 * stage + 2)) * (4 * rows_in)
    last = base + ROWS * (4 * order + place) if trials_first is None else trials_first
    half_order = (last - base) // (2 * ROWS)
    starts = [base + ROWS * half_order, base + 2 * rows_in + ROWS * half_order, last]
    return base, order, half_order, starts


def tables_kernel(lead_all, tail_all, order_after, *refs, stages, sections, local, strides, trials):
    del order_after
    outs, (lead, tail, sems) = refs[:stages], refs[stages:]
    freq = lax.axis_index("freq")
    plans = []
    for stage in range(stages):
        section = local + 2 * stage
        first_trial = None
        if stage == stages - 1:
            first_trial = 4 * ROWS * order_of(freq, stage) + trials * lax.axis_index("tm")
        base, order, half_order, starts = stage_places(stage, section, freq, first_trial)
        plans.append((section, order, half_order, [base] if stage == 0 else starts))
    copies = []
    slot = 0
    for *_, wheres in plans:
        for where in wheres:
            for table, to in ((lead_all, lead), (tail_all, tail)):
                part = table.at[:, pl.ds(window(where), LANES)]
                copies.append(pltpu.make_async_copy(part, to.at[slot], sems.at[len(copies)]))
            slot += 1
    for copy in copies:
        copy.start()
    for copy in copies:
        copy.wait()
    lane = lax.broadcasted_iota(jnp.int32, (1, LANES), 1)
    slot = 0
    for stage, (section, order, half_order, wheres) in enumerate(plans):
        out, at = outs[stage], 0
        jobs = []
        if stage == 0:
            for now in range(1, local):
                band = lane // (2 * 2**now)
                rows = (2 * band, 2 * band + 1) if now == 1 else (2 * band * 2**now, (2 * band + 1) * 2**now)
                jobs.append((slot, now, *rows, now > 1, strides[now]))
            band = lane // (2 * ROWS)
            jobs.append((slot, section, 2 * band * ROWS, (2 * band + 1) * ROWS, True, strides[section]))
            jobs.append((slot, section + 1, -ROWS * half_order, ROWS - ROWS * half_order, True, strides[section + 1]))
        else:
            for band in range(2):
                low = 2 * band * ROWS - ROWS * order
                jobs.append((slot + band, section, low, low + ROWS, True, strides[section]))
            low = -ROWS * half_order
            jobs.append((slot + 2, section + 1, low, low + ROWS, True, strides[section + 1]))
        for where, row, low, up, picks, (stride, ahead) in jobs:
            e, h = lead[where, pl.ds(row, 1), :], tail[where, pl.ds(row, 1), :]
            out[pl.ds(at, 1), :] = (low + e if picks else low) * stride + ahead
            out[pl.ds(at + 1, 1), :] = (up + h if picks else up) * stride + ahead - (e >> 7)
            out[pl.ds(at + 2, 1), :] = e & (LANES - 1)
            at += 3
        slot += len(wheres)


def quad_kernel(packed, *refs, stage, section, local, segs_of):
    inputs, tips, out = refs[:4], refs[4:-5], refs[-5]
    buf_a, buf_b, table, sem = refs[-4:]
    copy = pltpu.make_async_copy(packed, table, sem)
    copy.start()
    freq = lax.axis_index("freq")
    place = (freq >> (2 * stage)) & 3
    _, _, half_order, starts = stage_places(stage, section, freq)
    segs = segs_of(1) if local else segs_of(section)
    size = inputs[0].shape[0]
    buf_a[pl.ds(0, PAD), :] = jnp.zeros((PAD, LANES), jnp.float32)
    buf_b[pl.ds(0, PAD), :] = jnp.zeros((PAD, LANES), jnp.float32)
    for by, ref in enumerate(inputs):
        if not local:
            to = pl.multiple_of(PAD + (place ^ by) * size, 8)
            buf_a[pl.ds(to, size), :] = ref[...]
            continue
        rows = ROWS // 2
        main_segs = size // rows
        halo = segs - main_segs
        to = PAD + (place ^ by) * (rows * segs)
        for seg in range(halo):
            tip = tips[0][pl.ds((by * halo + seg) * rows, rows), :]
            tip = jnp.where(lax.axis_index("tm") > 0, tip, 0.0)
            buf_a[pl.ds(to + seg, rows, stride=segs), :] = tip
        for row in range(rows):
            buf_a[pl.ds(to + row * segs + halo, main_segs), :] = ref[pl.ds(row * main_segs, main_segs), :]
    copy.wait()
    src, dst = buf_a, buf_b
    for now in range(1, local):
        section_rows(
            src,
            dst,
            lambda k: PAD + k * segs,
            segs,
            4 * ROWS,
            table,
            lambda k, now=now: (3 * (now - 1), k),
        )
        src, dst = dst, src
    mid_segs, out_segs = segs_of(section + 1), segs_of(section + 2)

    def mid_entry(k):
        band = k // ROWS
        if local:
            return 3 * (local - 1), 2 * ROWS * band + ROWS * half_order + k % ROWS
        return 3 * band, starts[band] % LANES + k % ROWS

    section_rows(src, dst, lambda k: PAD + k * mid_segs, mid_segs, 2 * ROWS, table, mid_entry)
    at = 3 * local if local else 6
    column = starts[2] % LANES
    section_rows(dst, out, lambda k: k * out_segs, out_segs, ROWS, table, lambda k: (at, column + k))


def final_kernel(packed, widths_all, *refs, stage, section, n_time, main_segs, trials, place_rows):
    own, moved = refs[:4], refs[4 : 3 + n_time]
    outs = refs[3 + n_time : 3 + 2 * n_time]
    buf, mid, data, edges, over, scale, table, widths, sems = refs[3 + 2 * n_time :]
    copies = [
        pltpu.make_async_copy(packed, table, sems.at[0]),
        pltpu.make_async_copy(widths_all, widths, sems.at[1]),
    ]
    for copy in copies:
        copy.start()
    freq = lax.axis_index("freq")
    tm = lax.axis_index("tm")
    place = (freq >> (2 * stage)) & 3
    first_trial = 4 * ROWS * order_of(freq, stage) + trials * tm
    _, _, _, starts = stage_places(stage, section, freq, first_trial)
    total_segs = n_time * main_segs
    total_time = total_segs * LANES
    stride = PAD + total_segs
    zeros = jnp.zeros((PAD, LANES), jnp.float32)
    for row in range(4 * ROWS):
        buf[pl.ds(row * stride, PAD), :] = zeros
    for row in range(2 * ROWS):
        mid[pl.ds(row * stride, PAD), :] = zeros
    size = ROWS * main_segs
    for by_band in range(4):
        for by_time in range(n_time):
            start = (place ^ by_band) * (ROWS * stride) + PAD + (tm ^ by_time) * main_segs
            ref, at = (own[by_band], 0) if by_time == 0 else (moved[by_time - 1], by_band * size)
            for row in range(ROWS):
                to = pl.multiple_of(start + row * stride, 8)
                buf[pl.ds(to, main_segs), :] = ref[pl.ds(at + row * main_segs, main_segs), :]
    for copy in copies:
        copy.wait()

    section_rows(
        buf,
        mid,
        lambda k: PAD + k * stride,
        total_segs,
        2 * ROWS,
        table,
        lambda k: (3 * (k // ROWS), starts[k // ROWS] % LANES + k % ROWS),
    )
    column = first_trial % LANES
    section_rows(mid, data, lambda k: k * total_segs, total_segs, trials, table, lambda k: (6, column + k))

    def samples(seg):
        return data[pl.ds(seg, trials, stride=total_segs), :]

    total = samples(0)
    for seg in range(1, total_segs):
        total = total + samples(seg)
    mean = jnp.sum(total, axis=1, keepdims=True) / total_time

    row_at = lax.broadcasted_iota(jnp.int32, (2 * LANES, LANES), 0)
    column_at = lax.broadcasted_iota(jnp.int32, (2 * LANES, LANES), 1)
    after = jnp.where(column_at > row_at, -1.0, 0.0)
    upto = jnp.where(column_at <= row_at - LANES, 1.0, 0.0)
    ones = jnp.where(row_at < LANES, after, upto).astype(jnp.bfloat16)
    ones = jnp.concatenate([ones] * 3, axis=1)
    squares = jnp.zeros((trials, LANES), jnp.float32)
    for seg in range(-1, main_segs):
        parts = []
        for part in range(n_time):
            at = part * main_segs + seg
            centred = samples(at) - mean if at >= 0 else jnp.zeros((trials, LANES), jnp.float32)
            if seg >= 0:
                squares = squares + centred * centred
            parts.append(centred)
        values = jnp.concatenate(parts, axis=0)
        terms = []
        for _ in range(3):
            term = values.astype(jnp.bfloat16)
            terms.append(term)
            values = values - term.astype(jnp.float32)
        both = lax.dot_general(
            ones,
            jnp.concatenate(terms, axis=1),
            (((1,), (1,)), ((), ())),
            preferred_element_type=jnp.float32,
        )
        if seg + 1 < main_segs:
            edges[pl.ds((seg + 1) * 2 * LANES, LANES), :] = both[:LANES]
        if seg >= 0:
            edges[pl.ds(seg * 2 * LANES + LANES, LANES), :] = both[LANES:]
    squares = jnp.sum(squares, axis=1, keepdims=True)
    inverse = 1.0 / jnp.sqrt(squares / total_time + eps_var)
    inverse = jnp.concatenate([jnp.broadcast_to(inverse, (trials, LANES))] * n_time, axis=0).T[:8]

    count = widths.shape[0]
    for j in range(count):
        scale[pl.ds(j * 8, 8), :] = jnp.full((8, LANES), widths[j], jnp.int32).astype(jnp.float32)
    scale[...] = 1.0 / jnp.sqrt(scale[...])
    tall = 64

    def spread_rows(value):
        return jnp.concatenate([value] * (tall // 8), axis=0)

    def fold(value):
        out = value[:8]
        for n in range(8, value.shape[0], 8):
            out = jnp.maximum(out, value[n : n + 8])
        return out

    peaks = jnp.full((8, LANES), -jnp.inf, jnp.float32)
    for seg in range(main_segs):
        blocks = []
        for first in range(0, LANES, tall):
            at = seg * 2 * LANES + LANES + first
            ends = edges[pl.ds(at, tall), :]
            best = None
            for j in range(count):
                score = (ends - edges[pl.ds(at - widths[j], tall), :]) * spread_rows(scale[pl.ds(j * 8, 8), :])
                best = score if j == 0 else jnp.maximum(best, score)
            best = best * spread_rows(inverse)
            peaks = jnp.maximum(peaks, fold(best))
            blocks.append(best)
        turned = jnp.concatenate(blocks, axis=0).T
        for part in range(n_time):
            over[pl.ds((part * main_segs + seg) * 8, 8), :] = fold(turned[part * trials : (part + 1) * trials])
    best_all = over[pl.ds(0, total_segs, stride=8), :]
    for n in range(1, 8):
        best_all = jnp.maximum(best_all, over[pl.ds(n, total_segs, stride=8), :])
    buf[pl.ds(0, total_segs), :] = best_all
    peak_row = jnp.max(peaks, axis=0, keepdims=True)
    step = trials
    while step < LANES:
        peak_row = jnp.maximum(peak_row, pltpu.roll(peak_row, step, axis=1))
        step *= 2
    offset = first_trial % LANES
    lane = lax.broadcasted_iota(jnp.int32, (1, LANES), 1)
    peak_row = jnp.where((lane >= offset) & (lane < offset + trials), peak_row, -jnp.inf)
    for by in range(n_time):
        at = pl.multiple_of((tm ^ by) * main_segs, 8)
        outs[by][pl.ds(0, main_segs), :] = buf[pl.ds(at, main_segs), :]
        outs[by][pl.ds(main_segs, place_rows), :] = jnp.full((place_rows, LANES), -jnp.inf, jnp.float32)
        outs[by][pl.ds(main_segs + first_trial // LANES, 1), :] = peak_row


def finish_kernel(*refs, main_segs, channels):
    inputs, (best_out, peaks_out), (best, row, peaks, sems) = refs[:-6], refs[-6:-4], refs[-4:]
    merged = inputs[0][...]
    for ref in inputs[1:]:
        merged = jnp.maximum(merged, ref[...])
    best[...] = merged[:main_segs]
    row[...] = merged[main_segs:]
    first = pltpu.make_async_copy(best, best_out, sems.at[0])
    first.start()
    start = lax.axis_index("freq") * channels
    mine = pltpu.roll(row[pl.ds(start // LANES, 1), :], (LANES - start % LANES) % LANES, axis=1)
    peaks[...] = mine[:, :channels]
    second = pltpu.make_async_copy(peaks, peaks_out, sems.at[1])
    second.start()
    first.wait()
    second.wait()


def call(kernel, name, inputs, out_shapes, scratch=(), tables=(), out_specs=VMEM, dtype=jnp.float32):
    outs = [jax.ShapeDtypeStruct(shape, dtype) for shape in out_shapes]
    used = sum(4 * v.size for v in inputs) + sum(4 * o.size for o in outs)
    used += sum(4 * s.shape[0] * s.shape[1] for s in scratch if len(s.shape) == 2)
    return pl.pallas_call(
        kernel,
        out_shape=outs,
        in_specs=[ANY] * len(tables) + [VMEM] * len(inputs),
        out_specs=[out_specs] * len(outs),
        scratch_shapes=list(scratch),
        compiler_params=pltpu.CompilerParams(vmem_limit_bytes=used + (2 << 20)),
        name=name,
    )(*tables, *inputs)


def floats(rows):
    return pltpu.VMEM((rows, LANES), jnp.float32)


def shards(spectra, lead_delay, tail_delay, widths):
    channels, span = spectra.shape
    n_freq = lax.axis_size("freq")
    n_time = lax.axis_size("tm")
    freq = lax.axis_index("freq")
    sections = lead_delay.shape[0]
    local = channels.bit_length() - 1
    stages = (n_freq.bit_length() - 1) // 2
    main_segs = span // LANES
    full_time = sections - 2

    def segs_of(section):
        need = sum(2**s - 1 for s in range(section, full_time))
        return main_segs + -(-need // LANES)

    pairs = channels // 2
    segs = segs_of(1)
    halo = segs - main_segs
    (current,) = call(
        pair_kernel,
        "pairs",
        [spectra],
        [(pairs * main_segs, LANES)],
        [floats(channels * main_segs)],
    )
    trials = 4 * ROWS // n_time
    total_segs = n_time * main_segs
    stride = PAD + total_segs
    strides = {}
    for section in range(1, sections):
        if section >= full_time:
            strides[section] = (stride, PAD)
        elif section < local:
            strides[section] = (segs, PAD)
        else:
            strides[section] = (segs_of(section), PAD + segs_of(section) - segs_of(section + 1))
    strides[local] = (segs, PAD + segs - segs_of(local + 1))
    windows = 1 + 3 * (stages - 1)
    tables = call(
        functools.partial(
            tables_kernel, stages=stages, sections=sections, local=local, strides=strides, trials=trials
        ),
        "tables",
        [current],
        [(3 * (local + 1), LANES)] + [(9, LANES)] * (stages - 1),
        [pltpu.VMEM((windows, sections, LANES), jnp.int32)] * 2 + [pltpu.SemaphoreType.DMA((2 * windows,))],
        (lead_delay, tail_delay),
        dtype=jnp.int32,
    )
    for stage in range(stages - 1):
        section = local + 2 * stage
        others = [xor_permute(current, "freq", by << (2 * stage)) for by in (1, 2, 3)]
        inputs = [current, *others]
        if stage == 0:
            (tips,) = call(
                functools.partial(tips_kernel, main_segs=main_segs, halo=halo),
                "tips",
                inputs,
                [(4 * pairs * halo, LANES)],
            )
            inputs.append(rotate_right(tips, "tm"))
        rows = 4 * ROWS * (segs_of(1) if stage == 0 else segs_of(section))
        (current,) = call(
            functools.partial(
                quad_kernel,
                stage=stage,
                section=section,
                local=local if stage == 0 else 0,
                segs_of=segs_of,
            ),
            "quad",
            inputs,
            [(ROWS * segs_of(section + 2), LANES)],
            [
                floats(PAD + rows),
                floats(PAD + rows),
                pltpu.SMEM(tables[stage].shape, jnp.int32),
                pltpu.SemaphoreType.DMA(()),
            ],
            [tables[stage]],
        )
    stage = stages - 1
    two = xor_permute(current, "freq", 2 << (2 * stage))
    one = xor_permute(current, "freq", 1 << (2 * stage))
    three = xor_permute(two, "freq", 1 << (2 * stage))
    bands = [current, one, two, three]
    stacked = jnp.concatenate(bands, axis=0)
    arrays = bands + [xor_permute(stacked, "tm", by) for by in range(1, n_time)]
    peak_rows = channels * n_freq // LANES
    place_rows = -(-peak_rows // 8) * 8
    pieces = call(
        functools.partial(
            final_kernel,
            stage=stage,
            section=full_time,
            n_time=n_time,
            main_segs=main_segs,
            trials=trials,
            place_rows=place_rows,
        ),
        "final",
        arrays,
        [(main_segs + place_rows, LANES)] * n_time,
        [
            floats(4 * ROWS * stride),
            floats(2 * ROWS * stride),
            floats(trials * total_segs),
            floats(2 * LANES * main_segs),
            floats(8 * total_segs),
            floats(widths.shape[0] * 8),
            pltpu.SMEM(tables[stage].shape, jnp.int32),
            pltpu.SMEM(widths.shape, jnp.int32),
            pltpu.SemaphoreType.DMA((2,)),
        ],
        [tables[stage], widths],
    )
    merged = pieces[0]
    for by in range(1, n_time):
        merged = jnp.maximum(merged, xor_permute(pieces[by], "tm", by))
    for stage in range(stages - 1):
        received = [merged] + [xor_permute(merged, "freq", by << (2 * stage)) for by in (1, 2, 3)]
        if stage < stages - 2:
            merged = functools.reduce(jnp.maximum, received)
    best_snr, trial_peak = call(
        functools.partial(finish_kernel, main_segs=main_segs, channels=channels),
        "finish",
        received,
        [(main_segs, LANES), (1, channels)],
        [
            floats(main_segs),
            floats(place_rows),
            pltpu.VMEM((1, channels), jnp.float32),
            pltpu.SemaphoreType.DMA((2,)),
        ],
        out_specs=ANY,
    )
    return (best_snr.reshape(span), trial_peak.reshape(channels))


def solution(mesh):
    placed = (P("freq", "tm"), P(), P(), P())
    return jax.shard_map(
        shards, mesh=mesh, in_specs=placed, out_specs=(P("tm"), P("freq")), check_vma=False
    )
```

time: 43.8 us -> 41.6 us (0.950)
  starting transfers between devices: 14.5 us -> 13.2 us
  local copies, waits for them, and re-layouts: 2.09 us -> 0.92 us
  Pallas kernels: 6.19 us -> 6.81 us
  waiting for transfers between devices: 20.2 us -> 19.7 us
    ppermute x1, starting transfers between devices: 2.36 us -> 0.07 us  [rotate_right(): lax.ppermute(value, axis, [(i, (i + 1) % count) for i in range(count)])]
    ppermute x11, starting transfers between devices: 12.1 us -> 13.2 us  [xor_permute(): lax.ppermute(value, axis, [(i, i ^ by) for i in range(lax.axis_size(axis))])]
    ppermute x11, waiting for transfers between devices: 19.4 us -> 18.8 us  [xor_permute(): lax.ppermute(value, axis, [(i, i ^ by) for i in range(lax.axis_size(axis))])]
    pallas_call x4 -> x6, Pallas kernels: 6.19 us -> 6.81 us  [call(): pl.pallas_call(kernel, out_shape=outs, in_specs=[ANY] * len(tables) + [VM...]
    reshape x2 -> x0, local copies, waits for them, and re-layouts: 0.6 us -> none  [the longest x1 0.59 us: shards(): best_snr = merged[:main_segs].reshape(span)]
    dynamic_slice x1 -> x0, local copies, waits for them, and re-layouts: 0.58 us -> none  [shards(): trial_peak = lax.dynamic_slice_in_dim(peaks, freq * channels, channels)]
where the time goes in v3:
time: 41.6 us; the launch traced here: 41.5 us
  waiting for transfers between devices  19.7 us (47%)
  starting transfers between devices  13.2 us (32%)
  Pallas kernels  6.81 us (16%)
  local copies, waits for them, and re-layouts  0.92 us (2%)
  between operations  0.74 us (2%)
    ppermute x11, waiting for transfers between devices, xor_permute(): lax.ppermute(value, axis, [(i, i ^ by) for i in range(lax.axis_size(axis))])  18.8 us
    ppermute x11, starting transfers between devices, xor_permute(): lax.ppermute(value, axis, [(i, i ^ by) for i in range(lax.axis_size(axis))])  13.2 us
    pallas_call x6, Pallas kernels, call(): pl.pallas_call(kernel, out_shape=outs, in_specs=[ANY] * len(tables) + [VM...  6.81 us
    ppermute x1, waiting for transfers between devices, rotate_right(): lax.ppermute(value, axis, [(i, (i + 1) % count) for i in range(count)])  0.97 us
    unnamed x8, local copies, waits for them, and re-layouts  0.92 us
  transfers between devices with their start and end apart: 12, of which 11 were waited for; matrix products, arithmetic and copies ran while one was open for 0% of the time, Pallas kernels for 0%

profile of v3, /device:TPU:0, one launch (start us, length us, event | category | flops | bytes accessed | tf_op | source)
XLA Modules:
  0.0 41.5 jit_solution(6718519737271583476)
XLA Ops:
  0.6 0.0 copy-start
  0.6 0.9 %copy-done = f32[32,1024]{1,0:T(8,128)S(1)} copy-done((f32[32,1024]{1,0:T(8,128)S(1)}, f32[32,1024]{1,0:T(8,128)}, u32[]{:S(2)}) %copy-start) | copy-done | bytes 131096
  1.6 0.0 copy-start.1
  1.6 0.0 copy-start.2
  1.6 4.0 %collective-permute-start.2 = (f32[128,128]{1,0:T(8,128)S(1)}, f32[128,128]{1,0:T(8,128)S(1)}, u32[]{:S(2)}, u32[]{:S(2)}) collective-permute-start(f32[128,128]{1,0:T(8,128)S(1)} %pairs.1.order_after.refs_0_), channel_id=1, source_target_pairs={{0,6},{2,4},{4,2},{6,0},{8,14},{10,12},{12,10},{14,8},{16,22},{18,... | collective-permute-start | bytes 196616 | tf_op jit(solution)/shard_map/ppermute | solution.py:20
  5.5 0.5 %collective-permute-start.1 = (f32[128,128]{1,0:T(8,128)S(1)}, f32[128,128]{1,0:T(8,128)S(1)}, u32[]{:S(2)}, u32[]{:S(2)}) collective-permute-start(f32[128,128]{1,0:T(8,128)S(1)} %pairs.1.order_after.refs_0_), channel_id=1, source_target_pairs={{0,4},{2,6},{4,0},{6,2},{8,12},{10,14},{12,8},{14,10},{16,20},{18,... | collective-permute-start | bytes 196616 | tf_op jit(solution)/shard_map/ppermute | solution.py:20
  6.1 0.1 collective-permute-start
  6.2 1.6 %collective-permute-done.2.refs_3_ = f32[128,128]{1,0:T(8,128)S(1)} collective-permute-done((f32[128,128]{1,0:T(8,128)S(1)}, f32[128,128]{1,0:T(8,128)S(1)}, u32[]{:S(2)}, u32[]{:S(2)}) %collective-permute-start.2) | collective-permute-done | bytes 65568 | tf_op jit(solution)/shard_map/ppermute | solution.py:20
  7.8 2.0 %collective-permute-done.1.refs_2_ = f32[128,128]{1,0:T(8,128)S(1)} collective-permute-done((f32[128,128]{1,0:T(8,128)S(1)}, f32[128,128]{1,0:T(8,128)S(1)}, u32[]{:S(2)}, u32[]{:S(2)}) %collective-permute-start.1) | collective-permute-done | bytes 65568 | tf_op jit(solution)/shard_map/ppermute | solution.py:20
  9.8 0.5 %collective-permute-done.refs_1_ = f32[128,128]{1,0:T(8,128)S(1)} collective-permute-done((f32[128,128]{1,0:T(8,128)S(1)}, f32[128,128]{1,0:T(8,128)S(1)}, u32[]{:S(2)}, u32[]{:S(2)}) %collective-permute-start) | collective-permute-done | bytes 65568 | tf_op jit(solution)/shard_map/ppermute | solution.py:20
  10.3 0.1 collective-permute-start.3
  10.4 0.0 copy-done.1
  10.4 0.0 copy-done.2
  10.4 0.2 tables.1
  10.6 1.0 %collective-permute-done.3.refs_4_ = f32[64,128]{1,0:T(8,128)S(1)} collective-permute-done((f32[64,128]{1,0:T(8,128)S(1)}, f32[64,128]{1,0:T(8,128)S(1)}, u32[]{:S(2)}, u32[]{:S(2)}) %collective-permute-start.3) | collective-permute-done | bytes 32800 | tf_op jit(solution)/shard_map/ppermute | solution.py:25
  11.6 2.6 %quad.1.refs_0_ = f32[256,128]{1,0:T(8,128)S(1)} custom-call(s32[18,128]{1,0:T(8,128)S(1)} %get-tuple-element.9.packed, f32[128,128]{1,0:T(8,128)S(1)} %pairs.1.order_after.refs_0_, f32[128,128]{1,0:T(8,128)S(1)} %collective-permute-done.refs_1_, f32[128,128]{1,0:T(8,128)S(1)} %collective-permute-done.1.refs_2_, ...), custom_call_target="tpu_custom_call" | custom-call | tf_op jit(solution)/shard_map/quad/pallas_call | solution.py:352
  14.2 2.6 %collective-permute-start.5 = (f32[256,128]{1,0:T(8,128)S(1)}, f32[256,128]{1,0:T(8,128)S(1)}, u32[]{:S(2)}, u32[]{:S(2)}) collective-permute-start(f32[256,128]{1,0:T(8,128)S(1)} %quad.1.refs_0_), channel_id=1, source_target_pairs={{0,16},{2,18},{4,20},{6,22},{8,24},{10,26},{12,28},{14,30},{16,0},... | collective-permute-start | bytes 393224 | tf_op jit(solution)/shard_map/ppermute | solution.py:20
  16.8 1.6 %collective-permute-start.4 = (f32[256,128]{1,0:T(8,128)S(1)}, f32[256,128]{1,0:T(8,128)S(1)}, u32[]{:S(2)}, u32[]{:S(2)}) collective-permute-start(f32[256,128]{1,0:T(8,128)S(1)} %quad.1.refs_0_), channel_id=1, source_target_pairs={{0,8},{2,10},{4,12},{6,14},{8,0},{10,2},{12,4},{14,6},{16,24},{18,... | collective-permute-start | bytes 393224 | tf_op jit(solution)/shard_map/ppermute | solution.py:20
  18.4 5.2 %collective-permute-done.5.refs_2_ = f32[256,128]{1,0:T(8,128)S(1)} collective-permute-done((f32[256,128]{1,0:T(8,128)S(1)}, f32[256,128]{1,0:T(8,128)S(1)}, u32[]{:S(2)}, u32[]{:S(2)}) %collective-permute-start.5) | collective-permute-done | bytes 131104 | tf_op jit(solution)/shard_map/ppermute | solution.py:20
  23.6 0.6 %collective-permute-start.6 = (f32[256,128]{1,0:T(8,128)S(1)}, f32[256,128]{1,0:T(8,128)S(1)}, u32[]{:S(2)}, u32[]{:S(2)}) collective-permute-start(f32[256,128]{1,0:T(8,128)S(1)} %collective-permute-done.5.refs_2_), channel_id=1, source_target_pairs={{0,8},{2,10},{4,12},{6,14},{8,0},{10,2},{12,4},{14,6},{16,24},{18,... | collective-permute-start | bytes 393224 | tf_op jit(solution)/shard_map/ppermute | solution.py:20
  24.2 0.0 collective-permute-done.4.refs_1_
  24.2 4.4 %collective-permute-done.6.refs_3_ = f32[256,128]{1,0:T(8,128)S(1)} collective-permute-done((f32[256,128]{1,0:T(8,128)S(1)}, f32[256,128]{1,0:T(8,128)S(1)}, u32[]{:S(2)}, u32[]{:S(2)}) %collective-permute-start.6) | collective-permute-done | bytes 131104 | tf_op jit(solution)/shard_map/ppermute | solution.py:20
  28.6 0.0 copy-start.3
  28.7 0.1 collective-permute-start.7
  28.7 1.9 %collective-permute-done.7.refs_4_ = f32[1024,128]{1,0:T(8,128)S(1)} collective-permute-done((f32[1024,128]{1,0:T(8,128)S(1)}, f32[1024,128]{1,0:T(8,128)S(1)}, u32[]{:S(2)}, u32[]{:S(2)}) %collective-permute-start.7) | collective-permute-done | bytes 524320 | tf_op jit(solution)/shard_map/ppermute | solution.py:20
  30.6 0.0 copy-done.3
  30.6 3.4 %final.1 = (f32[16,128]{1,0:T(8,128)S(1)}, f32[16,128]{1,0:T(8,128)S(1)}) custom-call(s32[9,128]{1,0:T(8,128)S(1)} %get-tuple-element.8.packed, s32[16]{0:T(128)S(1)} %copy-done.3, f32[256,128]{1,0:T(8,128)S(1)} %quad.1.refs_0_, f32[256,128]{1,0:T(8,128)S(1)} %collective-permute-done.4.refs_1_, f32[256,128]{1,0:T(8,128)S(1)} %collective-permute-done.5.refs_2_, ...), custom_call_target="tpu_custom_call" | custom-call | tf_op jit(solution)/shard_map/final/pallas_call | solution.py:352
  34.0 0.2 collective-permute-start.8
  34.2 1.0 %collective-permute-done.8 = f32[16,128]{1,0:T(8,128)S(1)} collective-permute-done((f32[16,128]{1,0:T(8,128)S(1)}, f32[16,128]{1,0:T(8,128)S(1)}, u32[]{:S(2)}, u32[]{:S(2)}) %collective-permute-start.8) | collective-permute-done | bytes 8224 | tf_op jit(solution)/shard_map/ppermute | solution.py:20
  35.3 1.5 %collective-permute-start.11 = (f32[16,128]{1,0:T(8,128)S(1)}, f32[16,128]{1,0:T(8,128)S(1)}, u32[]{:S(2)}, u32[]{:S(2)}) collective-permute-start(f32[16,128]{1,0:T(8,128)S(1)} %max.3.refs_0_), channel_id=1, source_target_pairs={{0,6},{2,4},{4,2},{6,0},{8,14},{10,12},{12,10},{14,8},{16,22},{18,... | collective-permute-start | bytes 24584 | tf_op jit(solution)/shard_map/ppermute | solution.py:20
  36.7 0.4 %collective-permute-start.10 = (f32[16,128]{1,0:T(8,128)S(1)}, f32[16,128]{1,0:T(8,128)S(1)}, u32[]{:S(2)}, u32[]{:S(2)}) collective-permute-start(f32[16,128]{1,0:T(8,128)S(1)} %max.3.refs_0_), channel_id=1, source_target_pairs={{0,4},{2,6},{4,0},{6,2},{8,12},{10,14},{12,8},{14,10},{16,20},{18,... | collective-permute-start | bytes 24584 | tf_op jit(solution)/shard_map/ppermute | solution.py:20
  37.2 1.6 %collective-permute-start.9 = (f32[16,128]{1,0:T(8,128)S(1)}, f32[16,128]{1,0:T(8,128)S(1)}, u32[]{:S(2)}, u32[]{:S(2)}) collective-permute-start(f32[16,128]{1,0:T(8,128)S(1)} %max.3.refs_0_), channel_id=1, source_target_pairs={{0,2},{2,0},{4,6},{6,4},{8,10},{10,8},{12,14},{14,12},{16,18},{18,... | collective-permute-start | bytes 24584 | tf_op jit(solution)/shard_map/ppermute | solution.py:20
  38.8 1.1 %collective-permute-done.11.refs_3_ = f32[16,128]{1,0:T(8,128)S(1)} collective-permute-done((f32[16,128]{1,0:T(8,128)S(1)}, f32[16,128]{1,0:T(8,128)S(1)}, u32[]{:S(2)}, u32[]{:S(2)}) %collective-permute-start.11) | collective-permute-done | bytes 8224 | tf_op jit(solution)/shard_map/ppermute | solution.py:20
  39.8 0.6 %collective-permute-done.10.refs_2_ = f32[16,128]{1,0:T(8,128)S(1)} collective-permute-done((f32[16,128]{1,0:T(8,128)S(1)}, f32[16,128]{1,0:T(8,128)S(1)}, u32[]{:S(2)}, u32[]{:S(2)}) %collective-permute-start.10) | collective-permute-done | bytes 8224 | tf_op jit(solution)/shard_map/ppermute | solution.py:20
  40.4 0.4 %collective-permute-done.9.refs_1_ = f32[16,128]{1,0:T(8,128)S(1)} collective-permute-done((f32[16,128]{1,0:T(8,128)S(1)}, f32[16,128]{1,0:T(8,128)S(1)}, u32[]{:S(2)}, u32[]{:S(2)}) %collective-permute-start.9) | collective-permute-done | bytes 8224 | tf_op jit(solution)/shard_map/ppermute | solution.py:20
  40.8 0.6 %finish.1 = (f32[8,128]{1,0:T(8,128)}, f32[1,32]{1,0:T(1,128)}) custom-call(f32[16,128]{1,0:T(8,128)S(1)} %max.3.refs_0_, f32[16,128]{1,0:T(8,128)S(1)} %collective-permute-done.9.refs_1_, f32[16,128]{1,0:T(8,128)S(1)} %collective-permute-done.10.refs_2_, f32[16,128]{1,0:T(8,128)S(1)} %collective-permute-done.11.refs_3_), custom_call_target="tpu_custom_call" | custom-call | tf_op jit(solution)/shard_map/finish/pallas_call | solution.py:352
  (4 shorter events, 0.1 us)
Async XLA Ops:
  0.6 0.9 %copy-start = (f32[32,1024]{1,0:T(8,128)S(1)}, f32[32,1024]{1,0:T(8,128)}, u32[]{:S(2)}) copy-start(f32[32,1024]{1,0:T(8,128)} %x.1) | copy-start | bytes 393220
  1.6 8.9 %copy-start.1 = (s32[9,512]{1,0:T(8,128)S(1)}, s32[9,512]{1,0:T(8,128)}, u32[]{:S(2)}) copy-start(s32[9,512]{1,0:T(8,128)} %lead_all.1) | copy-start | bytes 55300
  1.6 8.8 %copy-start.2 = (s32[9,512]{1,0:T(8,128)S(1)}, s32[9,512]{1,0:T(8,128)}, u32[]{:S(2)}) copy-start(s32[9,512]{1,0:T(8,128)} %tail_all.1) | copy-start | bytes 55300
  1.6 6.2 %collective-permute-start.2 = (f32[128,128]{1,0:T(8,128)S(1)}, f32[128,128]{1,0:T(8,128)S(1)}, u32[]{:S(2)}, u32[]{:S(2)}) collective-permute-start(f32[128,128]{1,0:T(8,128)S(1)} %pairs.1.order_after.refs_0_), channel_id=1, source_target_pairs={{0,6},{2,4},{4,2},{6,0},{8,14},{10,12},{12,10},{14,8},{16,22},{18,... | collective-permute-start | bytes 196616 | tf_op jit(solution)/shard_map/ppermute | solution.py:20
  5.5 4.3 %collective-permute-start.1 = (f32[128,128]{1,0:T(8,128)S(1)}, f32[128,128]{1,0:T(8,128)S(1)}, u32[]{:S(2)}, u32[]{:S(2)}) collective-permute-start(f32[128,128]{1,0:T(8,128)S(1)} %pairs.1.order_after.refs_0_), channel_id=1, source_target_pairs={{0,4},{2,6},{4,0},{6,2},{8,12},{10,14},{12,8},{14,10},{16,20},{18,... | collective-permute-start | bytes 196616 | tf_op jit(solution)/shard_map/ppermute | solution.py:20
  6.1 4.3 %collective-permute-start = (f32[128,128]{1,0:T(8,128)S(1)}, f32[128,128]{1,0:T(8,128)S(1)}, u32[]{:S(2)}, u32[]{:S(2)}) collective-permute-start(f32[128,128]{1,0:T(8,128)S(1)} %pairs.1.order_after.refs_0_), channel_id=1, source_target_pairs={{0,2},{2,0},{4,6},{6,4},{8,10},{10,8},{12,14},{14,12},{16,18},{18,... | collective-permute-start | bytes 196616 | tf_op jit(solution)/shard_map/ppermute | solution.py:20
  10.3 1.3 %collective-permute-start.3 = (f32[64,128]{1,0:T(8,128)S(1)}, f32[64,128]{1,0:T(8,128)S(1)}, u32[]{:S(2)}, u32[]{:S(2)}) collective-permute-start(f32[64,128]{1,0:T(8,128)S(1)} %tips.1), channel_id=1, source_target_pairs={{0,1},{1,0},{2,3},{3,2},{4,5},{5,4},{6,7},{7,6},{8,9},{9,8},{10,11... | collective-permute-start | bytes 98312 | tf_op jit(solution)/shard_map/ppermute | solution.py:25
  14.2 9.4 %collective-permute-start.5 = (f32[256,128]{1,0:T(8,128)S(1)}, f32[256,128]{1,0:T(8,128)S(1)}, u32[]{:S(2)}, u32[]{:S(2)}) collective-permute-start(f32[256,128]{1,0:T(8,128)S(1)} %quad.1.refs_0_), channel_id=1, source_target_pairs={{0,16},{2,18},{4,20},{6,22},{8,24},{10,26},{12,28},{14,30},{16,0},... | collective-permute-start | bytes 393224 | tf_op jit(solution)/shard_map/ppermute | solution.py:20
  16.8 7.4 %collective-permute-start.4 = (f32[256,128]{1,0:T(8,128)S(1)}, f32[256,128]{1,0:T(8,128)S(1)}, u32[]{:S(2)}, u32[]{:S(2)}) collective-permute-start(f32[256,128]{1,0:T(8,128)S(1)} %quad.1.refs_0_), channel_id=1, source_target_pairs={{0,8},{2,10},{4,12},{6,14},{8,0},{10,2},{12,4},{14,6},{16,24},{18,... | collective-permute-start | bytes 393224 | tf_op jit(solution)/shard_map/ppermute | solution.py:20
  23.6 5.0 %collective-permute-start.6 = (f32[256,128]{1,0:T(8,128)S(1)}, f32[256,128]{1,0:T(8,128)S(1)}, u32[]{:S(2)}, u32[]{:S(2)}) collective-permute-start(f32[256,128]{1,0:T(8,128)S(1)} %collective-permute-done.5.refs_2_), channel_id=1, source_target_pairs={{0,8},{2,10},{4,12},{6,14},{8,0},{10,2},{12,4},{14,6},{16,24},{18,... | collective-permute-start | bytes 393224 | tf_op jit(solution)/shard_map/ppermute | solution.py:20
  28.6 2.0 %copy-start.3 = (s32[16]{0:T(128)S(1)}, s32[16]{0:T(128)}, u32[]{:S(2)}) copy-start(s32[16]{0:T(128)} %widths_all.1) | copy-start | bytes 196
  28.7 2.0 %collective-permute-start.7 = (f32[1024,128]{1,0:T(8,128)S(1)}, f32[1024,128]{1,0:T(8,128)S(1)}, u32[]{:S(2)}, u32[]{:S(2)}) collective-permute-start(f32[1024,128]{1,0:T(8,128)S(1)} %pad_maximum_fusion), channel_id=1, source_target_pairs={{0,1},{1,0},{2,3},{3,2},{4,5},{5,4},{6,7},{7,6},{8,9},{9,8},{10,11... | collective-permute-start | bytes 1572872 | tf_op jit(solution)/shard_map/ppermute | solution.py:20
  34.0 1.2 %collective-permute-start.8 = (f32[16,128]{1,0:T(8,128)S(1)}, f32[16,128]{1,0:T(8,128)S(1)}, u32[]{:S(2)}, u32[]{:S(2)}) collective-permute-start(f32[16,128]{1,0:T(8,128)S(1)} %get-tuple-element.11), channel_id=1, source_target_pairs={{0,1},{1,0},{2,3},{3,2},{4,5},{5,4},{6,7},{7,6},{8,9},{9,8},{10,11... | collective-permute-start | bytes 24584 | tf_op jit(solution)/shard_map/ppermute | solution.py:20
  35.3 4.5 %collective-permute-start.11 = (f32[16,128]{1,0:T(8,128)S(1)}, f32[16,128]{1,0:T(8,128)S(1)}, u32[]{:S(2)}, u32[]{:S(2)}) collective-permute-start(f32[16,128]{1,0:T(8,128)S(1)} %max.3.refs_0_), channel_id=1, source_target_pairs={{0,6},{2,4},{4,2},{6,0},{8,14},{10,12},{12,10},{14,8},{16,22},{18,... | collective-permute-start | bytes 24584 | tf_op jit(solution)/shard_map/ppermute | solution.py:20
  36.7 3.7 %collective-permute-start.10 = (f32[16,128]{1,0:T(8,128)S(1)}, f32[16,128]{1,0:T(8,128)S(1)}, u32[]{:S(2)}, u32[]{:S(2)}) collective-permute-start(f32[16,128]{1,0:T(8,128)S(1)} %max.3.refs_0_), channel_id=1, source_target_pairs={{0,4},{2,6},{4,0},{6,2},{8,12},{10,14},{12,8},{14,10},{16,20},{18,... | collective-permute-start | bytes 24584 | tf_op jit(solution)/shard_map/ppermute | solution.py:20
  37.2 3.7 %collective-permute-start.9 = (f32[16,128]{1,0:T(8,128)S(1)}, f32[16,128]{1,0:T(8,128)S(1)}, u32[]{:S(2)}, u32[]{:S(2)}) collective-permute-start(f32[16,128]{1,0:T(8,128)S(1)} %max.3.refs_0_), channel_id=1, source_target_pairs={{0,2},{2,0},{4,6},{6,4},{8,10},{10,8},{12,14},{14,12},{16,18},{18,... | collective-permute-start | bytes 24584 | tf_op jit(solution)/shard_map/ppermute | solution.py:20

commit v4 on v3

--- a/solution.py
+++ b/solution.py
@@ -18,11 +18,6 @@
 
 def xor_permute(value, axis, by):
     return lax.ppermute(value, axis, [(i, i ^ by) for i in range(lax.axis_size(axis))])
-
-
-def rotate_right(value, axis):
-    count = lax.axis_size(axis)
-    return lax.ppermute(value, axis, [(i, (i + 1) % count) for i in range(count)])
 
 
 def section_rows(src, dst, dst_row, segs, rows, table, entry, group=16):
@@ -60,15 +55,6 @@
         first = seg * channels
         summed = stage[pl.ds(first, half, stride=2), :] + stage[pl.ds(first + 1, half, stride=2), :]
         out[pl.ds(seg, half, stride=segs), :] = summed
-
-
-def tips_kernel(*refs, main_segs, halo):
-    *inputs, out = refs
-    rows = inputs[0].shape[0] // main_segs
-    for n, ref in enumerate(inputs):
-        for seg in range(halo):
-            to = (n * halo + seg) * rows
-            out[pl.ds(to, rows), :] = ref[pl.ds(main_segs - halo + seg, rows, stride=main_segs), :]
 
 
 def stage_places(stage, section, freq, trials_first=None):
@@ -134,47 +120,32 @@
         slot += len(wheres)
 
 
-def quad_kernel(packed, *refs, stage, section, local, segs_of):
-    inputs, tips, out = refs[:4], refs[4:-5], refs[-5]
-    buf_a, buf_b, table, sem = refs[-4:]
+def quad_kernel(packed, *refs, stage, section, local, ahead, segs):
+    inputs, out = refs[:4], refs[4]
+    buf_a, buf_b, table, sem = refs[5:]
     copy = pltpu.make_async_copy(packed, table, sem)
     copy.start()
     freq = lax.axis_index("freq")
     place = (freq >> (2 * stage)) & 3
     _, _, half_order, starts = stage_places(stage, section, freq)
-    segs = segs_of(1) if local else segs_of(section)
-    size = inputs[0].shape[0]
-    buf_a[pl.ds(0, PAD), :] = jnp.zeros((PAD, LANES), jnp.float32)
-    buf_b[pl.ds(0, PAD), :] = jnp.zeros((PAD, LANES), jnp.float32)
+    stride = ahead + segs
+    for buf in (buf_a, buf_b):
+        buf[...] = jnp.zeros(buf.shape, jnp.float32)
+    rows = ROWS // 2 if local else ROWS
+    in_segs = inputs[0].shape[0] // rows
     for by, ref in enumerate(inputs):
-        if not local:
-            to = pl.multiple_of(PAD + (place ^ by) * size, 8)
-            buf_a[pl.ds(to, size), :] = ref[...]
-            continue
-        rows = ROWS // 2
-        main_segs = size // rows
-        halo = segs - main_segs
-        to = PAD + (place ^ by) * (rows * segs)
-        for seg in range(halo):
-            tip = tips[0][pl.ds((by * halo + seg) * rows, rows), :]
-            tip = jnp.where(lax.axis_index("tm") > 0, tip, 0.0)
-            buf_a[pl.ds(to + seg, rows, stride=segs), :] = tip
+        to = (place ^ by) * (rows * stride) + ahead
         for row in range(rows):
-            buf_a[pl.ds(to + row * segs + halo, main_segs), :] = ref[pl.ds(row * main_segs, main_segs), :]
+            buf_a[pl.ds(to + row * stride, in_segs), :] = ref[pl.ds(row * in_segs, in_segs), :]
     copy.wait()
     src, dst = buf_a, buf_b
+
+    def at_row(k):
+        return k * stride + ahead
+
     for now in range(1, local):
-        section_rows(
-            src,
-            dst,
-            lambda k: PAD + k * segs,
-            segs,
-            4 * ROWS,
-            table,
-            lambda k, now=now: (3 * (now - 1), k),
-        )
+        section_rows(src, dst, at_row, segs, 4 * ROWS, table, lambda k, now=now: (3 * (now - 1), k))
         src, dst = dst, src
-    mid_segs, out_segs = segs_of(section + 1), segs_of(section + 2)
 
     def mid_entry(k):
         band = k // ROWS
@@ -182,10 +153,10 @@
             return 3 * (local - 1), 2 * ROWS * band + ROWS * half_order + k % ROWS
         return 3 * band, starts[band] % LANES + k % ROWS
 
-    section_rows(src, dst, lambda k: PAD + k * mid_segs, mid_segs, 2 * ROWS, table, mid_entry)
+    section_rows(src, dst, at_row, segs, 2 * ROWS, table, mid_entry)
     at = 3 * local if local else 6
     column = starts[2] % LANES
-    section_rows(dst, out, lambda k: k * out_segs, out_segs, ROWS, table, lambda k: (at, column + k))
+    section_rows(dst, out, lambda k: k * segs, segs, ROWS, table, lambda k: (at, column + k))
 
 
 def final_kernel(packed, widths_all, *refs, stage, section, n_time, main_segs, trials, place_rows):
@@ -211,14 +182,25 @@
         buf[pl.ds(row * stride, PAD), :] = zeros
     for row in range(2 * ROWS):
         mid[pl.ds(row * stride, PAD), :] = zeros
-    size = ROWS * main_segs
+    in_segs = own[0].shape[0] // ROWS
+    size = ROWS * in_segs
+    sources = []
     for by_band in range(4):
         for by_time in range(n_time):
-            start = (place ^ by_band) * (ROWS * stride) + PAD + (tm ^ by_time) * main_segs
+            start = (place ^ by_band) * (ROWS * stride) + PAD
+            part = tm ^ by_time
             ref, at = (own[by_band], 0) if by_time == 0 else (moved[by_time - 1], by_band * size)
-            for row in range(ROWS):
-                to = pl.multiple_of(start + row * stride, 8)
-                buf[pl.ds(to, main_segs), :] = ref[pl.ds(at + row * main_segs, main_segs), :]
+            sources.append((start, part, ref, at))
+    for start, part, ref, at in sources:
+        for row in range(ROWS):
+            to = pl.multiple_of(start + part * main_segs + row * stride, 8)
+            buf[pl.ds(to, main_segs), :] = ref[pl.ds(at + row * in_segs, main_segs), :]
+    for start, part, ref, at in sources:
+        to = start + jnp.minimum(part + 1, n_time - 1) * main_segs
+        for seg in range(in_segs - main_segs):
+            spill = ref[pl.ds(at + main_segs + seg, ROWS, stride=in_segs), :]
+            where = pl.ds(to + seg, ROWS, stride=stride)
+            buf[where, :] = buf[where, :] + jnp.where(part + 1 < n_time, spill, 0.0)
     for copy in copies:
         copy.wait()
 
@@ -375,13 +357,14 @@
     main_segs = span // LANES
     full_time = sections - 2
 
-    def segs_of(section):
-        need = sum(2**s - 1 for s in range(section, full_time))
-        return main_segs + -(-need // LANES)
+    def segs_after(stage):
+        spill = sum(2**s - 1 for s in range(1, local + 2 * stage + 2))
+        return main_segs + -(-spill // LANES)
+
+    def ahead_of(stage):
+        return 1 + ((2 ** (local + 2 * stage + 1) - 1) >> 7)
 
     pairs = channels // 2
-    segs = segs_of(1)
-    halo = segs - main_segs
     (current,) = call(
         pair_kernel,
         "pairs",
@@ -394,13 +377,11 @@
     stride = PAD + total_segs
     strides = {}
     for section in range(1, sections):
+        stage = max(0, section - local) // 2
         if section >= full_time:
             strides[section] = (stride, PAD)
-        elif section < local:
-            strides[section] = (segs, PAD)
         else:
-            strides[section] = (segs_of(section), PAD + segs_of(section) - segs_of(section + 1))
-    strides[local] = (segs, PAD + segs - segs_of(local + 1))
+            strides[section] = (ahead_of(stage) + segs_after(stage), ahead_of(stage))
     windows = 1 + 3 * (stages - 1)
     tables = call(
         functools.partial(
@@ -416,30 +397,22 @@
     for stage in range(stages - 1):
         section = local + 2 * stage
         others = [xor_permute(current, "freq", by << (2 * stage)) for by in (1, 2, 3)]
-        inputs = [current, *others]
-        if stage == 0:
-            (tips,) = call(
-                functools.partial(tips_kernel, main_segs=main_segs, halo=halo),
-                "tips",
-                inputs,
-                [(4 * pairs * halo, LANES)],
-            )
-            inputs.append(rotate_right(tips, "tm"))
-        rows = 4 * ROWS * (segs_of(1) if stage == 0 else segs_of(section))
+        ahead, segs = ahead_of(stage), segs_after(stage)
         (current,) = call(
             functools.partial(
                 quad_kernel,
                 stage=stage,
                 section=section,
                 local=local if stage == 0 else 0,
-                segs_of=segs_of,
+                ahead=ahead,
+                segs=segs,
             ),
             "quad",
-            inputs,
-            [(ROWS * segs_of(section + 2), LANES)],
+            [current, *others],
+            [(ROWS * segs, LANES)],
             [
-                floats(PAD + rows),
-                floats(PAD + rows),
+                floats(4 * ROWS * (ahead + segs)),
+                floats(4 * ROWS * (ahead + segs)),
                 pltpu.SMEM(tables[stage].shape, jnp.int32),
                 pltpu.SemaphoreType.DMA(()),
             ],

time: 41.6 us -> 40.4 us (0.971)
  waiting for transfers between devices: 19.7 us -> 18.7 us
    ppermute x1 -> x0, waiting for transfers between devices: 0.97 us -> none  [rotate_right(): lax.ppermute(value, axis, [(i, (i + 1) % count) for i in range(count)])]
    pallas_call x6 -> x5, Pallas kernels: 6.81 us -> 6.74 us  [call(): pl.pallas_call(kernel, out_shape=outs, in_specs=[ANY] * len(tables) + [VM...]
  transfers between devices with their start and end apart: 12 -> 11, of which waited for: 11 -> 10; matrix products, arithmetic and copies ran while one was open for 0% -> 0% of each run, Pallas kernels for 0% -> 0%
where the time goes in v4:
time: 40.4 us; the launch traced here: 40.2 us
  waiting for transfers between devices  18.7 us (46%)
  starting transfers between devices  13.2 us (33%)
  Pallas kernels  6.74 us (17%)
  local copies, waits for them, and re-layouts  0.91 us (2%)
  between operations  0.7 us (2%)
    ppermute x11, waiting for transfers between devices, xor_permute(): lax.ppermute(value, axis, [(i, i ^ by) for i in range(lax.axis_size(axis))])  18.7 us
    ppermute x11, starting transfers between devices, xor_permute(): lax.ppermute(value, axis, [(i, i ^ by) for i in range(lax.axis_size(axis))])  13.2 us
    pallas_call x5, Pallas kernels, call(): pl.pallas_call(kernel, out_shape=outs, in_specs=[ANY] * len(tables) + [VM...  6.74 us
    unnamed x8, local copies, waits for them, and re-layouts  0.91 us
  transfers between devices with their start and end apart: 11, of which 10 were waited for; matrix products, arithmetic and copies ran while one was open for 0% of the time, Pallas kernels for 0%

profile of v4, /device:TPU:0, one launch (start us, length us, event | category | flops | bytes accessed | tf_op | source)
XLA Modules:
  0.0 40.2 jit_solution(9915416653643348085)
XLA Ops:
  0.6 0.0 copy-start
  0.6 0.9 %copy-done = f32[32,1024]{1,0:T(8,128)S(1)} copy-done((f32[32,1024]{1,0:T(8,128)S(1)}, f32[32,1024]{1,0:T(8,128)}, u32[]{:S(2)}) %copy-start) | copy-done | bytes 131096
  1.5 0.0 copy-start.1
  1.5 0.0 copy-start.2
  1.6 4.0 %collective-permute-start.2 = (f32[128,128]{1,0:T(8,128)S(1)}, f32[128,128]{1,0:T(8,128)S(1)}, u32[]{:S(2)}, u32[]{:S(2)}) collective-permute-start(f32[128,128]{1,0:T(8,128)S(1)} %pairs.1.order_after.refs_0_), channel_id=1, source_target_pairs={{0,6},{2,4},{4,2},{6,0},{8,14},{10,12},{12,10},{14,8},{16,22},{18,... | collective-permute-start | bytes 196616 | tf_op jit(solution)/shard_map/ppermute | solution.py:20
  5.5 0.5 %collective-permute-start.1 = (f32[128,128]{1,0:T(8,128)S(1)}, f32[128,128]{1,0:T(8,128)S(1)}, u32[]{:S(2)}, u32[]{:S(2)}) collective-permute-start(f32[128,128]{1,0:T(8,128)S(1)} %pairs.1.order_after.refs_0_), channel_id=1, source_target_pairs={{0,4},{2,6},{4,0},{6,2},{8,12},{10,14},{12,8},{14,10},{16,20},{18,... | collective-permute-start | bytes 196616 | tf_op jit(solution)/shard_map/ppermute | solution.py:20
  6.0 0.1 collective-permute-start
  6.2 0.0 copy-done.1
  6.2 0.0 copy-done.2
  6.2 0.1 tables.1
  6.3 1.4 %collective-permute-done.2.refs_3_ = f32[128,128]{1,0:T(8,128)S(1)} collective-permute-done((f32[128,128]{1,0:T(8,128)S(1)}, f32[128,128]{1,0:T(8,128)S(1)}, u32[]{:S(2)}, u32[]{:S(2)}) %collective-permute-start.2) | collective-permute-done | bytes 65568 | tf_op jit(solution)/shard_map/ppermute | solution.py:20
  7.8 2.0 %collective-permute-done.1.refs_2_ = f32[128,128]{1,0:T(8,128)S(1)} collective-permute-done((f32[128,128]{1,0:T(8,128)S(1)}, f32[128,128]{1,0:T(8,128)S(1)}, u32[]{:S(2)}, u32[]{:S(2)}) %collective-permute-start.1) | collective-permute-done | bytes 65568 | tf_op jit(solution)/shard_map/ppermute | solution.py:20
  9.8 0.5 %collective-permute-done.refs_1_ = f32[128,128]{1,0:T(8,128)S(1)} collective-permute-done((f32[128,128]{1,0:T(8,128)S(1)}, f32[128,128]{1,0:T(8,128)S(1)}, u32[]{:S(2)}, u32[]{:S(2)}) %collective-permute-start) | collective-permute-done | bytes 65568 | tf_op jit(solution)/shard_map/ppermute | solution.py:20
  10.3 2.6 %quad.1.refs_0_ = f32[288,128]{1,0:T(8,128)S(1)} custom-call(s32[18,128]{1,0:T(8,128)S(1)} %get-tuple-element.9.packed, f32[128,128]{1,0:T(8,128)S(1)} %pairs.1.order_after.refs_0_, f32[128,128]{1,0:T(8,128)S(1)} %collective-permute-done.refs_1_, f32[128,128]{1,0:T(8,128)S(1)} %collective-permute-done.1.refs_2_, f32[128,128]{1,0:T(8,128)S(1)} %collective-permute-done.2.refs_3_), custom_call_target="tpu_custom_call" | custom-call | tf_op jit(solution)/shard_map/quad/pallas_call | solution.py:334
  12.9 2.6 %collective-permute-start.4 = (f32[288,128]{1,0:T(8,128)S(1)}, f32[288,128]{1,0:T(8,128)S(1)}, u32[]{:S(2)}, u32[]{:S(2)}) collective-permute-start(f32[288,128]{1,0:T(8,128)S(1)} %quad.1.refs_0_), channel_id=1, source_target_pairs={{0,16},{2,18},{4,20},{6,22},{8,24},{10,26},{12,28},{14,30},{16,0},... | collective-permute-start | bytes 442376 | tf_op jit(solution)/shard_map/ppermute | solution.py:20
  15.5 1.6 %collective-permute-start.3 = (f32[288,128]{1,0:T(8,128)S(1)}, f32[288,128]{1,0:T(8,128)S(1)}, u32[]{:S(2)}, u32[]{:S(2)}) collective-permute-start(f32[288,128]{1,0:T(8,128)S(1)} %quad.1.refs_0_), channel_id=1, source_target_pairs={{0,8},{2,10},{4,12},{6,14},{8,0},{10,2},{12,4},{14,6},{16,24},{18,... | collective-permute-start | bytes 442376 | tf_op jit(solution)/shard_map/ppermute | solution.py:20
  17.1 4.3 %collective-permute-done.4.refs_2_ = f32[288,128]{1,0:T(8,128)S(1)} collective-permute-done((f32[288,128]{1,0:T(8,128)S(1)}, f32[288,128]{1,0:T(8,128)S(1)}, u32[]{:S(2)}, u32[]{:S(2)}) %collective-permute-start.4) | collective-permute-done | bytes 147488 | tf_op jit(solution)/shard_map/ppermute | solution.py:20
  21.4 0.6 %collective-permute-start.5 = (f32[288,128]{1,0:T(8,128)S(1)}, f32[288,128]{1,0:T(8,128)S(1)}, u32[]{:S(2)}, u32[]{:S(2)}) collective-permute-start(f32[288,128]{1,0:T(8,128)S(1)} %collective-permute-done.4.refs_2_), channel_id=1, source_target_pairs={{0,8},{2,10},{4,12},{6,14},{8,0},{10,2},{12,4},{14,6},{16,24},{18,... | collective-permute-start | bytes 442376 | tf_op jit(solution)/shard_map/ppermute | solution.py:20
  22.0 0.0 collective-permute-done.3.refs_1_
  22.0 4.6 %collective-permute-done.5.refs_3_ = f32[288,128]{1,0:T(8,128)S(1)} collective-permute-done((f32[288,128]{1,0:T(8,128)S(1)}, f32[288,128]{1,0:T(8,128)S(1)}, u32[]{:S(2)}, u32[]{:S(2)}) %collective-permute-start.5) | collective-permute-done | bytes 147488 | tf_op jit(solution)/shard_map/ppermute | solution.py:20
  26.6 0.0 copy-start.3
  26.6 0.1 collective-permute-start.6
  26.7 2.0 %collective-permute-done.6.refs_4_ = f32[1152,128]{1,0:T(8,128)S(1)} collective-permute-done((f32[1152,128]{1,0:T(8,128)S(1)}, f32[1152,128]{1,0:T(8,128)S(1)}, u32[]{:S(2)}, u32[]{:S(2)}) %collective-permute-start.6) | collective-permute-done | bytes 589856 | tf_op jit(solution)/shard_map/ppermute | solution.py:20
  28.7 0.0 copy-done.3
  28.7 3.4 %final.1 = (f32[16,128]{1,0:T(8,128)S(1)}, f32[16,128]{1,0:T(8,128)S(1)}) custom-call(s32[9,128]{1,0:T(8,128)S(1)} %get-tuple-element.8.packed, s32[16]{0:T(128)S(1)} %copy-done.3, f32[288,128]{1,0:T(8,128)S(1)} %quad.1.refs_0_, f32[288,128]{1,0:T(8,128)S(1)} %collective-permute-done.3.refs_1_, f32[288,128]{1,0:T(8,128)S(1)} %collective-permute-done.4.refs_2_, ...), custom_call_target="tpu_custom_call" | custom-call | tf_op jit(solution)/shard_map/final/pallas_call | solution.py:334
  32.0 0.2 collective-permute-start.7
  32.2 1.0 %collective-permute-done.7 = f32[16,128]{1,0:T(8,128)S(1)} collective-permute-done((f32[16,128]{1,0:T(8,128)S(1)}, f32[16,128]{1,0:T(8,128)S(1)}, u32[]{:S(2)}, u32[]{:S(2)}) %collective-permute-start.7) | collective-permute-done | bytes 8224 | tf_op jit(solution)/shard_map/ppermute | solution.py:20
  33.3 1.7 %collective-permute-start.10 = (f32[16,128]{1,0:T(8,128)S(1)}, f32[16,128]{1,0:T(8,128)S(1)}, u32[]{:S(2)}, u32[]{:S(2)}) collective-permute-start(f32[16,128]{1,0:T(8,128)S(1)} %max.3.refs_0_), channel_id=1, source_target_pairs={{0,6},{2,4},{4,2},{6,0},{8,14},{10,12},{12,10},{14,8},{16,22},{18,... | collective-permute-start | bytes 24584 | tf_op jit(solution)/shard_map/ppermute | solution.py:20
  35.0 0.9 %collective-permute-start.9 = (f32[16,128]{1,0:T(8,128)S(1)}, f32[16,128]{1,0:T(8,128)S(1)}, u32[]{:S(2)}, u32[]{:S(2)}) collective-permute-start(f32[16,128]{1,0:T(8,128)S(1)} %max.3.refs_0_), channel_id=1, source_target_pairs={{0,4},{2,6},{4,0},{6,2},{8,12},{10,14},{12,8},{14,10},{16,20},{18,... | collective-permute-start | bytes 24584 | tf_op jit(solution)/shard_map/ppermute | solution.py:20
  35.9 0.8 %collective-permute-start.8 = (f32[16,128]{1,0:T(8,128)S(1)}, f32[16,128]{1,0:T(8,128)S(1)}, u32[]{:S(2)}, u32[]{:S(2)}) collective-permute-start(f32[16,128]{1,0:T(8,128)S(1)} %max.3.refs_0_), channel_id=1, source_target_pairs={{0,2},{2,0},{4,6},{6,4},{8,10},{10,8},{12,14},{14,12},{16,18},{18,... | collective-permute-start | bytes 24584 | tf_op jit(solution)/shard_map/ppermute | solution.py:20
  36.8 1.1 %collective-permute-done.10.refs_3_ = f32[16,128]{1,0:T(8,128)S(1)} collective-permute-done((f32[16,128]{1,0:T(8,128)S(1)}, f32[16,128]{1,0:T(8,128)S(1)}, u32[]{:S(2)}, u32[]{:S(2)}) %collective-permute-start.10) | collective-permute-done | bytes 8224 | tf_op jit(solution)/shard_map/ppermute | solution.py:20
  37.8 0.8 %collective-permute-done.9.refs_2_ = f32[16,128]{1,0:T(8,128)S(1)} collective-permute-done((f32[16,128]{1,0:T(8,128)S(1)}, f32[16,128]{1,0:T(8,128)S(1)}, u32[]{:S(2)}, u32[]{:S(2)}) %collective-permute-start.9) | collective-permute-done | bytes 8224 | tf_op jit(solution)/shard_map/ppermute | solution.py:20
  38.7 0.9 %collective-permute-done.8.refs_1_ = f32[16,128]{1,0:T(8,128)S(1)} collective-permute-done((f32[16,128]{1,0:T(8,128)S(1)}, f32[16,128]{1,0:T(8,128)S(1)}, u32[]{:S(2)}, u32[]{:S(2)}) %collective-permute-start.8) | collective-permute-done | bytes 8224 | tf_op jit(solution)/shard_map/ppermute | solution.py:20
  39.6 0.6 %finish.1 = (f32[8,128]{1,0:T(8,128)}, f32[1,32]{1,0:T(1,128)}) custom-call(f32[16,128]{1,0:T(8,128)S(1)} %max.3.refs_0_, f32[16,128]{1,0:T(8,128)S(1)} %collective-permute-done.8.refs_1_, f32[16,128]{1,0:T(8,128)S(1)} %collective-permute-done.9.refs_2_, f32[16,128]{1,0:T(8,128)S(1)} %collective-permute-done.10.refs_3_), custom_call_target="tpu_custom_call" | custom-call | tf_op jit(solution)/shard_map/finish/pallas_call | solution.py:334
  (3 shorter events, 0.1 us)
Async XLA Ops:
  0.6 0.9 %copy-start = (f32[32,1024]{1,0:T(8,128)S(1)}, f32[32,1024]{1,0:T(8,128)}, u32[]{:S(2)}) copy-start(f32[32,1024]{1,0:T(8,128)} %x.1) | copy-start | bytes 393220
  1.5 4.6 %copy-start.1 = (s32[9,512]{1,0:T(8,128)S(1)}, s32[9,512]{1,0:T(8,128)}, u32[]{:S(2)}) copy-start(s32[9,512]{1,0:T(8,128)} %lead_all.1) | copy-start | bytes 55300
  1.5 4.6 %copy-start.2 = (s32[9,512]{1,0:T(8,128)S(1)}, s32[9,512]{1,0:T(8,128)}, u32[]{:S(2)}) copy-start(s32[9,512]{1,0:T(8,128)} %tail_all.1) | copy-start | bytes 55300
  1.6 6.2 %collective-permute-start.2 = (f32[128,128]{1,0:T(8,128)S(1)}, f32[128,128]{1,0:T(8,128)S(1)}, u32[]{:S(2)}, u32[]{:S(2)}) collective-permute-start(f32[128,128]{1,0:T(8,128)S(1)} %pairs.1.order_after.refs_0_), channel_id=1, source_target_pairs={{0,6},{2,4},{4,2},{6,0},{8,14},{10,12},{12,10},{14,8},{16,22},{18,... | collective-permute-start | bytes 196616 | tf_op jit(solution)/shard_map/ppermute | solution.py:20
  5.5 4.3 %collective-permute-start.1 = (f32[128,128]{1,0:T(8,128)S(1)}, f32[128,128]{1,0:T(8,128)S(1)}, u32[]{:S(2)}, u32[]{:S(2)}) collective-permute-start(f32[128,128]{1,0:T(8,128)S(1)} %pairs.1.order_after.refs_0_), channel_id=1, source_target_pairs={{0,4},{2,6},{4,0},{6,2},{8,12},{10,14},{12,8},{14,10},{16,20},{18,... | collective-permute-start | bytes 196616 | tf_op jit(solution)/shard_map/ppermute | solution.py:20
  6.0 4.3 %collective-permute-start = (f32[128,128]{1,0:T(8,128)S(1)}, f32[128,128]{1,0:T(8,128)S(1)}, u32[]{:S(2)}, u32[]{:S(2)}) collective-permute-start(f32[128,128]{1,0:T(8,128)S(1)} %pairs.1.order_after.refs_0_), channel_id=1, source_target_pairs={{0,2},{2,0},{4,6},{6,4},{8,10},{10,8},{12,14},{14,12},{16,18},{18,... | collective-permute-start | bytes 196616 | tf_op jit(solution)/shard_map/ppermute | solution.py:20
  12.9 8.5 %collective-permute-start.4 = (f32[288,128]{1,0:T(8,128)S(1)}, f32[288,128]{1,0:T(8,128)S(1)}, u32[]{:S(2)}, u32[]{:S(2)}) collective-permute-start(f32[288,128]{1,0:T(8,128)S(1)} %quad.1.refs_0_), channel_id=1, source_target_pairs={{0,16},{2,18},{4,20},{6,22},{8,24},{10,26},{12,28},{14,30},{16,0},... | collective-permute-start | bytes 442376 | tf_op jit(solution)/shard_map/ppermute | solution.py:20
  15.5 6.4 %collective-permute-start.3 = (f32[288,128]{1,0:T(8,128)S(1)}, f32[288,128]{1,0:T(8,128)S(1)}, u32[]{:S(2)}, u32[]{:S(2)}) collective-permute-start(f32[288,128]{1,0:T(8,128)S(1)} %quad.1.refs_0_), channel_id=1, source_target_pairs={{0,8},{2,10},{4,12},{6,14},{8,0},{10,2},{12,4},{14,6},{16,24},{18,... | collective-permute-start | bytes 442376 | tf_op jit(solution)/shard_map/ppermute | solution.py:20
  21.4 5.1 %collective-permute-start.5 = (f32[288,128]{1,0:T(8,128)S(1)}, f32[288,128]{1,0:T(8,128)S(1)}, u32[]{:S(2)}, u32[]{:S(2)}) collective-permute-start(f32[288,128]{1,0:T(8,128)S(1)} %collective-permute-done.4.refs_2_), channel_id=1, source_target_pairs={{0,8},{2,10},{4,12},{6,14},{8,0},{10,2},{12,4},{14,6},{16,24},{18,... | collective-permute-start | bytes 442376 | tf_op jit(solution)/shard_map/ppermute | solution.py:20
  26.6 2.1 %copy-start.3 = (s32[16]{0:T(128)S(1)}, s32[16]{0:T(128)}, u32[]{:S(2)}) copy-start(s32[16]{0:T(128)} %widths_all.1) | copy-start | bytes 196
  26.6 2.1 %collective-permute-start.6 = (f32[1152,128]{1,0:T(8,128)S(1)}, f32[1152,128]{1,0:T(8,128)S(1)}, u32[]{:S(2)}, u32[]{:S(2)}) collective-permute-start(f32[1152,128]{1,0:T(8,128)S(1)} %pad_maximum_fusion), channel_id=1, source_target_pairs={{0,1},{1,0},{2,3},{3,2},{4,5},{5,4},{6,7},{7,6},{8,9},{9,8},{10,11... | collective-permute-start | bytes 1769480 | tf_op jit(solution)/shard_map/ppermute | solution.py:20
  32.0 1.2 %collective-permute-start.7 = (f32[16,128]{1,0:T(8,128)S(1)}, f32[16,128]{1,0:T(8,128)S(1)}, u32[]{:S(2)}, u32[]{:S(2)}) collective-permute-start(f32[16,128]{1,0:T(8,128)S(1)} %get-tuple-element.11), channel_id=1, source_target_pairs={{0,1},{1,0},{2,3},{3,2},{4,5},{5,4},{6,7},{7,6},{8,9},{9,8},{10,11... | collective-permute-start | bytes 24584 | tf_op jit(solution)/shard_map/ppermute | solution.py:20
  33.3 4.5 %collective-permute-start.10 = (f32[16,128]{1,0:T(8,128)S(1)}, f32[16,128]{1,0:T(8,128)S(1)}, u32[]{:S(2)}, u32[]{:S(2)}) collective-permute-start(f32[16,128]{1,0:T(8,128)S(1)} %max.3.refs_0_), channel_id=1, source_target_pairs={{0,6},{2,4},{4,2},{6,0},{8,14},{10,12},{12,10},{14,8},{16,22},{18,... | collective-permute-start | bytes 24584 | tf_op jit(solution)/shard_map/ppermute | solution.py:20
  35.0 3.7 %collective-permute-start.9 = (f32[16,128]{1,0:T(8,128)S(1)}, f32[16,128]{1,0:T(8,128)S(1)}, u32[]{:S(2)}, u32[]{:S(2)}) collective-permute-start(f32[16,128]{1,0:T(8,128)S(1)} %max.3.refs_0_), channel_id=1, source_target_pairs={{0,4},{2,6},{4,0},{6,2},{8,12},{10,14},{12,8},{14,10},{16,20},{18,... | collective-permute-start | bytes 24584 | tf_op jit(solution)/shard_map/ppermute | solution.py:20
  35.9 3.7 %collective-permute-start.8 = (f32[16,128]{1,0:T(8,128)S(1)}, f32[16,128]{1,0:T(8,128)S(1)}, u32[]{:S(2)}, u32[]{:S(2)}) collective-permute-start(f32[16,128]{1,0:T(8,128)S(1)} %max.3.refs_0_), channel_id=1, source_target_pairs={{0,2},{2,0},{4,6},{6,4},{8,10},{10,8},{12,14},{14,12},{16,18},{18,... | collective-permute-start | bytes 24584 | tf_op jit(solution)/shard_map/ppermute | solution.py:20

commit v5 on v4

--- a/solution.py
+++ b/solution.py
@@ -1,4 +1,5 @@
 import functools
+import math
 
 import jax
 import jax.numpy as jnp
@@ -14,6 +15,7 @@
 eps_var = 1e-06
 VMEM = pl.BlockSpec(memory_space=pltpu.VMEM)
 ANY = pl.BlockSpec(memory_space=pl.ANY)
+SMEM = pl.BlockSpec(memory_space=pltpu.SMEM)
 
 
 def xor_permute(value, axis, by):
@@ -68,9 +70,10 @@
     return base, order, half_order, starts
 
 
-def tables_kernel(lead_all, tail_all, order_after, *refs, stages, sections, local, strides, trials):
+def tables_kernel(lead_all, tail_all, widths_all, order_after, *refs, stages, sections, local, strides, trials):
     del order_after
-    outs, (lead, tail, sems) = refs[:stages], refs[stages:]
+    finals, widths = refs[:stages], refs[stages]
+    outs, (lead, tail, sems) = refs[stages + 1 : 2 * stages + 1], refs[2 * stages + 1 :]
     freq = lax.axis_index("freq")
     plans = []
     for stage in range(stages):
@@ -88,6 +91,7 @@
                 part = table.at[:, pl.ds(window(where), LANES)]
                 copies.append(pltpu.make_async_copy(part, to.at[slot], sems.at[len(copies)]))
             slot += 1
+    copies.append(pltpu.make_async_copy(widths_all, widths, sems.at[len(copies)]))
     for copy in copies:
         copy.start()
     for copy in copies:
@@ -118,13 +122,16 @@
             out[pl.ds(at + 2, 1), :] = e & (LANES - 1)
             at += 3
         slot += len(wheres)
-
-
-def quad_kernel(packed, *refs, stage, section, local, ahead, segs):
+    copies = [pltpu.make_async_copy(outs[n], finals[n], sems.at[n]) for n in range(stages)]
+    for copy in copies:
+        copy.start()
+    for copy in copies:
+        copy.wait()
+
+
+def quad_kernel(table, *refs, stage, section, local, ahead, segs):
     inputs, out = refs[:4], refs[4]
-    buf_a, buf_b, table, sem = refs[5:]
-    copy = pltpu.make_async_copy(packed, table, sem)
-    copy.start()
+    buf_a, buf_b = refs[5:]
     freq = lax.axis_index("freq")
     place = (freq >> (2 * stage)) & 3
     _, _, half_order, starts = stage_places(stage, section, freq)
@@ -137,7 +144,6 @@
         to = (place ^ by) * (rows * stride) + ahead
         for row in range(rows):
             buf_a[pl.ds(to + row * stride, in_segs), :] = ref[pl.ds(row * in_segs, in_segs), :]
-    copy.wait()
     src, dst = buf_a, buf_b
 
     def at_row(k):
@@ -159,16 +165,10 @@
     section_rows(dst, out, lambda k: k * segs, segs, ROWS, table, lambda k: (at, column + k))
 
 
-def final_kernel(packed, widths_all, *refs, stage, section, n_time, main_segs, trials, place_rows):
+def final_kernel(table, widths, *refs, stage, section, n_time, main_segs, trials, place_rows):
     own, moved = refs[:4], refs[4 : 3 + n_time]
     outs = refs[3 + n_time : 3 + 2 * n_time]
-    buf, mid, data, edges, over, scale, table, widths, sems = refs[3 + 2 * n_time :]
-    copies = [
-        pltpu.make_async_copy(packed, table, sems.at[0]),
-        pltpu.make_async_copy(widths_all, widths, sems.at[1]),
-    ]
-    for copy in copies:
-        copy.start()
+    buf, mid, data, edges, over, scale = refs[3 + 2 * n_time :]
     freq = lax.axis_index("freq")
     tm = lax.axis_index("tm")
     place = (freq >> (2 * stage)) & 3
@@ -201,8 +201,6 @@
             spill = ref[pl.ds(at + main_segs + seg, ROWS, stride=in_segs), :]
             where = pl.ds(to + seg, ROWS, stride=stride)
             buf[where, :] = buf[where, :] + jnp.where(part + 1 < n_time, spill, 0.0)
-    for copy in copies:
-        copy.wait()
 
     section_rows(
         buf,
@@ -327,14 +325,14 @@
     second.wait()
 
 
-def call(kernel, name, inputs, out_shapes, scratch=(), tables=(), out_specs=VMEM, dtype=jnp.float32):
-    outs = [jax.ShapeDtypeStruct(shape, dtype) for shape in out_shapes]
-    used = sum(4 * v.size for v in inputs) + sum(4 * o.size for o in outs)
-    used += sum(4 * s.shape[0] * s.shape[1] for s in scratch if len(s.shape) == 2)
+def call(kernel, name, inputs, outs, scratch=(), tables=(), table_specs=SMEM, out_specs=VMEM):
+    outs = [jax.ShapeDtypeStruct(out, jnp.float32) if isinstance(out, tuple) else out for out in outs]
+    used = sum(4 * v.size for v in inputs) + sum(4 * math.prod(o.shape) for o in outs)
+    used += sum(4 * math.prod(s.shape) for s in scratch)
     return pl.pallas_call(
         kernel,
         out_shape=outs,
-        in_specs=[ANY] * len(tables) + [VMEM] * len(inputs),
+        in_specs=[table_specs] * len(tables) + [VMEM] * len(inputs),
         out_specs=[out_specs] * len(outs),
         scratch_shapes=list(scratch),
         compiler_params=pltpu.CompilerParams(vmem_limit_bytes=used + (2 << 20)),
@@ -383,16 +381,22 @@
         else:
             strides[section] = (ahead_of(stage) + segs_after(stage), ahead_of(stage))
     windows = 1 + 3 * (stages - 1)
-    tables = call(
+    shapes = [(3 * (local + 1), LANES)] + [(9, LANES)] * (stages - 1)
+    *tables, widths = call(
         functools.partial(
             tables_kernel, stages=stages, sections=sections, local=local, strides=strides, trials=trials
         ),
         "tables",
         [current],
-        [(3 * (local + 1), LANES)] + [(9, LANES)] * (stages - 1),
-        [pltpu.VMEM((windows, sections, LANES), jnp.int32)] * 2 + [pltpu.SemaphoreType.DMA((2 * windows,))],
-        (lead_delay, tail_delay),
-        dtype=jnp.int32,
+        [pltpu.SMEM(shape, jnp.int32) for shape in [*shapes, widths.shape]],
+        [
+            *[pltpu.VMEM(shape, jnp.int32) for shape in shapes],
+            *[pltpu.VMEM((windows, sections, LANES), jnp.int32)] * 2,
+            pltpu.SemaphoreType.DMA((2 * windows + 1,)),
+        ],
+        (lead_delay, tail_delay, widths),
+        table_specs=ANY,
+        out_specs=SMEM,
     )
     for stage in range(stages - 1):
         section = local + 2 * stage
@@ -413,8 +417,6 @@
             [
                 floats(4 * ROWS * (ahead + segs)),
                 floats(4 * ROWS * (ahead + segs)),
-                pltpu.SMEM(tables[stage].shape, jnp.int32),
-                pltpu.SemaphoreType.DMA(()),
             ],
             [tables[stage]],
         )
@@ -447,9 +449,6 @@
             floats(2 * LANES * main_segs),
             floats(8 * total_segs),
             floats(widths.shape[0] * 8),
-            pltpu.SMEM(tables[stage].shape, jnp.int32),
-            pltpu.SMEM(widths.shape, jnp.int32),
-            pltpu.SemaphoreType.DMA((2,)),
         ],
         [tables[stage], widths],
     )

time: 40.4 us -> 39.8 us (0.985)
  waiting for transfers between devices: 18.7 us -> 17.3 us
  Pallas kernels: 6.74 us -> 7.53 us
    ppermute x11, waiting for transfers between devices: 18.7 us -> 17.3 us  [xor_permute(): lax.ppermute(value, axis, [(i, i ^ by) for i in range(lax.axis_size(axis))])]
    pallas_call x5, Pallas kernels: 6.74 us -> 7.53 us  [call(): pl.pallas_call(kernel, out_shape=outs, in_specs=[table_specs] * len(table...]
  transfers between devices with their start and end apart: 11 -> 11, of which waited for: 10 -> 10; matrix products, arithmetic and copies ran while one was open for 0% -> 0% of each run, Pallas kernels for 0% -> 4%
where the time goes in v5:
time: 39.8 us; the launch traced here: 39.6 us
  waiting for transfers between devices  17.3 us (43%)
  starting transfers between devices  13.1 us (33%)
  Pallas kernels  7.53 us (19%)
  local copies, waits for them, and re-layouts  0.91 us (2%)
  between operations  0.68 us (2%)
    ppermute x11, waiting for transfers between devices, xor_permute(): lax.ppermute(value, axis, [(i, i ^ by) for i in range(lax.axis_size(axis))])  17.3 us
    ppermute x11, starting transfers between devices, xor_permute(): lax.ppermute(value, axis, [(i, i ^ by) for i in range(lax.axis_size(axis))])  13.1 us
    pallas_call x5, Pallas kernels, call(): pl.pallas_call(kernel, out_shape=outs, in_specs=[table_specs] * len(table...  7.53 us
    unnamed x8, local copies, waits for them, and re-layouts  0.91 us
  transfers between devices with their start and end apart: 11, of which 10 were waited for; matrix products, arithmetic and copies ran while one was open for 0% of the time, Pallas kernels for 4%

profile of v5, /device:TPU:0, one launch (start us, length us, event | category | flops | bytes accessed | tf_op | source)
XLA Modules:
  0.0 39.6 jit_solution(7379681249119068240)
XLA Ops:
  0.6 0.0 copy-start
  0.6 0.9 %copy-done = f32[32,1024]{1,0:T(8,128)S(1)} copy-done((f32[32,1024]{1,0:T(8,128)S(1)}, f32[32,1024]{1,0:T(8,128)}, u32[]{:S(2)}) %copy-start) | copy-done | bytes 131096
  1.5 0.0 copy-start.1
  1.5 0.0 copy-start.2
  1.5 0.0 copy-start.3
  1.6 4.0 %collective-permute-start.2 = (f32[128,128]{1,0:T(8,128)S(1)}, f32[128,128]{1,0:T(8,128)S(1)}, u32[]{:S(2)}, u32[]{:S(2)}) collective-permute-start(f32[128,128]{1,0:T(8,128)S(1)} %pairs.1.order_after.refs_0_), channel_id=1, source_target_pairs={{0,6},{2,4},{4,2},{6,0},{8,14},{10,12},{12,10},{14,8},{16,22},{18,... | collective-permute-start | bytes 196616 | tf_op jit(solution)/shard_map/ppermute | solution.py:22
  5.5 0.5 %collective-permute-start.1 = (f32[128,128]{1,0:T(8,128)S(1)}, f32[128,128]{1,0:T(8,128)S(1)}, u32[]{:S(2)}, u32[]{:S(2)}) collective-permute-start(f32[128,128]{1,0:T(8,128)S(1)} %pairs.1.order_after.refs_0_), channel_id=1, source_target_pairs={{0,4},{2,6},{4,0},{6,2},{8,12},{10,14},{12,8},{14,10},{16,20},{18,... | collective-permute-start | bytes 196616 | tf_op jit(solution)/shard_map/ppermute | solution.py:22
  6.0 0.1 collective-permute-start
  6.2 0.0 copy-done.1
  6.2 0.0 copy-done.2
  6.2 0.0 copy-done.3
  6.2 1.5 %tables.1 = (s32[18,128]{1,0:T(8,128)S(4)}, s32[9,128]{1,0:T(8,128)S(4)}, s32[16]{0:T(128)S(4)}) custom-call(s32[9,512]{1,0:T(8,128)S(1)} %copy-done.1, s32[9,512]{1,0:T(8,128)S(1)} %copy-done.2, s32[16]{0:T(128)S(1)} %copy-done.3, f32[128,128]{1,0:T(8,128)S(1)} %pairs.1.order_after.refs_0_), custom_call_target="tpu_custom_call" | custom-call | tf_op jit(solution)/shard_map/tables/pallas_call | solution.py:332
  7.7 0.1 collective-permute-done.2.refs_3_
  7.8 2.0 %collective-permute-done.1.refs_2_ = f32[128,128]{1,0:T(8,128)S(1)} collective-permute-done((f32[128,128]{1,0:T(8,128)S(1)}, f32[128,128]{1,0:T(8,128)S(1)}, u32[]{:S(2)}, u32[]{:S(2)}) %collective-permute-start.1) | collective-permute-done | bytes 65568 | tf_op jit(solution)/shard_map/ppermute | solution.py:22
  9.8 0.5 %collective-permute-done.refs_1_ = f32[128,128]{1,0:T(8,128)S(1)} collective-permute-done((f32[128,128]{1,0:T(8,128)S(1)}, f32[128,128]{1,0:T(8,128)S(1)}, u32[]{:S(2)}, u32[]{:S(2)}) %collective-permute-start) | collective-permute-done | bytes 65568 | tf_op jit(solution)/shard_map/ppermute | solution.py:22
  10.3 2.5 %quad.1.refs_0_ = f32[288,128]{1,0:T(8,128)S(1)} custom-call(s32[18,128]{1,0:T(8,128)S(4)} %get-tuple-element.11.table, f32[128,128]{1,0:T(8,128)S(1)} %pairs.1.order_after.refs_0_, f32[128,128]{1,0:T(8,128)S(1)} %collective-permute-done.refs_1_, f32[128,128]{1,0:T(8,128)S(1)} %collective-permute-done.1.refs_2_, f32[128,128]{1,0:T(8,128)S(1)} %collective-permute-done.2.refs_3_), custom_call_target="tpu_custom_call" | custom-call | tf_op jit(solution)/shard_map/quad/pallas_call | solution.py:332
  12.8 2.6 %collective-permute-start.4 = (f32[288,128]{1,0:T(8,128)S(1)}, f32[288,128]{1,0:T(8,128)S(1)}, u32[]{:S(2)}, u32[]{:S(2)}) collective-permute-start(f32[288,128]{1,0:T(8,128)S(1)} %quad.1.refs_0_), channel_id=1, source_target_pairs={{0,16},{2,18},{4,20},{6,22},{8,24},{10,26},{12,28},{14,30},{16,0},... | collective-permute-start | bytes 442376 | tf_op jit(solution)/shard_map/ppermute | solution.py:22
  15.4 1.6 %collective-permute-start.3 = (f32[288,128]{1,0:T(8,128)S(1)}, f32[288,128]{1,0:T(8,128)S(1)}, u32[]{:S(2)}, u32[]{:S(2)}) collective-permute-start(f32[288,128]{1,0:T(8,128)S(1)} %quad.1.refs_0_), channel_id=1, source_target_pairs={{0,8},{2,10},{4,12},{6,14},{8,0},{10,2},{12,4},{14,6},{16,24},{18,... | collective-permute-start | bytes 442376 | tf_op jit(solution)/shard_map/ppermute | solution.py:22
  17.0 4.3 %collective-permute-done.4.refs_2_ = f32[288,128]{1,0:T(8,128)S(1)} collective-permute-done((f32[288,128]{1,0:T(8,128)S(1)}, f32[288,128]{1,0:T(8,128)S(1)}, u32[]{:S(2)}, u32[]{:S(2)}) %collective-permute-start.4) | collective-permute-done | bytes 147488 | tf_op jit(solution)/shard_map/ppermute | solution.py:22
  21.3 0.6 %collective-permute-start.5 = (f32[288,128]{1,0:T(8,128)S(1)}, f32[288,128]{1,0:T(8,128)S(1)}, u32[]{:S(2)}, u32[]{:S(2)}) collective-permute-start(f32[288,128]{1,0:T(8,128)S(1)} %collective-permute-done.4.refs_2_), channel_id=1, source_target_pairs={{0,8},{2,10},{4,12},{6,14},{8,0},{10,2},{12,4},{14,6},{16,24},{18,... | collective-permute-start | bytes 442376 | tf_op jit(solution)/shard_map/ppermute | solution.py:22
  21.8 0.0 collective-permute-done.3.refs_1_
  21.8 4.6 %collective-permute-done.5.refs_3_ = f32[288,128]{1,0:T(8,128)S(1)} collective-permute-done((f32[288,128]{1,0:T(8,128)S(1)}, f32[288,128]{1,0:T(8,128)S(1)}, u32[]{:S(2)}, u32[]{:S(2)}) %collective-permute-start.5) | collective-permute-done | bytes 147488 | tf_op jit(solution)/shard_map/ppermute | solution.py:22
  26.5 0.1 collective-permute-start.6
  26.5 2.0 %collective-permute-done.6.refs_4_ = f32[1152,128]{1,0:T(8,128)S(1)} collective-permute-done((f32[1152,128]{1,0:T(8,128)S(1)}, f32[1152,128]{1,0:T(8,128)S(1)}, u32[]{:S(2)}, u32[]{:S(2)}) %collective-permute-start.6) | collective-permute-done | bytes 589856 | tf_op jit(solution)/shard_map/ppermute | solution.py:22
  28.5 2.9 %final.1 = (f32[16,128]{1,0:T(8,128)S(1)}, f32[16,128]{1,0:T(8,128)S(1)}) custom-call(s32[9,128]{1,0:T(8,128)S(4)} %get-tuple-element.9.table, s32[16]{0:T(128)S(4)} %get-tuple-element.10.widths, f32[288,128]{1,0:T(8,128)S(1)} %quad.1.refs_0_, f32[288,128]{1,0:T(8,128)S(1)} %collective-permute-done.3.refs_1_, f32[288,128]{1,0:T(8,128)S(1)} %collective-permute-done.4.refs_2_, ...), custom_call_target="tpu_custom_call" | custom-call | tf_op jit(solution)/shard_map/final/pallas_call | solution.py:332
  31.5 0.2 collective-permute-start.7
  31.7 1.0 %collective-permute-done.7 = f32[16,128]{1,0:T(8,128)S(1)} collective-permute-done((f32[16,128]{1,0:T(8,128)S(1)}, f32[16,128]{1,0:T(8,128)S(1)}, u32[]{:S(2)}, u32[]{:S(2)}) %collective-permute-start.7) | collective-permute-done | bytes 8224 | tf_op jit(solution)/shard_map/ppermute | solution.py:22
  32.7 1.7 %collective-permute-start.10 = (f32[16,128]{1,0:T(8,128)S(1)}, f32[16,128]{1,0:T(8,128)S(1)}, u32[]{:S(2)}, u32[]{:S(2)}) collective-permute-start(f32[16,128]{1,0:T(8,128)S(1)} %max.3.refs_0_), channel_id=1, source_target_pairs={{0,6},{2,4},{4,2},{6,0},{8,14},{10,12},{12,10},{14,8},{16,22},{18,... | collective-permute-start | bytes 24584 | tf_op jit(solution)/shard_map/ppermute | solution.py:22
  34.4 0.9 %collective-permute-start.9 = (f32[16,128]{1,0:T(8,128)S(1)}, f32[16,128]{1,0:T(8,128)S(1)}, u32[]{:S(2)}, u32[]{:S(2)}) collective-permute-start(f32[16,128]{1,0:T(8,128)S(1)} %max.3.refs_0_), channel_id=1, source_target_pairs={{0,4},{2,6},{4,0},{6,2},{8,12},{10,14},{12,8},{14,10},{16,20},{18,... | collective-permute-start | bytes 24584 | tf_op jit(solution)/shard_map/ppermute | solution.py:22
  35.3 0.9 %collective-permute-start.8 = (f32[16,128]{1,0:T(8,128)S(1)}, f32[16,128]{1,0:T(8,128)S(1)}, u32[]{:S(2)}, u32[]{:S(2)}) collective-permute-start(f32[16,128]{1,0:T(8,128)S(1)} %max.3.refs_0_), channel_id=1, source_target_pairs={{0,2},{2,0},{4,6},{6,4},{8,10},{10,8},{12,14},{14,12},{16,18},{18,... | collective-permute-start | bytes 24584 | tf_op jit(solution)/shard_map/ppermute | solution.py:22
  36.2 1.1 %collective-permute-done.10.refs_3_ = f32[16,128]{1,0:T(8,128)S(1)} collective-permute-done((f32[16,128]{1,0:T(8,128)S(1)}, f32[16,128]{1,0:T(8,128)S(1)}, u32[]{:S(2)}, u32[]{:S(2)}) %collective-permute-start.10) | collective-permute-done | bytes 8224 | tf_op jit(solution)/shard_map/ppermute | solution.py:22
  37.3 0.8 %collective-permute-done.9.refs_2_ = f32[16,128]{1,0:T(8,128)S(1)} collective-permute-done((f32[16,128]{1,0:T(8,128)S(1)}, f32[16,128]{1,0:T(8,128)S(1)}, u32[]{:S(2)}, u32[]{:S(2)}) %collective-permute-start.9) | collective-permute-done | bytes 8224 | tf_op jit(solution)/shard_map/ppermute | solution.py:22
  38.1 0.9 %collective-permute-done.8.refs_1_ = f32[16,128]{1,0:T(8,128)S(1)} collective-permute-done((f32[16,128]{1,0:T(8,128)S(1)}, f32[16,128]{1,0:T(8,128)S(1)}, u32[]{:S(2)}, u32[]{:S(2)}) %collective-permute-start.8) | collective-permute-done | bytes 8224 | tf_op jit(solution)/shard_map/ppermute | solution.py:22
  39.0 0.6 %finish.1 = (f32[8,128]{1,0:T(8,128)}, f32[1,32]{1,0:T(1,128)}) custom-call(f32[16,128]{1,0:T(8,128)S(1)} %max.3.refs_0_, f32[16,128]{1,0:T(8,128)S(1)} %collective-permute-done.8.refs_1_, f32[16,128]{1,0:T(8,128)S(1)} %collective-permute-done.9.refs_2_, f32[16,128]{1,0:T(8,128)S(1)} %collective-permute-done.10.refs_3_), custom_call_target="tpu_custom_call" | custom-call | tf_op jit(solution)/shard_map/finish/pallas_call | solution.py:332
  (3 shorter events, 0.1 us)
Async XLA Ops:
  0.6 0.9 %copy-start = (f32[32,1024]{1,0:T(8,128)S(1)}, f32[32,1024]{1,0:T(8,128)}, u32[]{:S(2)}) copy-start(f32[32,1024]{1,0:T(8,128)} %x.1) | copy-start | bytes 393220
  1.5 4.6 %copy-start.1 = (s32[9,512]{1,0:T(8,128)S(1)}, s32[9,512]{1,0:T(8,128)}, u32[]{:S(2)}) copy-start(s32[9,512]{1,0:T(8,128)} %lead_all.1) | copy-start | bytes 55300
  1.5 4.6 %copy-start.2 = (s32[9,512]{1,0:T(8,128)S(1)}, s32[9,512]{1,0:T(8,128)}, u32[]{:S(2)}) copy-start(s32[9,512]{1,0:T(8,128)} %tail_all.1) | copy-start | bytes 55300
  1.5 4.6 %copy-start.3 = (s32[16]{0:T(128)S(1)}, s32[16]{0:T(128)}, u32[]{:S(2)}) copy-start(s32[16]{0:T(128)} %widths_all.1) | copy-start | bytes 196
  1.6 6.2 %collective-permute-start.2 = (f32[128,128]{1,0:T(8,128)S(1)}, f32[128,128]{1,0:T(8,128)S(1)}, u32[]{:S(2)}, u32[]{:S(2)}) collective-permute-start(f32[128,128]{1,0:T(8,128)S(1)} %pairs.1.order_after.refs_0_), channel_id=1, source_target_pairs={{0,6},{2,4},{4,2},{6,0},{8,14},{10,12},{12,10},{14,8},{16,22},{18,... | collective-permute-start | bytes 196616 | tf_op jit(solution)/shard_map/ppermute | solution.py:22
  5.5 4.3 %collective-permute-start.1 = (f32[128,128]{1,0:T(8,128)S(1)}, f32[128,128]{1,0:T(8,128)S(1)}, u32[]{:S(2)}, u32[]{:S(2)}) collective-permute-start(f32[128,128]{1,0:T(8,128)S(1)} %pairs.1.order_after.refs_0_), channel_id=1, source_target_pairs={{0,4},{2,6},{4,0},{6,2},{8,12},{10,14},{12,8},{14,10},{16,20},{18,... | collective-permute-start | bytes 196616 | tf_op jit(solution)/shard_map/ppermute | solution.py:22
  6.0 4.3 %collective-permute-start = (f32[128,128]{1,0:T(8,128)S(1)}, f32[128,128]{1,0:T(8,128)S(1)}, u32[]{:S(2)}, u32[]{:S(2)}) collective-permute-start(f32[128,128]{1,0:T(8,128)S(1)} %pairs.1.order_after.refs_0_), channel_id=1, source_target_pairs={{0,2},{2,0},{4,6},{6,4},{8,10},{10,8},{12,14},{14,12},{16,18},{18,... | collective-permute-start | bytes 196616 | tf_op jit(solution)/shard_map/ppermute | solution.py:22
  12.8 8.5 %collective-permute-start.4 = (f32[288,128]{1,0:T(8,128)S(1)}, f32[288,128]{1,0:T(8,128)S(1)}, u32[]{:S(2)}, u32[]{:S(2)}) collective-permute-start(f32[288,128]{1,0:T(8,128)S(1)} %quad.1.refs_0_), channel_id=1, source_target_pairs={{0,16},{2,18},{4,20},{6,22},{8,24},{10,26},{12,28},{14,30},{16,0},... | collective-permute-start | bytes 442376 | tf_op jit(solution)/shard_map/ppermute | solution.py:22
  15.4 6.4 %collective-permute-start.3 = (f32[288,128]{1,0:T(8,128)S(1)}, f32[288,128]{1,0:T(8,128)S(1)}, u32[]{:S(2)}, u32[]{:S(2)}) collective-permute-start(f32[288,128]{1,0:T(8,128)S(1)} %quad.1.refs_0_), channel_id=1, source_target_pairs={{0,8},{2,10},{4,12},{6,14},{8,0},{10,2},{12,4},{14,6},{16,24},{18,... | collective-permute-start | bytes 442376 | tf_op jit(solution)/shard_map/ppermute | solution.py:22
  21.3 5.1 %collective-permute-start.5 = (f32[288,128]{1,0:T(8,128)S(1)}, f32[288,128]{1,0:T(8,128)S(1)}, u32[]{:S(2)}, u32[]{:S(2)}) collective-permute-start(f32[288,128]{1,0:T(8,128)S(1)} %collective-permute-done.4.refs_2_), channel_id=1, source_target_pairs={{0,8},{2,10},{4,12},{6,14},{8,0},{10,2},{12,4},{14,6},{16,24},{18,... | collective-permute-start | bytes 442376 | tf_op jit(solution)/shard_map/ppermute | solution.py:22
  26.5 2.1 %collective-permute-start.6 = (f32[1152,128]{1,0:T(8,128)S(1)}, f32[1152,128]{1,0:T(8,128)S(1)}, u32[]{:S(2)}, u32[]{:S(2)}) collective-permute-start(f32[1152,128]{1,0:T(8,128)S(1)} %pad_maximum_fusion), channel_id=1, source_target_pairs={{0,1},{1,0},{2,3},{3,2},{4,5},{5,4},{6,7},{7,6},{8,9},{9,8},{10,11... | collective-permute-start | bytes 1769480 | tf_op jit(solution)/shard_map/ppermute | solution.py:22
  31.5 1.2 %collective-permute-start.7 = (f32[16,128]{1,0:T(8,128)S(1)}, f32[16,128]{1,0:T(8,128)S(1)}, u32[]{:S(2)}, u32[]{:S(2)}) collective-permute-start(f32[16,128]{1,0:T(8,128)S(1)} %get-tuple-element.13), channel_id=1, source_target_pairs={{0,1},{1,0},{2,3},{3,2},{4,5},{5,4},{6,7},{7,6},{8,9},{9,8},{10,11... | collective-permute-start | bytes 24584 | tf_op jit(solution)/shard_map/ppermute | solution.py:22
  32.7 4.5 %collective-permute-start.10 = (f32[16,128]{1,0:T(8,128)S(1)}, f32[16,128]{1,0:T(8,128)S(1)}, u32[]{:S(2)}, u32[]{:S(2)}) collective-permute-start(f32[16,128]{1,0:T(8,128)S(1)} %max.3.refs_0_), channel_id=1, source_target_pairs={{0,6},{2,4},{4,2},{6,0},{8,14},{10,12},{12,10},{14,8},{16,22},{18,... | collective-permute-start | bytes 24584 | tf_op jit(solution)/shard_map/ppermute | solution.py:22
  34.4 3.7 %collective-permute-start.9 = (f32[16,128]{1,0:T(8,128)S(1)}, f32[16,128]{1,0:T(8,128)S(1)}, u32[]{:S(2)}, u32[]{:S(2)}) collective-permute-start(f32[16,128]{1,0:T(8,128)S(1)} %max.3.refs_0_), channel_id=1, source_target_pairs={{0,4},{2,6},{4,0},{6,2},{8,12},{10,14},{12,8},{14,10},{16,20},{18,... | collective-permute-start | bytes 24584 | tf_op jit(solution)/shard_map/ppermute | solution.py:22
  35.3 3.7 %collective-permute-start.8 = (f32[16,128]{1,0:T(8,128)S(1)}, f32[16,128]{1,0:T(8,128)S(1)}, u32[]{:S(2)}, u32[]{:S(2)}) collective-permute-start(f32[16,128]{1,0:T(8,128)S(1)} %max.3.refs_0_), channel_id=1, source_target_pairs={{0,2},{2,0},{4,6},{6,4},{8,10},{10,8},{12,14},{14,12},{16,18},{18,... | collective-permute-start | bytes 24584 | tf_op jit(solution)/shard_map/ppermute | solution.py:22

commit v6 on v5

--- a/solution.py
+++ b/solution.py
@@ -97,6 +97,14 @@
     for copy in copies:
         copy.wait()
     lane = lax.broadcasted_iota(jnp.int32, (1, LANES), 1)
+
+    def by_distance(value):
+        for bit, width in enumerate((ROWS, 2 * ROWS)):
+            ahead = pltpu.roll(value, LANES - width, axis=1)
+            swapped = jnp.where((lane // width) % 2 == 0, ahead, pltpu.roll(value, width, axis=1))
+            value = jnp.where(((freq >> bit) & 1) == 1, swapped, value)
+        return value
+
     slot = 0
     for stage, (section, order, half_order, wheres) in enumerate(plans):
         out, at = outs[stage], 0
@@ -107,7 +115,9 @@
                 rows = (2 * band, 2 * band + 1) if now == 1 else (2 * band * 2**now, (2 * band + 1) * 2**now)
                 jobs.append((slot, now, *rows, now > 1, strides[now]))
             band = lane // (2 * ROWS)
-            jobs.append((slot, section, 2 * band * ROWS, (2 * band + 1) * ROWS, True, strides[section]))
+            place = freq & 3
+            rows = ((2 * band) ^ place) * ROWS, ((2 * band + 1) ^ place) * ROWS
+            jobs.append((slot, section, *rows, True, strides[section]))
             jobs.append((slot, section + 1, -ROWS * half_order, ROWS - ROWS * half_order, True, strides[section + 1]))
         else:
             for band in range(2):
@@ -117,6 +127,8 @@
             jobs.append((slot + 2, section + 1, low, low + ROWS, True, strides[section + 1]))
         for where, row, low, up, picks, (stride, ahead) in jobs:
             e, h = lead[where, pl.ds(row, 1), :], tail[where, pl.ds(row, 1), :]
+            if row < section:
+                e, h = by_distance(e), by_distance(h)
             out[pl.ds(at, 1), :] = (low + e if picks else low) * stride + ahead
             out[pl.ds(at + 1, 1), :] = (up + h if picks else up) * stride + ahead - (e >> 7)
             out[pl.ds(at + 2, 1), :] = e & (LANES - 1)
@@ -129,29 +141,62 @@
         copy.wait()
 
 
+def local_sections(table, pieces, buf_a, buf_b, local, ahead, segs, out=None):
+    stride = ahead + segs
+    half = ROWS // 2
+    for buf in (buf_a, buf_b):
+        buf[...] = jnp.zeros(buf.shape, jnp.float32)
+    for by, ref in pieces:
+        in_segs = ref.shape[0] // half
+        to = by * (half * stride) + ahead
+        for row in range(half):
+            buf_a[pl.ds(to + row * stride, in_segs), :] = ref[pl.ds(row * in_segs, in_segs), :]
+    src, dst = buf_a, buf_b
+    for now in range(1, local):
+        to_out = out is not None and now == local - 1
+        for n, (by, _) in enumerate(pieces):
+            base = by * ROWS
+            first, step = (n * ROWS * segs, segs) if to_out else (base * stride + ahead, stride)
+            section_rows(
+                src,
+                out if to_out else dst,
+                lambda k, first=first, step=step: first + k * step,
+                segs,
+                ROWS,
+                table,
+                lambda k, now=now, base=base: (3 * (now - 1), base + k),
+            )
+        src, dst = dst, src
+    return src, dst
+
+
+def early_kernel(table, own, two, three, out, buf_a, buf_b, *, local, ahead, segs):
+    local_sections(table, [(0, own), (2, two), (3, three)], buf_a, buf_b, local, ahead, segs, out)
+
+
 def quad_kernel(table, *refs, stage, section, local, ahead, segs):
-    inputs, out = refs[:4], refs[4]
-    buf_a, buf_b = refs[5:]
+    *inputs, out, buf_a, buf_b = refs
     freq = lax.axis_index("freq")
     place = (freq >> (2 * stage)) & 3
     _, _, half_order, starts = stage_places(stage, section, freq)
     stride = ahead + segs
-    for buf in (buf_a, buf_b):
-        buf[...] = jnp.zeros(buf.shape, jnp.float32)
-    rows = ROWS // 2 if local else ROWS
-    in_segs = inputs[0].shape[0] // rows
-    for by, ref in enumerate(inputs):
-        to = (place ^ by) * (rows * stride) + ahead
-        for row in range(rows):
-            buf_a[pl.ds(to + row * stride, in_segs), :] = ref[pl.ds(row * in_segs, in_segs), :]
-    src, dst = buf_a, buf_b
 
     def at_row(k):
         return k * stride + ahead
 
-    for now in range(1, local):
-        section_rows(src, dst, at_row, segs, 4 * ROWS, table, lambda k, now=now: (3 * (now - 1), k))
-        src, dst = dst, src
+    if local:
+        early, late = inputs
+        src, dst = local_sections(table, [(1, late)], buf_a, buf_b, local, ahead, segs)
+        ready = [(by, early, n * ROWS * segs, segs) for n, by in enumerate((0, 2, 3))]
+    else:
+        src, dst = buf_a, buf_b
+        for buf in (buf_a, buf_b):
+            buf[...] = jnp.zeros(buf.shape, jnp.float32)
+        ready = [(by, ref, 0, ref.shape[0] // ROWS) for by, ref in enumerate(inputs)]
+    for by, ref, at, in_segs in ready:
+        to = (by if local else place ^ by) * (ROWS * stride) + ahead
+        for row in range(ROWS):
+            src[pl.ds(to + row * stride, in_segs), :] = ref[pl.ds(at + row * in_segs, in_segs), :]
 
     def mid_entry(k):
         band = k // ROWS
@@ -400,8 +445,20 @@
     )
     for stage in range(stages - 1):
         section = local + 2 * stage
-        others = [xor_permute(current, "freq", by << (2 * stage)) for by in (1, 2, 3)]
+        one, two, three = (xor_permute(current, "freq", by << (2 * stage)) for by in (1, 2, 3))
         ahead, segs = ahead_of(stage), segs_after(stage)
+        buffers = [floats(4 * ROWS * (ahead + segs))] * 2
+        inputs = [current, one, two, three]
+        if stage == 0:
+            (early,) = call(
+                functools.partial(early_kernel, local=local, ahead=ahead, segs=segs),
+                "early",
+                [current, two, three],
+                [(3 * ROWS * segs, LANES)],
+                buffers,
+                [tables[0]],
+            )
+            inputs = [early, one]
         (current,) = call(
             functools.partial(
                 quad_kernel,
@@ -412,12 +469,9 @@
                 segs=segs,
             ),
             "quad",
-            [current, *others],
+            inputs,
             [(ROWS * segs, LANES)],
-            [
-                floats(4 * ROWS * (ahead + segs)),
-                floats(4 * ROWS * (ahead + segs)),
-            ],
+            buffers,
             [tables[stage]],
         )
     stage = stages - 1

time: 39.8 us -> 40 us (level)
    pallas_call x5 -> x6, Pallas kernels: 7.53 us -> 7.86 us  [call(): pl.pallas_call(kernel, out_shape=outs, in_specs=[table_specs] * len(table...]
  transfers between devices with their start and end apart: 11 -> 11, of which waited for: 10 -> 8; matrix products, arithmetic and copies ran while one was open for 0% -> 0% of each run, Pallas kernels for 4% -> 8%
where the time goes in v6:
time: 40 us; the launch traced here: 39.8 us
  waiting for transfers between devices  17.1 us (43%)
  starting transfers between devices  13.2 us (33%)
  Pallas kernels  7.86 us (20%)
  local copies, waits for them, and re-layouts  0.91 us (2%)
  between operations  0.7 us (2%)
    ppermute x11, waiting for transfers between devices, xor_permute(): lax.ppermute(value, axis, [(i, i ^ by) for i in range(lax.axis_size(axis))])  17.1 us
    ppermute x11, starting transfers between devices, xor_permute(): lax.ppermute(value, axis, [(i, i ^ by) for i in range(lax.axis_size(axis))])  13.2 us
    pallas_call x6, Pallas kernels, call(): pl.pallas_call(kernel, out_shape=outs, in_specs=[table_specs] * len(table...  7.86 us
    unnamed x8, local copies, waits for them, and re-layouts  0.91 us
  transfers between devices with their start and end apart: 11, of which 8 were waited for; matrix products, arithmetic and copies ran while one was open for 0% of the time, Pallas kernels for 8%

profile of v6, /device:TPU:0, one launch (start us, length us, event | category | flops | bytes accessed | tf_op | source)
XLA Modules:
  0.0 39.8 jit_solution(16765798629355276930)
XLA Ops:
  0.6 0.0 copy-start
  0.6 0.9 %copy-done = f32[32,1024]{1,0:T(8,128)S(1)} copy-done((f32[32,1024]{1,0:T(8,128)S(1)}, f32[32,1024]{1,0:T(8,128)}, u32[]{:S(2)}) %copy-start) | copy-done | bytes 131096
  1.5 0.0 copy-start.1
  1.5 0.0 copy-start.2
  1.5 0.0 copy-start.3
  1.6 4.0 %collective-permute-start.1 = (f32[128,128]{1,0:T(8,128)S(1)}, f32[128,128]{1,0:T(8,128)S(1)}, u32[]{:S(2)}, u32[]{:S(2)}) collective-permute-start(f32[128,128]{1,0:T(8,128)S(1)} %pairs.1.order_after.own), channel_id=1, source_target_pairs={{0,6},{2,4},{4,2},{6,0},{8,14},{10,12},{12,10},{14,8},{16,22},{18,... | collective-permute-start | bytes 196616 | tf_op jit(solution)/shard_map/ppermute | solution.py:22
  5.5 0.5 %collective-permute-start = (f32[128,128]{1,0:T(8,128)S(1)}, f32[128,128]{1,0:T(8,128)S(1)}, u32[]{:S(2)}, u32[]{:S(2)}) collective-permute-start(f32[128,128]{1,0:T(8,128)S(1)} %pairs.1.order_after.own), channel_id=1, source_target_pairs={{0,4},{2,6},{4,0},{6,2},{8,12},{10,14},{12,8},{14,10},{16,20},{18,... | collective-permute-start | bytes 196616 | tf_op jit(solution)/shard_map/ppermute | solution.py:22
  6.0 0.1 collective-permute-start.2
  6.2 0.0 copy-done.1
  6.2 0.0 copy-done.2
  6.2 0.0 copy-done.3
  6.2 1.6 %tables.1 = (s32[18,128]{1,0:T(8,128)S(4)}, s32[9,128]{1,0:T(8,128)S(4)}, s32[16]{0:T(128)S(4)}) custom-call(s32[9,512]{1,0:T(8,128)S(1)} %copy-done.1, s32[9,512]{1,0:T(8,128)S(1)} %copy-done.2, s32[16]{0:T(128)S(1)} %copy-done.3, f32[128,128]{1,0:T(8,128)S(1)} %pairs.1.order_after.own), custom_call_target="tpu_custom_call" | custom-call | tf_op jit(solution)/shard_map/tables/pallas_call | solution.py:377
  7.8 0.0 collective-permute-done.1.three
  7.8 2.0 %collective-permute-done.two = f32[128,128]{1,0:T(8,128)S(1)} collective-permute-done((f32[128,128]{1,0:T(8,128)S(1)}, f32[128,128]{1,0:T(8,128)S(1)}, u32[]{:S(2)}, u32[]{:S(2)}) %collective-permute-start) | collective-permute-done | bytes 65568 | tf_op jit(solution)/shard_map/ppermute | solution.py:22
  9.8 1.5 %early.1.refs_0_ = f32[864,128]{1,0:T(8,128)S(1)} custom-call(s32[18,128]{1,0:T(8,128)S(4)} %get-tuple-element.11.table, f32[128,128]{1,0:T(8,128)S(1)} %pairs.1.order_after.own, f32[128,128]{1,0:T(8,128)S(1)} %collective-permute-done.two, f32[128,128]{1,0:T(8,128)S(1)} %collective-permute-done.1.three), custom_call_target="tpu_custom_call" | custom-call | tf_op jit(solution)/shard_map/early/pallas_call | solution.py:377
  11.3 0.0 collective-permute-done.2.refs_1_
  11.3 1.2 %quad.1.refs_0_ = f32[288,128]{1,0:T(8,128)S(1)} custom-call(s32[18,128]{1,0:T(8,128)S(4)} %get-tuple-element.11.table, f32[864,128]{1,0:T(8,128)S(1)} %early.1.refs_0_, f32[128,128]{1,0:T(8,128)S(1)} %collective-permute-done.2.refs_1_), custom_call_target="tpu_custom_call" | custom-call | tf_op jit(solution)/shard_map/quad/pallas_call | solution.py:377
  12.5 2.6 %collective-permute-start.4 = (f32[288,128]{1,0:T(8,128)S(1)}, f32[288,128]{1,0:T(8,128)S(1)}, u32[]{:S(2)}, u32[]{:S(2)}) collective-permute-start(f32[288,128]{1,0:T(8,128)S(1)} %quad.1.refs_0_), channel_id=1, source_target_pairs={{0,16},{2,18},{4,20},{6,22},{8,24},{10,26},{12,28},{14,30},{16,0},... | collective-permute-start | bytes 442376 | tf_op jit(solution)/shard_map/ppermute | solution.py:22
  15.1 1.6 %collective-permute-start.3 = (f32[288,128]{1,0:T(8,128)S(1)}, f32[288,128]{1,0:T(8,128)S(1)}, u32[]{:S(2)}, u32[]{:S(2)}) collective-permute-start(f32[288,128]{1,0:T(8,128)S(1)} %quad.1.refs_0_), channel_id=1, source_target_pairs={{0,8},{2,10},{4,12},{6,14},{8,0},{10,2},{12,4},{14,6},{16,24},{18,... | collective-permute-start | bytes 442376 | tf_op jit(solution)/shard_map/ppermute | solution.py:22
  16.7 4.6 %collective-permute-done.4.refs_2_ = f32[288,128]{1,0:T(8,128)S(1)} collective-permute-done((f32[288,128]{1,0:T(8,128)S(1)}, f32[288,128]{1,0:T(8,128)S(1)}, u32[]{:S(2)}, u32[]{:S(2)}) %collective-permute-start.4) | collective-permute-done | bytes 147488 | tf_op jit(solution)/shard_map/ppermute | solution.py:22
  21.3 0.7 %collective-permute-start.5 = (f32[288,128]{1,0:T(8,128)S(1)}, f32[288,128]{1,0:T(8,128)S(1)}, u32[]{:S(2)}, u32[]{:S(2)}) collective-permute-start(f32[288,128]{1,0:T(8,128)S(1)} %collective-permute-done.4.refs_2_), channel_id=1, source_target_pairs={{0,8},{2,10},{4,12},{6,14},{8,0},{10,2},{12,4},{14,6},{16,24},{18,... | collective-permute-start | bytes 442376 | tf_op jit(solution)/shard_map/ppermute | solution.py:22
  22.0 0.0 collective-permute-done.3.refs_1_
  22.0 4.5 %collective-permute-done.5.refs_3_ = f32[288,128]{1,0:T(8,128)S(1)} collective-permute-done((f32[288,128]{1,0:T(8,128)S(1)}, f32[288,128]{1,0:T(8,128)S(1)}, u32[]{:S(2)}, u32[]{:S(2)}) %collective-permute-start.5) | collective-permute-done | bytes 147488 | tf_op jit(solution)/shard_map/ppermute | solution.py:22
  26.5 0.1 collective-permute-start.6
  26.6 2.0 %collective-permute-done.6.refs_4_ = f32[1152,128]{1,0:T(8,128)S(1)} collective-permute-done((f32[1152,128]{1,0:T(8,128)S(1)}, f32[1152,128]{1,0:T(8,128)S(1)}, u32[]{:S(2)}, u32[]{:S(2)}) %collective-permute-start.6) | collective-permute-done | bytes 589856 | tf_op jit(solution)/shard_map/ppermute | solution.py:22
  28.5 3.0 %final.1 = (f32[16,128]{1,0:T(8,128)S(1)}, f32[16,128]{1,0:T(8,128)S(1)}) custom-call(s32[9,128]{1,0:T(8,128)S(4)} %get-tuple-element.9.table, s32[16]{0:T(128)S(4)} %get-tuple-element.10.widths, f32[288,128]{1,0:T(8,128)S(1)} %quad.1.refs_0_, f32[288,128]{1,0:T(8,128)S(1)} %collective-permute-done.3.refs_1_, f32[288,128]{1,0:T(8,128)S(1)} %collective-permute-done.4.refs_2_, ...), custom_call_target="tpu_custom_call" | custom-call | tf_op jit(solution)/shard_map/final/pallas_call | solution.py:377
  31.5 0.2 collective-permute-start.7
  31.7 1.0 %collective-permute-done.7 = f32[16,128]{1,0:T(8,128)S(1)} collective-permute-done((f32[16,128]{1,0:T(8,128)S(1)}, f32[16,128]{1,0:T(8,128)S(1)}, u32[]{:S(2)}, u32[]{:S(2)}) %collective-permute-start.7) | collective-permute-done | bytes 8224 | tf_op jit(solution)/shard_map/ppermute | solution.py:22
  32.7 1.0 %collective-permute-start.10 = (f32[16,128]{1,0:T(8,128)S(1)}, f32[16,128]{1,0:T(8,128)S(1)}, u32[]{:S(2)}, u32[]{:S(2)}) collective-permute-start(f32[16,128]{1,0:T(8,128)S(1)} %max.3.refs_0_), channel_id=1, source_target_pairs={{0,6},{2,4},{4,2},{6,0},{8,14},{10,12},{12,10},{14,8},{16,22},{18,... | collective-permute-start | bytes 24584 | tf_op jit(solution)/shard_map/ppermute | solution.py:22
  33.7 1.8 %collective-permute-start.9 = (f32[16,128]{1,0:T(8,128)S(1)}, f32[16,128]{1,0:T(8,128)S(1)}, u32[]{:S(2)}, u32[]{:S(2)}) collective-permute-start(f32[16,128]{1,0:T(8,128)S(1)} %max.3.refs_0_), channel_id=1, source_target_pairs={{0,4},{2,6},{4,0},{6,2},{8,12},{10,14},{12,8},{14,10},{16,20},{18,... | collective-permute-start | bytes 24584 | tf_op jit(solution)/shard_map/ppermute | solution.py:22
  35.6 0.7 %collective-permute-start.8 = (f32[16,128]{1,0:T(8,128)S(1)}, f32[16,128]{1,0:T(8,128)S(1)}, u32[]{:S(2)}, u32[]{:S(2)}) collective-permute-start(f32[16,128]{1,0:T(8,128)S(1)} %max.3.refs_0_), channel_id=1, source_target_pairs={{0,2},{2,0},{4,6},{6,4},{8,10},{10,8},{12,14},{14,12},{16,18},{18,... | collective-permute-start | bytes 24584 | tf_op jit(solution)/shard_map/ppermute | solution.py:22
  36.2 1.1 %collective-permute-done.10.refs_3_ = f32[16,128]{1,0:T(8,128)S(1)} collective-permute-done((f32[16,128]{1,0:T(8,128)S(1)}, f32[16,128]{1,0:T(8,128)S(1)}, u32[]{:S(2)}, u32[]{:S(2)}) %collective-permute-start.10) | collective-permute-done | bytes 8224 | tf_op jit(solution)/shard_map/ppermute | solution.py:22
  37.3 0.1 collective-permute-done.9.refs_2_
  37.4 1.8 %collective-permute-done.8.refs_1_ = f32[16,128]{1,0:T(8,128)S(1)} collective-permute-done((f32[16,128]{1,0:T(8,128)S(1)}, f32[16,128]{1,0:T(8,128)S(1)}, u32[]{:S(2)}, u32[]{:S(2)}) %collective-permute-start.8) | collective-permute-done | bytes 8224 | tf_op jit(solution)/shard_map/ppermute | solution.py:22
  39.2 0.6 %finish.1 = (f32[8,128]{1,0:T(8,128)}, f32[1,32]{1,0:T(1,128)}) custom-call(f32[16,128]{1,0:T(8,128)S(1)} %max.3.refs_0_, f32[16,128]{1,0:T(8,128)S(1)} %collective-permute-done.8.refs_1_, f32[16,128]{1,0:T(8,128)S(1)} %collective-permute-done.9.refs_2_, f32[16,128]{1,0:T(8,128)S(1)} %collective-permute-done.10.refs_3_), custom_call_target="tpu_custom_call" | custom-call | tf_op jit(solution)/shard_map/finish/pallas_call | solution.py:377
  (3 shorter events, 0.1 us)
Async XLA Ops:
  0.6 0.9 %copy-start = (f32[32,1024]{1,0:T(8,128)S(1)}, f32[32,1024]{1,0:T(8,128)}, u32[]{:S(2)}) copy-start(f32[32,1024]{1,0:T(8,128)} %x.1) | copy-start | bytes 393220
  1.5 4.6 %copy-start.1 = (s32[9,512]{1,0:T(8,128)S(1)}, s32[9,512]{1,0:T(8,128)}, u32[]{:S(2)}) copy-start(s32[9,512]{1,0:T(8,128)} %lead_all.1) | copy-start | bytes 55300
  1.5 4.6 %copy-start.2 = (s32[9,512]{1,0:T(8,128)S(1)}, s32[9,512]{1,0:T(8,128)}, u32[]{:S(2)}) copy-start(s32[9,512]{1,0:T(8,128)} %tail_all.1) | copy-start | bytes 55300
  1.5 4.6 %copy-start.3 = (s32[16]{0:T(128)S(1)}, s32[16]{0:T(128)}, u32[]{:S(2)}) copy-start(s32[16]{0:T(128)} %widths_all.1) | copy-start | bytes 196
  1.6 6.2 %collective-permute-start.1 = (f32[128,128]{1,0:T(8,128)S(1)}, f32[128,128]{1,0:T(8,128)S(1)}, u32[]{:S(2)}, u32[]{:S(2)}) collective-permute-start(f32[128,128]{1,0:T(8,128)S(1)} %pairs.1.order_after.own), channel_id=1, source_target_pairs={{0,6},{2,4},{4,2},{6,0},{8,14},{10,12},{12,10},{14,8},{16,22},{18,... | collective-permute-start | bytes 196616 | tf_op jit(solution)/shard_map/ppermute | solution.py:22
  5.5 4.3 %collective-permute-start = (f32[128,128]{1,0:T(8,128)S(1)}, f32[128,128]{1,0:T(8,128)S(1)}, u32[]{:S(2)}, u32[]{:S(2)}) collective-permute-start(f32[128,128]{1,0:T(8,128)S(1)} %pairs.1.order_after.own), channel_id=1, source_target_pairs={{0,4},{2,6},{4,0},{6,2},{8,12},{10,14},{12,8},{14,10},{16,20},{18,... | collective-permute-start | bytes 196616 | tf_op jit(solution)/shard_map/ppermute | solution.py:22
  6.0 5.2 %collective-permute-start.2 = (f32[128,128]{1,0:T(8,128)S(1)}, f32[128,128]{1,0:T(8,128)S(1)}, u32[]{:S(2)}, u32[]{:S(2)}) collective-permute-start(f32[128,128]{1,0:T(8,128)S(1)} %pairs.1.order_after.own), channel_id=1, source_target_pairs={{0,2},{2,0},{4,6},{6,4},{8,10},{10,8},{12,14},{14,12},{16,18},{18,... | collective-permute-start | bytes 196616 | tf_op jit(solution)/shard_map/ppermute | solution.py:22
  12.5 8.8 %collective-permute-start.4 = (f32[288,128]{1,0:T(8,128)S(1)}, f32[288,128]{1,0:T(8,128)S(1)}, u32[]{:S(2)}, u32[]{:S(2)}) collective-permute-start(f32[288,128]{1,0:T(8,128)S(1)} %quad.1.refs_0_), channel_id=1, source_target_pairs={{0,16},{2,18},{4,20},{6,22},{8,24},{10,26},{12,28},{14,30},{16,0},... | collective-permute-start | bytes 442376 | tf_op jit(solution)/shard_map/ppermute | solution.py:22
  15.1 6.9 %collective-permute-start.3 = (f32[288,128]{1,0:T(8,128)S(1)}, f32[288,128]{1,0:T(8,128)S(1)}, u32[]{:S(2)}, u32[]{:S(2)}) collective-permute-start(f32[288,128]{1,0:T(8,128)S(1)} %quad.1.refs_0_), channel_id=1, source_target_pairs={{0,8},{2,10},{4,12},{6,14},{8,0},{10,2},{12,4},{14,6},{16,24},{18,... | collective-permute-start | bytes 442376 | tf_op jit(solution)/shard_map/ppermute | solution.py:22
  21.3 5.1 %collective-permute-start.5 = (f32[288,128]{1,0:T(8,128)S(1)}, f32[288,128]{1,0:T(8,128)S(1)}, u32[]{:S(2)}, u32[]{:S(2)}) collective-permute-start(f32[288,128]{1,0:T(8,128)S(1)} %collective-permute-done.4.refs_2_), channel_id=1, source_target_pairs={{0,8},{2,10},{4,12},{6,14},{8,0},{10,2},{12,4},{14,6},{16,24},{18,... | collective-permute-start | bytes 442376 | tf_op jit(solution)/shard_map/ppermute | solution.py:22
  26.5 2.1 %collective-permute-start.6 = (f32[1152,128]{1,0:T(8,128)S(1)}, f32[1152,128]{1,0:T(8,128)S(1)}, u32[]{:S(2)}, u32[]{:S(2)}) collective-permute-start(f32[1152,128]{1,0:T(8,128)S(1)} %pad_maximum_fusion), channel_id=1, source_target_pairs={{0,1},{1,0},{2,3},{3,2},{4,5},{5,4},{6,7},{7,6},{8,9},{9,8},{10,11... | collective-permute-start | bytes 1769480 | tf_op jit(solution)/shard_map/ppermute | solution.py:22
  31.5 1.2 %collective-permute-start.7 = (f32[16,128]{1,0:T(8,128)S(1)}, f32[16,128]{1,0:T(8,128)S(1)}, u32[]{:S(2)}, u32[]{:S(2)}) collective-permute-start(f32[16,128]{1,0:T(8,128)S(1)} %get-tuple-element.13), channel_id=1, source_target_pairs={{0,1},{1,0},{2,3},{3,2},{4,5},{5,4},{6,7},{7,6},{8,9},{9,8},{10,11... | collective-permute-start | bytes 24584 | tf_op jit(solution)/shard_map/ppermute | solution.py:22
  32.7 4.5 %collective-permute-start.10 = (f32[16,128]{1,0:T(8,128)S(1)}, f32[16,128]{1,0:T(8,128)S(1)}, u32[]{:S(2)}, u32[]{:S(2)}) collective-permute-start(f32[16,128]{1,0:T(8,128)S(1)} %max.3.refs_0_), channel_id=1, source_target_pairs={{0,6},{2,4},{4,2},{6,0},{8,14},{10,12},{12,10},{14,8},{16,22},{18,... | collective-permute-start | bytes 24584 | tf_op jit(solution)/shard_map/ppermute | solution.py:22
  33.7 3.7 %collective-permute-start.9 = (f32[16,128]{1,0:T(8,128)S(1)}, f32[16,128]{1,0:T(8,128)S(1)}, u32[]{:S(2)}, u32[]{:S(2)}) collective-permute-start(f32[16,128]{1,0:T(8,128)S(1)} %max.3.refs_0_), channel_id=1, source_target_pairs={{0,4},{2,6},{4,0},{6,2},{8,12},{10,14},{12,8},{14,10},{16,20},{18,... | collective-permute-start | bytes 24584 | tf_op jit(solution)/shard_map/ppermute | solution.py:22
  35.6 3.7 %collective-permute-start.8 = (f32[16,128]{1,0:T(8,128)S(1)}, f32[16,128]{1,0:T(8,128)S(1)}, u32[]{:S(2)}, u32[]{:S(2)}) collective-permute-start(f32[16,128]{1,0:T(8,128)S(1)} %max.3.refs_0_), channel_id=1, source_target_pairs={{0,2},{2,0},{4,6},{6,4},{8,10},{10,8},{12,14},{14,12},{16,18},{18,... | collective-permute-start | bytes 24584 | tf_op jit(solution)/shard_map/ppermute | solution.py:22

commit v7 on v6

--- a/solution.py
+++ b/solution.py
@@ -70,10 +70,10 @@
     return base, order, half_order, starts
 
 
-def tables_kernel(lead_all, tail_all, widths_all, order_after, *refs, stages, sections, local, strides, trials):
+def tables_kernel(widths_all, lead_all, tail_all, order_after, *refs, stages, sections, local, strides, trials):
     del order_after
     finals, widths = refs[:stages], refs[stages]
-    outs, (lead, tail, sems) = refs[stages + 1 : 2 * stages + 1], refs[2 * stages + 1 :]
+    outs, sems = refs[stages + 1 : 2 * stages + 1], refs[-1]
     freq = lax.axis_index("freq")
     plans = []
     for stage in range(stages):
@@ -83,19 +83,7 @@
             first_trial = 4 * ROWS * order_of(freq, stage) + trials * lax.axis_index("tm")
         base, order, half_order, starts = stage_places(stage, section, freq, first_trial)
         plans.append((section, order, half_order, [base] if stage == 0 else starts))
-    copies = []
-    slot = 0
-    for *_, wheres in plans:
-        for where in wheres:
-            for table, to in ((lead_all, lead), (tail_all, tail)):
-                part = table.at[:, pl.ds(window(where), LANES)]
-                copies.append(pltpu.make_async_copy(part, to.at[slot], sems.at[len(copies)]))
-            slot += 1
-    copies.append(pltpu.make_async_copy(widths_all, widths, sems.at[len(copies)]))
-    for copy in copies:
-        copy.start()
-    for copy in copies:
-        copy.wait()
+    places = [window(where) for *_, wheres in plans for where in wheres]
     lane = lax.broadcasted_iota(jnp.int32, (1, LANES), 1)
 
     def by_distance(value):
@@ -126,7 +114,8 @@
             low = -ROWS * half_order
             jobs.append((slot + 2, section + 1, low, low + ROWS, True, strides[section + 1]))
         for where, row, low, up, picks, (stride, ahead) in jobs:
-            e, h = lead[where, pl.ds(row, 1), :], tail[where, pl.ds(row, 1), :]
+            part = (pl.ds(row, 1), pl.ds(places[where], LANES))
+            e, h = lead_all[part], tail_all[part]
             if row < section:
                 e, h = by_distance(e), by_distance(h)
             out[pl.ds(at, 1), :] = (low + e if picks else low) * stride + ahead
@@ -135,6 +124,7 @@
             at += 3
         slot += len(wheres)
     copies = [pltpu.make_async_copy(outs[n], finals[n], sems.at[n]) for n in range(stages)]
+    copies.append(pltpu.make_async_copy(widths_all, widths, sems.at[stages]))
     for copy in copies:
         copy.start()
     for copy in copies:
@@ -425,21 +415,19 @@
             strides[section] = (stride, PAD)
         else:
             strides[section] = (ahead_of(stage) + segs_after(stage), ahead_of(stage))
-    windows = 1 + 3 * (stages - 1)
     shapes = [(3 * (local + 1), LANES)] + [(9, LANES)] * (stages - 1)
     *tables, widths = call(
         functools.partial(
             tables_kernel, stages=stages, sections=sections, local=local, strides=strides, trials=trials
         ),
         "tables",
-        [current],
+        [lead_delay, tail_delay, current],
         [pltpu.SMEM(shape, jnp.int32) for shape in [*shapes, widths.shape]],
         [
             *[pltpu.VMEM(shape, jnp.int32) for shape in shapes],
-            *[pltpu.VMEM((windows, sections, LANES), jnp.int32)] * 2,
-            pltpu.SemaphoreType.DMA((2 * windows + 1,)),
+            pltpu.SemaphoreType.DMA((stages + 1,)),
         ],
-        (lead_delay, tail_delay, widths),
+        [widths],
         table_specs=ANY,
         out_specs=SMEM,
     )

time: 40 us -> 40 us (level)
  Pallas kernels: 7.86 us -> 7.19 us
  waiting for transfers between devices: 17.1 us -> 17.7 us
    pallas_call x6, Pallas kernels: 7.86 us -> 7.19 us  [call(): pl.pallas_call(kernel, out_shape=outs, in_specs=[table_specs] * len(table...]
    ppermute x11, waiting for transfers between devices: 17.1 us -> 17.7 us  [xor_permute(): lax.ppermute(value, axis, [(i, i ^ by) for i in range(lax.axis_size(axis))])]
  transfers between devices with their start and end apart: 11 -> 11, of which waited for: 8 -> 8; matrix products, arithmetic and copies ran while one was open for 0% -> 0% of each run, Pallas kernels for 8% -> 6%
where the time goes in v7:
time: 40 us; the launch traced here: 39.8 us
  waiting for transfers between devices  17.7 us (44%)
  starting transfers between devices  13.2 us (33%)
  Pallas kernels  7.19 us (18%)
  local copies, waits for them, and re-layouts  0.91 us (2%)
  between operations  0.69 us (2%)
    ppermute x11, waiting for transfers between devices, xor_permute(): lax.ppermute(value, axis, [(i, i ^ by) for i in range(lax.axis_size(axis))])  17.7 us
    ppermute x11, starting transfers between devices, xor_permute(): lax.ppermute(value, axis, [(i, i ^ by) for i in range(lax.axis_size(axis))])  13.2 us
    pallas_call x6, Pallas kernels, call(): pl.pallas_call(kernel, out_shape=outs, in_specs=[table_specs] * len(table...  7.19 us
    unnamed x8, local copies, waits for them, and re-layouts  0.91 us
  transfers between devices with their start and end apart: 11, of which 8 were waited for; matrix products, arithmetic and copies ran while one was open for 0% of the time, Pallas kernels for 6%

profile of v7, /device:TPU:0, one launch (start us, length us, event | category | flops | bytes accessed | tf_op | source)
XLA Modules:
  0.0 39.8 jit_solution(6506402086856834360)
XLA Ops:
  0.6 0.0 copy-start
  0.6 0.9 %copy-done = f32[32,1024]{1,0:T(8,128)S(1)} copy-done((f32[32,1024]{1,0:T(8,128)S(1)}, f32[32,1024]{1,0:T(8,128)}, u32[]{:S(2)}) %copy-start) | copy-done | bytes 131096
  1.5 0.0 copy-start.1
  1.5 0.0 copy-start.2
  1.5 0.0 copy-start.3
  1.6 4.0 %collective-permute-start.1 = (f32[128,128]{1,0:T(8,128)S(1)}, f32[128,128]{1,0:T(8,128)S(1)}, u32[]{:S(2)}, u32[]{:S(2)}) collective-permute-start(f32[128,128]{1,0:T(8,128)S(1)} %pairs.1.order_after.own), channel_id=1, source_target_pairs={{0,6},{2,4},{4,2},{6,0},{8,14},{10,12},{12,10},{14,8},{16,22},{18,... | collective-permute-start | bytes 196616 | tf_op jit(solution)/shard_map/ppermute | solution.py:22
  5.5 0.5 %collective-permute-start = (f32[128,128]{1,0:T(8,128)S(1)}, f32[128,128]{1,0:T(8,128)S(1)}, u32[]{:S(2)}, u32[]{:S(2)}) collective-permute-start(f32[128,128]{1,0:T(8,128)S(1)} %pairs.1.order_after.own), channel_id=1, source_target_pairs={{0,4},{2,6},{4,0},{6,2},{8,12},{10,14},{12,8},{14,10},{16,20},{18,... | collective-permute-start | bytes 196616 | tf_op jit(solution)/shard_map/ppermute | solution.py:22
  6.0 0.1 collective-permute-start.2
  6.2 0.0 copy-done.1
  6.2 0.0 copy-done.2
  6.2 0.0 copy-done.3
  6.2 1.0 %tables.1 = (s32[18,128]{1,0:T(8,128)S(4)}, s32[9,128]{1,0:T(8,128)S(4)}, s32[16]{0:T(128)S(4)}) custom-call(s32[16]{0:T(128)S(1)} %copy-done.3, s32[9,512]{1,0:T(8,128)S(1)} %copy-done.1, s32[9,512]{1,0:T(8,128)S(1)} %copy-done.2, f32[128,128]{1,0:T(8,128)S(1)} %pairs.1.order_after.own), custom_call_target="tpu_custom_call" | custom-call | tf_op jit(solution)/shard_map/tables/pallas_call | solution.py:367
  7.2 0.6 %collective-permute-done.1.three = f32[128,128]{1,0:T(8,128)S(1)} collective-permute-done((f32[128,128]{1,0:T(8,128)S(1)}, f32[128,128]{1,0:T(8,128)S(1)}, u32[]{:S(2)}, u32[]{:S(2)}) %collective-permute-start.1) | collective-permute-done | bytes 65568 | tf_op jit(solution)/shard_map/ppermute | solution.py:22
  7.8 2.0 %collective-permute-done.two = f32[128,128]{1,0:T(8,128)S(1)} collective-permute-done((f32[128,128]{1,0:T(8,128)S(1)}, f32[128,128]{1,0:T(8,128)S(1)}, u32[]{:S(2)}, u32[]{:S(2)}) %collective-permute-start) | collective-permute-done | bytes 65568 | tf_op jit(solution)/shard_map/ppermute | solution.py:22
  9.8 1.5 %early.1.refs_0_ = f32[864,128]{1,0:T(8,128)S(1)} custom-call(s32[18,128]{1,0:T(8,128)S(4)} %get-tuple-element.11.table, f32[128,128]{1,0:T(8,128)S(1)} %pairs.1.order_after.own, f32[128,128]{1,0:T(8,128)S(1)} %collective-permute-done.two, f32[128,128]{1,0:T(8,128)S(1)} %collective-permute-done.1.three), custom_call_target="tpu_custom_call" | custom-call | tf_op jit(solution)/shard_map/early/pallas_call | solution.py:367
  11.3 0.0 collective-permute-done.2.refs_1_
  11.3 1.2 %quad.1.refs_0_ = f32[288,128]{1,0:T(8,128)S(1)} custom-call(s32[18,128]{1,0:T(8,128)S(4)} %get-tuple-element.11.table, f32[864,128]{1,0:T(8,128)S(1)} %early.1.refs_0_, f32[128,128]{1,0:T(8,128)S(1)} %collective-permute-done.2.refs_1_), custom_call_target="tpu_custom_call" | custom-call | tf_op jit(solution)/shard_map/quad/pallas_call | solution.py:367
  12.5 2.6 %collective-permute-start.4 = (f32[288,128]{1,0:T(8,128)S(1)}, f32[288,128]{1,0:T(8,128)S(1)}, u32[]{:S(2)}, u32[]{:S(2)}) collective-permute-start(f32[288,128]{1,0:T(8,128)S(1)} %quad.1.refs_0_), channel_id=1, source_target_pairs={{0,16},{2,18},{4,20},{6,22},{8,24},{10,26},{12,28},{14,30},{16,0},... | collective-permute-start | bytes 442376 | tf_op jit(solution)/shard_map/ppermute | solution.py:22
  15.1 1.6 %collective-permute-start.3 = (f32[288,128]{1,0:T(8,128)S(1)}, f32[288,128]{1,0:T(8,128)S(1)}, u32[]{:S(2)}, u32[]{:S(2)}) collective-permute-start(f32[288,128]{1,0:T(8,128)S(1)} %quad.1.refs_0_), channel_id=1, source_target_pairs={{0,8},{2,10},{4,12},{6,14},{8,0},{10,2},{12,4},{14,6},{16,24},{18,... | collective-permute-start | bytes 442376 | tf_op jit(solution)/shard_map/ppermute | solution.py:22
  16.7 4.6 %collective-permute-done.4.refs_2_ = f32[288,128]{1,0:T(8,128)S(1)} collective-permute-done((f32[288,128]{1,0:T(8,128)S(1)}, f32[288,128]{1,0:T(8,128)S(1)}, u32[]{:S(2)}, u32[]{:S(2)}) %collective-permute-start.4) | collective-permute-done | bytes 147488 | tf_op jit(solution)/shard_map/ppermute | solution.py:22
  21.3 0.7 %collective-permute-start.5 = (f32[288,128]{1,0:T(8,128)S(1)}, f32[288,128]{1,0:T(8,128)S(1)}, u32[]{:S(2)}, u32[]{:S(2)}) collective-permute-start(f32[288,128]{1,0:T(8,128)S(1)} %collective-permute-done.4.refs_2_), channel_id=1, source_target_pairs={{0,8},{2,10},{4,12},{6,14},{8,0},{10,2},{12,4},{14,6},{16,24},{18,... | collective-permute-start | bytes 442376 | tf_op jit(solution)/shard_map/ppermute | solution.py:22
  22.0 0.0 collective-permute-done.3.refs_1_
  22.0 4.5 %collective-permute-done.5.refs_3_ = f32[288,128]{1,0:T(8,128)S(1)} collective-permute-done((f32[288,128]{1,0:T(8,128)S(1)}, f32[288,128]{1,0:T(8,128)S(1)}, u32[]{:S(2)}, u32[]{:S(2)}) %collective-permute-start.5) | collective-permute-done | bytes 147488 | tf_op jit(solution)/shard_map/ppermute | solution.py:22
  26.5 0.1 collective-permute-start.6
  26.6 2.0 %collective-permute-done.6.refs_4_ = f32[1152,128]{1,0:T(8,128)S(1)} collective-permute-done((f32[1152,128]{1,0:T(8,128)S(1)}, f32[1152,128]{1,0:T(8,128)S(1)}, u32[]{:S(2)}, u32[]{:S(2)}) %collective-permute-start.6) | collective-permute-done | bytes 589856 | tf_op jit(solution)/shard_map/ppermute | solution.py:22
  28.5 2.9 %final.1 = (f32[16,128]{1,0:T(8,128)S(1)}, f32[16,128]{1,0:T(8,128)S(1)}) custom-call(s32[9,128]{1,0:T(8,128)S(4)} %get-tuple-element.9.table, s32[16]{0:T(128)S(4)} %get-tuple-element.10.widths, f32[288,128]{1,0:T(8,128)S(1)} %quad.1.refs_0_, f32[288,128]{1,0:T(8,128)S(1)} %collective-permute-done.3.refs_1_, f32[288,128]{1,0:T(8,128)S(1)} %collective-permute-done.4.refs_2_, ...), custom_call_target="tpu_custom_call" | custom-call | tf_op jit(solution)/shard_map/final/pallas_call | solution.py:367
  31.5 0.2 collective-permute-start.7
  31.7 1.0 %collective-permute-done.7 = f32[16,128]{1,0:T(8,128)S(1)} collective-permute-done((f32[16,128]{1,0:T(8,128)S(1)}, f32[16,128]{1,0:T(8,128)S(1)}, u32[]{:S(2)}, u32[]{:S(2)}) %collective-permute-start.7) | collective-permute-done | bytes 8224 | tf_op jit(solution)/shard_map/ppermute | solution.py:22
  32.7 0.8 %collective-permute-start.10 = (f32[16,128]{1,0:T(8,128)S(1)}, f32[16,128]{1,0:T(8,128)S(1)}, u32[]{:S(2)}, u32[]{:S(2)}) collective-permute-start(f32[16,128]{1,0:T(8,128)S(1)} %max.3.refs_0_), channel_id=1, source_target_pairs={{0,6},{2,4},{4,2},{6,0},{8,14},{10,12},{12,10},{14,8},{16,22},{18,... | collective-permute-start | bytes 24584 | tf_op jit(solution)/shard_map/ppermute | solution.py:22
  33.5 2.0 %collective-permute-start.9 = (f32[16,128]{1,0:T(8,128)S(1)}, f32[16,128]{1,0:T(8,128)S(1)}, u32[]{:S(2)}, u32[]{:S(2)}) collective-permute-start(f32[16,128]{1,0:T(8,128)S(1)} %max.3.refs_0_), channel_id=1, source_target_pairs={{0,4},{2,6},{4,0},{6,2},{8,12},{10,14},{12,8},{14,10},{16,20},{18,... | collective-permute-start | bytes 24584 | tf_op jit(solution)/shard_map/ppermute | solution.py:22
  35.5 0.7 %collective-permute-start.8 = (f32[16,128]{1,0:T(8,128)S(1)}, f32[16,128]{1,0:T(8,128)S(1)}, u32[]{:S(2)}, u32[]{:S(2)}) collective-permute-start(f32[16,128]{1,0:T(8,128)S(1)} %max.3.refs_0_), channel_id=1, source_target_pairs={{0,2},{2,0},{4,6},{6,4},{8,10},{10,8},{12,14},{14,12},{16,18},{18,... | collective-permute-start | bytes 24584 | tf_op jit(solution)/shard_map/ppermute | solution.py:22
  36.2 1.1 %collective-permute-done.10.refs_3_ = f32[16,128]{1,0:T(8,128)S(1)} collective-permute-done((f32[16,128]{1,0:T(8,128)S(1)}, f32[16,128]{1,0:T(8,128)S(1)}, u32[]{:S(2)}, u32[]{:S(2)}) %collective-permute-start.10) | collective-permute-done | bytes 8224 | tf_op jit(solution)/shard_map/ppermute | solution.py:22
  37.3 0.0 collective-permute-done.9.refs_2_
  37.3 1.9 %collective-permute-done.8.refs_1_ = f32[16,128]{1,0:T(8,128)S(1)} collective-permute-done((f32[16,128]{1,0:T(8,128)S(1)}, f32[16,128]{1,0:T(8,128)S(1)}, u32[]{:S(2)}, u32[]{:S(2)}) %collective-permute-start.8) | collective-permute-done | bytes 8224 | tf_op jit(solution)/shard_map/ppermute | solution.py:22
  39.2 0.6 %finish.1 = (f32[8,128]{1,0:T(8,128)}, f32[1,32]{1,0:T(1,128)}) custom-call(f32[16,128]{1,0:T(8,128)S(1)} %max.3.refs_0_, f32[16,128]{1,0:T(8,128)S(1)} %collective-permute-done.8.refs_1_, f32[16,128]{1,0:T(8,128)S(1)} %collective-permute-done.9.refs_2_, f32[16,128]{1,0:T(8,128)S(1)} %collective-permute-done.10.refs_3_), custom_call_target="tpu_custom_call" | custom-call | tf_op jit(solution)/shard_map/finish/pallas_call | solution.py:367
  (3 shorter events, 0.1 us)
Async XLA Ops:
  0.6 0.9 %copy-start = (f32[32,1024]{1,0:T(8,128)S(1)}, f32[32,1024]{1,0:T(8,128)}, u32[]{:S(2)}) copy-start(f32[32,1024]{1,0:T(8,128)} %x.1) | copy-start | bytes 393220
  1.5 4.6 %copy-start.1 = (s32[9,512]{1,0:T(8,128)S(1)}, s32[9,512]{1,0:T(8,128)}, u32[]{:S(2)}) copy-start(s32[9,512]{1,0:T(8,128)} %lead_all.1) | copy-start | bytes 55300
  1.5 4.6 %copy-start.2 = (s32[9,512]{1,0:T(8,128)S(1)}, s32[9,512]{1,0:T(8,128)}, u32[]{:S(2)}) copy-start(s32[9,512]{1,0:T(8,128)} %tail_all.1) | copy-start | bytes 55300
  1.5 4.6 %copy-start.3 = (s32[16]{0:T(128)S(1)}, s32[16]{0:T(128)}, u32[]{:S(2)}) copy-start(s32[16]{0:T(128)} %widths_all.1) | copy-start | bytes 196
  1.6 6.2 %collective-permute-start.1 = (f32[128,128]{1,0:T(8,128)S(1)}, f32[128,128]{1,0:T(8,128)S(1)}, u32[]{:S(2)}, u32[]{:S(2)}) collective-permute-start(f32[128,128]{1,0:T(8,128)S(1)} %pairs.1.order_after.own), channel_id=1, source_target_pairs={{0,6},{2,4},{4,2},{6,0},{8,14},{10,12},{12,10},{14,8},{16,22},{18,... | collective-permute-start | bytes 196616 | tf_op jit(solution)/shard_map/ppermute | solution.py:22
  5.5 4.3 %collective-permute-start = (f32[128,128]{1,0:T(8,128)S(1)}, f32[128,128]{1,0:T(8,128)S(1)}, u32[]{:S(2)}, u32[]{:S(2)}) collective-permute-start(f32[128,128]{1,0:T(8,128)S(1)} %pairs.1.order_after.own), channel_id=1, source_target_pairs={{0,4},{2,6},{4,0},{6,2},{8,12},{10,14},{12,8},{14,10},{16,20},{18,... | collective-permute-start | bytes 196616 | tf_op jit(solution)/shard_map/ppermute | solution.py:22
  6.0 5.2 %collective-permute-start.2 = (f32[128,128]{1,0:T(8,128)S(1)}, f32[128,128]{1,0:T(8,128)S(1)}, u32[]{:S(2)}, u32[]{:S(2)}) collective-permute-start(f32[128,128]{1,0:T(8,128)S(1)} %pairs.1.order_after.own), channel_id=1, source_target_pairs={{0,2},{2,0},{4,6},{6,4},{8,10},{10,8},{12,14},{14,12},{16,18},{18,... | collective-permute-start | bytes 196616 | tf_op jit(solution)/shard_map/ppermute | solution.py:22
  12.5 8.8 %collective-permute-start.4 = (f32[288,128]{1,0:T(8,128)S(1)}, f32[288,128]{1,0:T(8,128)S(1)}, u32[]{:S(2)}, u32[]{:S(2)}) collective-permute-start(f32[288,128]{1,0:T(8,128)S(1)} %quad.1.refs_0_), channel_id=1, source_target_pairs={{0,16},{2,18},{4,20},{6,22},{8,24},{10,26},{12,28},{14,30},{16,0},... | collective-permute-start | bytes 442376 | tf_op jit(solution)/shard_map/ppermute | solution.py:22
  15.1 6.9 %collective-permute-start.3 = (f32[288,128]{1,0:T(8,128)S(1)}, f32[288,128]{1,0:T(8,128)S(1)}, u32[]{:S(2)}, u32[]{:S(2)}) collective-permute-start(f32[288,128]{1,0:T(8,128)S(1)} %quad.1.refs_0_), channel_id=1, source_target_pairs={{0,8},{2,10},{4,12},{6,14},{8,0},{10,2},{12,4},{14,6},{16,24},{18,... | collective-permute-start | bytes 442376 | tf_op jit(solution)/shard_map/ppermute | solution.py:22
  21.3 5.1 %collective-permute-start.5 = (f32[288,128]{1,0:T(8,128)S(1)}, f32[288,128]{1,0:T(8,128)S(1)}, u32[]{:S(2)}, u32[]{:S(2)}) collective-permute-start(f32[288,128]{1,0:T(8,128)S(1)} %collective-permute-done.4.refs_2_), channel_id=1, source_target_pairs={{0,8},{2,10},{4,12},{6,14},{8,0},{10,2},{12,4},{14,6},{16,24},{18,... | collective-permute-start | bytes 442376 | tf_op jit(solution)/shard_map/ppermute | solution.py:22
  26.5 2.1 %collective-permute-start.6 = (f32[1152,128]{1,0:T(8,128)S(1)}, f32[1152,128]{1,0:T(8,128)S(1)}, u32[]{:S(2)}, u32[]{:S(2)}) collective-permute-start(f32[1152,128]{1,0:T(8,128)S(1)} %pad_maximum_fusion), channel_id=1, source_target_pairs={{0,1},{1,0},{2,3},{3,2},{4,5},{5,4},{6,7},{7,6},{8,9},{9,8},{10,11... | collective-permute-start | bytes 1769480 | tf_op jit(solution)/shard_map/ppermute | solution.py:22
  31.5 1.2 %collective-permute-start.7 = (f32[16,128]{1,0:T(8,128)S(1)}, f32[16,128]{1,0:T(8,128)S(1)}, u32[]{:S(2)}, u32[]{:S(2)}) collective-permute-start(f32[16,128]{1,0:T(8,128)S(1)} %get-tuple-element.13), channel_id=1, source_target_pairs={{0,1},{1,0},{2,3},{3,2},{4,5},{5,4},{6,7},{7,6},{8,9},{9,8},{10,11... | collective-permute-start | bytes 24584 | tf_op jit(solution)/shard_map/ppermute | solution.py:22
  32.7 4.5 %collective-permute-start.10 = (f32[16,128]{1,0:T(8,128)S(1)}, f32[16,128]{1,0:T(8,128)S(1)}, u32[]{:S(2)}, u32[]{:S(2)}) collective-permute-start(f32[16,128]{1,0:T(8,128)S(1)} %max.3.refs_0_), channel_id=1, source_target_pairs={{0,6},{2,4},{4,2},{6,0},{8,14},{10,12},{12,10},{14,8},{16,22},{18,... | collective-permute-start | bytes 24584 | tf_op jit(solution)/shard_map/ppermute | solution.py:22
  33.5 3.8 %collective-permute-start.9 = (f32[16,128]{1,0:T(8,128)S(1)}, f32[16,128]{1,0:T(8,128)S(1)}, u32[]{:S(2)}, u32[]{:S(2)}) collective-permute-start(f32[16,128]{1,0:T(8,128)S(1)} %max.3.refs_0_), channel_id=1, source_target_pairs={{0,4},{2,6},{4,0},{6,2},{8,12},{10,14},{12,8},{14,10},{16,20},{18,... | collective-permute-start | bytes 24584 | tf_op jit(solution)/shard_map/ppermute | solution.py:22
  35.5 3.7 %collective-permute-start.8 = (f32[16,128]{1,0:T(8,128)S(1)}, f32[16,128]{1,0:T(8,128)S(1)}, u32[]{:S(2)}, u32[]{:S(2)}) collective-permute-start(f32[16,128]{1,0:T(8,128)S(1)} %max.3.refs_0_), channel_id=1, source_target_pairs={{0,2},{2,0},{4,6},{6,4},{8,10},{10,8},{12,14},{14,12},{16,18},{18,... | collective-permute-start | bytes 24584 | tf_op jit(solution)/shard_map/ppermute | solution.py:22
